TPU v7x, 32 devices: a whole 2x2x4 slice. The times are simulated.
32 devices in a mesh: dp: 16 (over z, x, core), tp: 2 (over y).
Axes of the slice: x: 2, y: 2, z: 4, core: 2. Of those that a mesh axis runs over, the one named last changes fastest.
Arguments:
- hidden_in: bfloat16 [2, 16, 1024, 768], P(None, 'dp', 'tp'), may hold values from -6 to 6
- segment_ids: int32 [2, 16, 1024], P(None, 'dp'), may hold values from 0 to 15, never falling along the last dimension, each value on 1 to 128 neighbouring positions
- bucket_of: int32 [2047], replicated, may hold values from 0 to 31
- attn_gain: bfloat16 [768], P('dp'), may hold values from 0.5 to 1.5
- w_query: bfloat16 [768, 768], P('dp', 'tp'), may hold values from -0.02734375 to 0.02734375
- w_key: bfloat16 [768, 768], P('dp', 'tp'), may hold values from -0.21875 to 0.21875
- w_value: bfloat16 [768, 768], P('dp', 'tp'), may hold values from -0.21875 to 0.21875
- w_attn_out: bfloat16 [768, 768], P('tp', 'dp'), may hold values from -0.875 to 0.875
- bias_table: float32 [32, 12], P(None, 'tp'), may hold values from -4 to 4
- ffn_gain: bfloat16 [768], P('dp'), may hold values from 0.5 to 1.5
- w_gate: bfloat16 [768, 2048], P('dp', 'tp'), may hold values from -0.21875 to 0.21875
- w_up: bfloat16 [768, 2048], P('dp', 'tp'), may hold values from -0.21875 to 0.21875
- w_down: bfloat16 [2048, 768], P('tp', 'dp'), may hold values from -0.125 to 0.125
- cotangent: bfloat16 [2, 16, 1024, 768], P(None, 'dp', 'tp'), may hold values from -6 to 6
Outputs:
- block_out: float32 [2, 16, 1024, 768], P(None, 'dp', 'tp')
- grad_in: float32 [2, 16, 1024, 768], P(None, 'dp', 'tp')
- grad_attn_gain: float32 [768], P('dp')
- grad_query: float32 [768, 768], P('dp', 'tp')
- grad_key: float32 [768, 768], P('dp', 'tp')
- grad_value: float32 [768, 768], P('dp', 'tp')
- grad_attn_out: float32 [768, 768], P('tp', 'dp')
- grad_bias: float32 [32, 12], P(None, 'tp')
- grad_ffn_gain: float32 [768], P('dp')
- grad_gate: float32 [768, 2048], P('dp', 'tp')
- grad_up: float32 [768, 2048], P('dp', 'tp')
- grad_down: float32 [2048, 768], P('tp', 'dp')
Inputs may be any that keep to these rules, and one draw needn't show every extreme that they name: `segment_ids`: within each row of 1024 positions the numbers never fall; each of the 16 documents spans 1 to 128 positions and one spans exactly 128.
All inputs are finite; a program needn't handle non-finite values.
Results may differ from a plain program's by a relative error of at most 0.019.
Values may be sent and summed in bfloat16 or wider, within the bound.
No kernel may reach another device: no remote copies, remote signals or barrier semaphores. Data moves between devices by JAX's collectives and lax.ppermute only.
A program may use at most 832 MiB of HBM per device.

v0:
```python
import functools

import jax
import jax.numpy as jnp
from jax import lax
from jax.experimental import pallas as pl
from jax.experimental.pallas import tpu as pltpu
from jax.sharding import PartitionSpec as P

EPSILON = 1e-06
MASKED = -1000000000.0
HIGHEST_PREC = lax.Precision.HIGHEST
BLOCK = 128
LANES = 128
FEED_CHUNK = 1024
BF = jnp.bfloat16
F32 = jnp.float32


def log2_of(count):
    return count.bit_length() - 1


def swap(value, axis, bit):
    count = lax.axis_size(axis)
    return lax.ppermute(value, axis, [(i, i ^ (1 << bit)) for i in range(count)])


def own_bit(axis, bit):
    return (lax.axis_index(axis) >> bit) & 1


def dp_stages():
    return [("dp", b) for b in range(log2_of(lax.axis_size("dp")) - 1, -1, -1)]


def stage_groups():
    stages = dp_stages()
    near = stages[-2:-1]
    return stages[:-2], (near + [("tp", 0)], [("tp", 0)] + near), stages[-1]


def merge(buf, have, stage):
    axis, bit = stage
    other = swap(buf, axis, bit)
    first = own_bit(axis, bit) == 0
    low, high = jnp.where(first, buf, other), jnp.where(first, other, buf)
    if axis == "tp":
        return jnp.concatenate([low, high], axis=-1), have
    where = sum(1 for s in have if s[1] > bit)
    return jnp.stack([low, high], axis=where), have + [stage]


def tie(values, others):
    both = lax.optimization_barrier((tuple(values), tuple(others)))
    return both[0], both[1]


def gather_halves(piece, cut, before_last):
    far, orders, _ = stage_groups()
    have = []
    for stage in far:
        piece, have = merge(piece, have, stage)
    halves = [(piece[..., :cut], have), (piece[..., cut:], have)]
    for step in range(len(orders[0])):
        if step == len(orders[0]) - 1:
            values, before_last = tie([h[0] for h in halves], before_last)
            halves = [(v, h[1]) for v, h in zip(values, halves)]
        halves = [merge(*half, order[step]) for half, order in zip(halves, orders)]
    shape = (-1, piece.shape[-2])
    return [h[0].reshape(shape + h[0].shape[-1:]) for h in halves], before_last


class Term:
    def __init__(self, array, stages, first=0, count=None):
        self.array, self.stages, self.first = array, list(stages), first
        self.count = array.shape[-1] if count is None else count

    def part(self, done, stage, index):
        starts, sizes, kept = [], [], []
        for dim, own in enumerate(self.stages):
            if own == stage:
                starts.append(index)
            elif own in done:
                starts.append(own_bit(*own))
            else:
                starts.append(0)
                kept.append(2)
            sizes.append(1 if own == stage or own in done else 2)
        rest = self.array.shape[len(self.stages) : -1]
        starts += [0] * len(rest) + [self.first]
        sizes += list(rest) + [self.count]
        part = lax.dynamic_slice(self.array, starts, sizes)
        return part.reshape(tuple(kept) + rest + (self.count,))


class Scatter:
    def __init__(self, terms):
        self.terms, self.done = terms, []
        self.stages = list(terms[0].stages)

    def split(self, stage):
        self.stages.remove(stage)
        send = sum(t.part(self.done, stage, 1 - own_bit(*stage)).astype(F32) for t in self.terms)
        self.done = self.done + [stage]
        return send.astype(BF)

    def add(self, array, first=0, count=None):
        self.terms.append(Term(array, self.stages, first, count))

    def total(self):
        return sum(t.part(self.done, None, 0).astype(F32) for t in self.terms)


def start_near(scatters, orders, step, later=()):
    sends = [s.split(order[step]) for s, order in zip(scatters, orders)]
    if later:
        sends, later = tie(sends, later)
    return [swap(send, *order[step]) for send, order in zip(sends, orders)], later


def end_near(scatters, others, later=()):
    if later:
        others, later = tie(others, later)
    for scatter, other in zip(scatters, others):
        scatter.add(other)
    return later


def far_stage(scatters, stage, later=()):
    send = jnp.concatenate([s.split(stage) for s in scatters], axis=-1)
    if later:
        (send,), later = tie([send], later)
    other = swap(send, *stage)
    wide = other.shape[-1] // len(scatters)
    for index, scatter in enumerate(scatters):
        scatter.add(other, index * wide, wide)
    return later


def sum_everywhere(value):
    for axis, bit in [("tp", 0)] + dp_stages():
        value = value + swap(value, axis, bit)
    return value


def inverse_rms(values):
    return lax.rsqrt(jnp.mean(values * values, axis=-1, keepdims=True) + EPSILON)


def key_blocks(block, last):
    return jnp.maximum(block - 1, 0), block, jnp.minimum(block + 1, last)


def block_mask(seg_rows_ref, seg_lanes_ref, block):
    seg_k = seg_rows_ref[0, pl.ds(pl.multiple_of(block * BLOCK, BLOCK), 3 * BLOCK), :]
    seg_q = seg_lanes_ref[0, pl.ds(block + 1, 1), :]
    mask = jnp.where(seg_k == seg_q, 0.0, MASKED)
    return jnp.concatenate([mask, mask], axis=1)


def place_of(block):
    return pl.ds(pl.multiple_of(block * BLOCK, BLOCK), BLOCK)


def lanes_of(column):
    return pl.ds(pl.multiple_of(column, LANES), LANES)


def window_of(ref, blocks, column):
    return jnp.concatenate([ref[0, place_of(b), lanes_of(column)] for b in blocks], axis=0)


def stack_heads(value):
    first = lax.broadcasted_iota(jnp.int32, value.shape, 1) < LANES // 2
    zero = jnp.zeros_like(value)
    return jnp.concatenate([jnp.where(first, value, zero), jnp.where(first, zero, value)], axis=0)


def unstack_heads(value):
    first = lax.broadcasted_iota(jnp.int32, (LANES, BLOCK), 0) < LANES // 2
    return jnp.where(first, value[:, :BLOCK], value[:, BLOCK:]).T


def dot_nt(left, right):
    return lax.dot_general(left, right, (((1,), (1,)), ((), ())), preferred_element_type=F32)


def dot_nn(left, right):
    return lax.dot_general(left, right, (((1,), (0,)), ((), ())), preferred_element_type=F32)


def dot_tn(left, right):
    return lax.dot_general(left, right, (((0,), (0,)), ((), ())), preferred_element_type=F32)


def pair_columns(pair, half_pairs):
    half, local = divmod(pair, half_pairs)
    width = half_pairs * LANES
    base = half * 3 * width + local * LANES
    return base, base + width, base + 2 * width


def softmax_of(logits):
    top = jnp.max(logits, axis=0, keepdims=True)
    powers = jnp.exp(logits - top)
    return powers * (1.0 / jnp.sum(powers, axis=0, keepdims=True))


def column_pieces(part_a, part_b):
    wide_a, wide_b = part_a.shape[1] // 2, part_b.shape[1] // 2
    at, pieces = 0, []
    for half in range(2):
        for ref, wide, used in ((part_a, wide_a, wide_a), (part_b, wide_b, wide_b - LANES)):
            pieces.append((ref, half * wide, at, used))
            at += used
    return pieces


def attend_kernel(
    pairs,
    last,
    shift_ref,
    x_ref,
    halo_ref,
    gain_ref,
    a_own_ref,
    a_other_ref,
    b_own_ref,
    b_other_ref,
    segr_ref,
    segl_ref,
    bias_ref,
    out_ref,
    qkv_ref,
    n1_ref,
    wa_ref,
    wb_ref,
    n1_s,
):
    own_blocks = pl.num_programs(1)
    shift = shift_ref[0]
    length = n1_s.shape[0]

    @pl.when(jnp.logical_and(pl.program_id(0) == 0, pl.program_id(1) == 0))
    def _():
        groups, shard = a_own_ref.shape[:2]
        for whole, own, other in (
            (wa_ref, a_own_ref, a_other_ref),
            (wb_ref, b_own_ref, b_other_ref),
        ):
            for core in range(2):

                @pl.when(shift_ref[1] == core)
                def _():
                    for group in range(groups):
                        for side, ref in ((core, own), (1 - core, other)):
                            start = (2 * group + side) * shard
                            whole[start : start + shard, :] = ref[group]

    @pl.when(pl.program_id(1) == 0)
    def _():
        def normed(value):
            value = value.astype(F32)
            return (value * inverse_rms(value) * gain_ref[...]).astype(BF)

        def own(index, carry):
            value = normed(x_ref[0, place_of(index), :])
            n1_ref[0, place_of(index), :] = value
            n1_s[place_of(index + shift), :] = value
            return carry

        lax.fori_loop(0, own_blocks, own, 0)
        n1_s[place_of((1 - shift) * own_blocks), :] = normed(halo_ref[0])
        chunk = length // 2

        def project(index, carry):
            place = pl.ds(pl.multiple_of(index * chunk, chunk), chunk)
            for ref, start, at, used in column_pieces(wa_ref, wb_ref):
                part = dot_nn(n1_s[place, :], ref[:, start : start + used])
                qkv_ref[0, place, at : at + used] = part.astype(BF)
            return carry

        lax.fori_loop(0, 2, project, 0)

    block = pl.program_id(1) + shift
    blocks = key_blocks(block, last)
    mask = block_mask(segr_ref, segl_ref, block)
    columns = [pair_columns(pair, pairs // 2) for pair in range(pairs)]
    logits = [
        dot_nt(
            window_of(qkv_ref, blocks, col_k),
            stack_heads(qkv_ref[0, place_of(block), col_q : col_q + LANES]),
        )
        for col_q, col_k, _ in columns
    ]
    weights = [
        softmax_of(value + (bias_ref[pair] + mask)).astype(BF) for pair, value in enumerate(logits)
    ]
    mixed = [
        dot_tn(window_of(qkv_ref, blocks, col_v), value)
        for (_, _, col_v), value in zip(columns, weights)
    ]
    for pair, value in enumerate(mixed):
        out_ref[0, :, pair * LANES : (pair + 1) * LANES] = unstack_heads(value).astype(BF)


def attend_forward(place, x_own, x_halo, gain, halves, others, seg_rows, seg_lanes, bias):
    rows, half, model = x_own.shape
    own_blocks = half // BLOCK
    length = half + BLOCK
    pairs = bias.shape[0]
    last = length // BLOCK - 1
    widths = [h.shape[-1] for h in halves]
    width = sum(widths) - 2 * LANES
    steps = rows * own_blocks * pairs
    once = pl.Buffered(1)
    cost = pl.CostEstimate(
        flops=steps * 8 * BLOCK * 3 * BLOCK * LANES + 2 * rows * length * model * width,
        transcendentals=steps * 6 * BLOCK * BLOCK,
        bytes_accessed=rows * length * (width + 2 * model) * 2 + bias.size * 4 + model * width * 2,
    )
    return pl.pallas_call(
        functools.partial(attend_kernel, pairs, last),
        out_shape=(
            jax.ShapeDtypeStruct((rows, half, pairs * LANES), BF),
            jax.ShapeDtypeStruct((rows, length, width), BF),
            jax.ShapeDtypeStruct((rows, half, model), BF),
            jax.ShapeDtypeStruct((model, widths[0]), BF),
            jax.ShapeDtypeStruct((model, widths[1]), BF),
        ),
        grid_spec=pltpu.PrefetchScalarGridSpec(
            num_scalar_prefetch=1,
            grid=(rows, own_blocks),
            in_specs=[
                pl.BlockSpec((1, half, model), lambda r, i, s: (r, 0, 0)),
                pl.BlockSpec((1, BLOCK, model), lambda r, i, s: (r, 0, 0)),
                pl.BlockSpec((1, model), lambda r, i, s: (0, 0), pipeline_mode=once),
                pl.BlockSpec(halves[0].shape, lambda r, i, s: (0, 0, 0), pipeline_mode=once),
                pl.BlockSpec(others[0].shape, lambda r, i, s: (0, 0, 0), pipeline_mode=once),
                pl.BlockSpec(halves[1].shape, lambda r, i, s: (0, 0, 0), pipeline_mode=once),
                pl.BlockSpec(others[1].shape, lambda r, i, s: (0, 0, 0), pipeline_mode=once),
                pl.BlockSpec((1,) + seg_rows.shape[1:], lambda r, i, s: (r, 0, 0)),
                pl.BlockSpec((1,) + seg_lanes.shape[1:], lambda r, i, s: (r, 0, 0)),
                pl.BlockSpec(bias.shape, lambda r, i, s: (0, 0, 0), pipeline_mode=once),
            ],
            out_specs=[
                pl.BlockSpec((1, BLOCK, pairs * LANES), lambda r, i, s: (r, i, 0)),
                pl.BlockSpec((1, length, width), lambda r, i, s: (r, 0, 0)),
                pl.BlockSpec((1, half, model), lambda r, i, s: (r, 0, 0)),
                pl.BlockSpec((model, widths[0]), lambda r, i, s: (0, 0), pipeline_mode=once),
                pl.BlockSpec((model, widths[1]), lambda r, i, s: (0, 0), pipeline_mode=once),
            ],
            scratch_shapes=[pltpu.VMEM((length, model), BF)],
        ),
        compiler_params=pltpu.CompilerParams(
            dimension_semantics=("arbitrary", "arbitrary"), vmem_limit_bytes=48 << 20
        ),
        cost_estimate=cost,
        name="attend_forward",
    )(
        place,
        x_own,
        x_halo,
        gain,
        halves[0],
        others[0],
        halves[1],
        others[1],
        seg_rows,
        seg_lanes,
        bias,
    )


def fold_diagonals(block_sum):
    third = [block_sum[step * BLOCK : (step + 1) * BLOCK] for step in range(3)]
    cur = jnp.concatenate([third[2], third[1], third[0], jnp.zeros((BLOCK, BLOCK), F32)], axis=1)
    count = BLOCK // 2
    while count >= 8:
        cur = cur[count:] + pltpu.roll(cur[:count], count, 1)
        count //= 2
    return cur


def attend_back_kernel(
    pairs,
    last,
    own_blocks,
    shift_ref,
    qkv_ref,
    grad_ref,
    halo_ref,
    wo0_ref,
    wo1_ref,
    segr_ref,
    segl_ref,
    bias_ref,
    out_ref,
    diag_ref,
    heads_s,
    acc_ref,
    sum_ref,
):
    row, block = pl.program_id(0), pl.program_id(1)
    shift = shift_ref[0]
    blocks = key_blocks(block, last)
    mask = block_mask(segr_ref, segl_ref, block)
    owned = jnp.logical_and(block >= shift, block < shift + own_blocks)
    keep = jnp.where(owned, 1.0, 0.0)

    @pl.when(block == 0)
    def _():
        acc_ref[...] = jnp.zeros_like(acc_ref)
        wide = wo0_ref.shape[1]
        own = pl.ds(pl.multiple_of(shift * BLOCK, BLOCK), own_blocks * BLOCK)
        other = place_of((1 - shift) * own_blocks)
        for half, ref in enumerate((wo0_ref, wo1_ref)):
            columns = slice(half * wide, (half + 1) * wide)
            heads_s[own, columns] = dot_nn(grad_ref[0], ref[...]).astype(BF)
            heads_s[other, columns] = dot_nn(halo_ref[0], ref[...]).astype(BF)

    @pl.when(jnp.logical_and(block == 0, row == 0))
    def _():
        sum_ref[...] = jnp.zeros_like(sum_ref)

    columns = [pair_columns(pair, pairs // 2) for pair in range(pairs)]
    here = place_of(block)
    queries = [stack_heads(qkv_ref[0, here, c[0] : c[0] + LANES]) for c in columns]
    grads = [stack_heads(heads_s[here, p * LANES : (p + 1) * LANES]) for p in range(pairs)]
    keys = [window_of(qkv_ref, blocks, c[1]) for c in columns]
    logits = [dot_nt(k, q) for k, q in zip(keys, queries)]
    grads_w = [dot_nt(window_of(qkv_ref, blocks, c[2]), g) for c, g in zip(columns, grads)]
    probs = [softmax_of(value + (bias_ref[p] + mask)) for p, value in enumerate(logits)]
    grads_v = [dot_nn(p.astype(BF), g) for p, g in zip(probs, grads)]
    grads_l = [
        (p * (g - jnp.sum(p * g, axis=0, keepdims=True))).astype(BF)
        for p, g in zip(probs, grads_w)
    ]
    grads_k = [dot_nn(g, q) for g, q in zip(grads_l, queries)]
    grads_q = [dot_tn(k, g) for k, g in zip(keys, grads_l)]
    for pair, (col_q, col_k, col_v) in enumerate(columns):
        sum_ref[pair] += grads_l[pair].astype(F32) * keep
        acc_ref[here, col_q : col_q + LANES] = unstack_heads(grads_q[pair])
        for part in range(3):
            piece = slice(part * BLOCK, (part + 1) * BLOCK)
            acc_ref[place_of(blocks[part]), col_k : col_k + LANES] += grads_k[pair][piece]
            acc_ref[place_of(blocks[part]), col_v : col_v + LANES] += grads_v[pair][piece]

    @pl.when(block == last)
    def _():
        start = pl.multiple_of(shift * BLOCK, BLOCK)
        out_ref[0] = acc_ref[pl.ds(start, own_blocks * BLOCK), :].astype(BF)

    @pl.when(jnp.logical_and(block == last, row == pl.num_programs(0) - 1))
    def _():
        def fold(pair, carry):
            diag_ref[2 * pair] = fold_diagonals(sum_ref[pair, :, :BLOCK])
            diag_ref[2 * pair + 1] = fold_diagonals(sum_ref[pair, :, BLOCK:])
            return carry

        lax.fori_loop(0, pairs, fold, 0)


def attend_backward(
    shift, qkv, grad_attn, grad_halo, weights, out_cols, seg_rows, seg_lanes, bias
):
    rows, length, width = qkv.shape
    half, model = grad_attn.shape[1:]
    own_blocks = half // BLOCK
    pairs = bias.shape[0]
    last = length // BLOCK - 1
    steps = rows * (last + 1) * pairs
    out_at = weights.shape[1] // out_cols - 1
    once = pl.Buffered(1)
    cost = pl.CostEstimate(
        flops=steps * 20 * BLOCK * 3 * BLOCK * LANES + 4 * rows * length * model * out_cols,
        transcendentals=steps * 6 * BLOCK * BLOCK,
        bytes_accessed=qkv.size * 4 + grad_attn.size * 2 + bias.size * 4 + model * out_cols * 4,
    )
    return pl.pallas_call(
        functools.partial(attend_back_kernel, pairs, last, own_blocks),
        out_shape=(
            jax.ShapeDtypeStruct((rows, half, width), BF),
            jax.ShapeDtypeStruct((2 * pairs, 8, 4 * BLOCK), F32),
        ),
        grid_spec=pltpu.PrefetchScalarGridSpec(
            num_scalar_prefetch=1,
            grid=(rows, last + 1),
            in_specs=[
                pl.BlockSpec((1, length, width), lambda r, i, s: (r, 0, 0)),
                pl.BlockSpec((1, half, model), lambda r, i, s: (r, 0, 0)),
                pl.BlockSpec((1, BLOCK, model), lambda r, i, s: (r, 0, 0)),
                pl.BlockSpec((model, out_cols), lambda r, i, s: (0, out_at), pipeline_mode=once),
                pl.BlockSpec((model, out_cols), lambda r, i, s: (1, out_at), pipeline_mode=once),
                pl.BlockSpec((1,) + seg_rows.shape[1:], lambda r, i, s: (r, 0, 0)),
                pl.BlockSpec((1,) + seg_lanes.shape[1:], lambda r, i, s: (r, 0, 0)),
                pl.BlockSpec(bias.shape, lambda r, i, s: (0, 0, 0), pipeline_mode=once),
            ],
            out_specs=[
                pl.BlockSpec((1, half, width), lambda r, i, s: (r, 0, 0)),
                pl.BlockSpec((2 * pairs, 8, 4 * BLOCK), lambda r, i, s: (0, 0, 0)),
            ],
            scratch_shapes=[
                pltpu.VMEM((length, pairs * LANES), BF),
                pltpu.VMEM((length, width), F32),
                pltpu.VMEM(bias.shape, F32),
            ],
        ),
        compiler_params=pltpu.CompilerParams(
            dimension_semantics=("arbitrary", "arbitrary"), vmem_limit_bytes=56 << 20
        ),
        cost_estimate=cost,
        name="attend_backward",
    )(shift, qkv, grad_attn, grad_halo, weights, weights, seg_rows, seg_lanes, bias)


def input_kernel(grad_ref, wa_ref, wb_ref, x_ref, gain_ref, gmid_ref, out_ref, ggain_ref):
    grad_n1 = None
    for ref, start, at, used in column_pieces(wa_ref, wb_ref):
        part = dot_nt(grad_ref[:, at : at + used], ref[:, start : start + used])
        grad_n1 = part if grad_n1 is None else grad_n1 + part
    x = x_ref[...].astype(F32)
    r1 = inverse_rms(x)

    @pl.when(pl.program_id(0) == 0)
    def _():
        ggain_ref[...] = jnp.zeros_like(ggain_ref)

    ggain_ref[...] += jnp.sum(grad_n1 * x * r1, axis=0, keepdims=True)
    scaled = grad_n1 * gain_ref[...]
    inner = jnp.mean(scaled * x, axis=-1, keepdims=True)
    out_ref[...] = gmid_ref[...] + r1 * scaled - x * (r1 * r1 * r1 * inner)


def input_gradient(grad_qkv, part_a, part_b, x_own, gain, grad_middle):
    tokens, width = grad_qkv.shape
    model = x_own.shape[1]
    chunk = min(256, tokens)
    once = pl.Buffered(1)
    here = lambda i: (i, 0)
    whole = lambda i: (0, 0)
    return pl.pallas_call(
        input_kernel,
        out_shape=(
            jax.ShapeDtypeStruct((tokens, model), F32),
            jax.ShapeDtypeStruct((1, model), F32),
        ),
        grid=(tokens // chunk,),
        in_specs=[
            pl.BlockSpec((chunk, width), here),
            pl.BlockSpec(part_a.shape, whole, pipeline_mode=once),
            pl.BlockSpec(part_b.shape, whole, pipeline_mode=once),
            pl.BlockSpec((chunk, model), here),
            pl.BlockSpec((1, model), whole, pipeline_mode=once),
            pl.BlockSpec((chunk, model), here),
        ],
        out_specs=[pl.BlockSpec((chunk, model), here), pl.BlockSpec((1, model), whole)],
        compiler_params=pltpu.CompilerParams(
            dimension_semantics=("arbitrary",), vmem_limit_bytes=40 << 20
        ),
        cost_estimate=pl.CostEstimate(
            flops=2 * tokens * width * model,
            transcendentals=tokens,
            bytes_accessed=tokens * (2 * width + 10 * model) + 2 * width * model,
        ),
        name="input_gradient",
    )(grad_qkv, part_a, part_b, x_own, gain, grad_middle)


def bias_kernel(turned_ref, out_ref):
    for side in range(2):
        wide = jnp.broadcast_to(turned_ref[side], (3 * BLOCK, 4 * BLOCK))
        out = pltpu.roll(wide, BLOCK + 1, 1, stride=1, stride_axis=0)
        out_ref[0, :, side * BLOCK : (side + 1) * BLOCK] = out[:, :BLOCK]


def window_bias(turned):
    pairs = turned.shape[0] // 2
    return pl.pallas_call(
        bias_kernel,
        out_shape=jax.ShapeDtypeStruct((pairs, 3 * BLOCK, 2 * BLOCK), F32),
        grid=(pairs,),
        in_specs=[pl.BlockSpec((2, 1, 4 * BLOCK), lambda h: (h, 0, 0))],
        out_specs=pl.BlockSpec((1, 3 * BLOCK, 2 * BLOCK), lambda h: (h, 0, 0)),
        name="window_bias",
    )(turned[:, None, :])


def gelu_parts(gate):
    c, a = 0.7978845608028654, 0.044715
    square = gate * gate
    tanh = jnp.tanh(gate * (c + (c * a) * square))
    t = 0.5 + 0.5 * tanh
    slope = t + (0.5 * gate) * (1.0 - tanh * tanh) * (c + (3.0 * c * a) * square)
    return gate * t, slope


def split_rows(own_core, shard, grad, keep_ref, send_ref, where):
    for core in range(2):
        first, second = (keep_ref, send_ref) if core == 0 else (send_ref, keep_ref)

        @pl.when(own_core == core)
        def _():
            for group in range(grad.shape[0] // (2 * shard)):
                start = group * 2 * shard
                first[(0, group) + where] = grad[start : start + shard]
                second[(0, group) + where] = grad[start + shard : start + 2 * shard]


def feed_kernel(
    chunk,
    shard,
    core_ref,
    heads_ref,
    x_ref,
    gain_ref,
    cot_ref,
    wo0_ref,
    wo1_ref,
    wg_ref,
    wu_ref,
    wd_ref,
    out_ref,
    gmid_ref,
    gattn_ref,
    ggain_ref,
    keep_ref,
    send_ref,
    mid_s,
    n2_s,
    n2t_s,
    cott_s,
    hid_s,
    gg_s,
    gu_s,
    gn2_s,
):
    tokens, width = x_ref.shape
    step = pl.program_id(0) * pl.num_programs(1) + pl.program_id(1)
    final = pl.num_programs(0) * pl.num_programs(1) - 1
    half = heads_ref.shape[1] // 2

    def for_chunks(work):
        def one(index, carry):
            work(pl.ds(pl.multiple_of(index * chunk, chunk), chunk))
            return carry

        lax.fori_loop(0, tokens // chunk, one, 0)

    @pl.when(step == 0)
    def _():
        def work(place):
            middle = x_ref[place, :].astype(F32)
            middle = middle + dot_nt(heads_ref[place, :half], wo0_ref[...])
            middle = middle + dot_nt(heads_ref[place, half:], wo1_ref[...])
            mid_s[place, :] = middle
            out_ref[place, :] = middle
            normed = (middle * inverse_rms(middle) * gain_ref[...]).astype(BF)
            n2_s[place, :] = normed
            n2t_s[:, place] = normed.T
            cott_s[:, place] = cot_ref[place, :].T
            gn2_s[place, :] = jnp.zeros((chunk, width), F32)

        for_chunks(work)

    def work(place):
        n2, cot = n2_s[place, :], cot_ref[place, :]
        act, slope = gelu_parts(dot_nn(n2, wg_ref[...]))
        up = dot_nn(n2, wu_ref[...])
        grad_hidden = dot_nn(cot, wd_ref[...])
        hidden = (act * up).astype(BF)
        grad_gate = (grad_hidden * up * slope).astype(BF)
        grad_up = (grad_hidden * act).astype(BF)
        hid_s[place, :] = hidden
        gg_s[place, :] = grad_gate
        gu_s[place, :] = grad_up
        out_ref[place, :] += dot_nt(hidden, wd_ref[...])
        gn2_s[place, :] += dot_nt(grad_gate, wg_ref[...]) + dot_nt(grad_up, wu_ref[...])

    for_chunks(work)

    def store(kind, grad):
        split_rows(core_ref[0], shard, grad.astype(BF), keep_ref, send_ref, (kind,))

    store(0, dot_nn(n2t_s[...], gg_s[...]))
    store(1, dot_nn(n2t_s[...], gu_s[...]))
    store(2, dot_nn(cott_s[...], hid_s[...]))

    @pl.when(step == final)
    def _():
        ggain_ref[...] = jnp.zeros_like(ggain_ref)

        def work(place):
            middle, grad_n2 = mid_s[place, :], gn2_s[place, :]
            r2 = inverse_rms(middle)
            ggain_ref[...] += jnp.sum(grad_n2 * middle * r2, axis=0, keepdims=True)
            scaled = grad_n2 * gain_ref[...]
            inner = jnp.mean(scaled * middle, axis=-1, keepdims=True)
            grad = cot_ref[place, :].astype(F32) + r2 * scaled - middle * (r2 * r2 * r2 * inner)
            gmid_ref[place, :] = grad
            gattn_ref[place, :] = grad.astype(BF)

        for_chunks(work)


def feed_forward(core, heads_out, x_own, gain, cotangent, weights, hidden_cols, shard):
    tokens, width = x_own.shape
    wide = min(512, hidden_cols)
    steps = hidden_cols // wide
    out_cols = heads_out.shape[1] // 2
    out_at = 3 * hidden_cols // out_cols
    groups = width // (2 * shard)
    whole = lambda t, j, c: (0, 0)
    once = pl.Buffered(1)
    piece = jax.ShapeDtypeStruct((2, groups, 3, shard, hidden_cols), BF)
    piece_spec = pl.BlockSpec((1, groups, 3, shard, wide), lambda t, j, c: (t, 0, 0, 0, j))
    return pl.pallas_call(
        functools.partial(feed_kernel, min(FEED_CHUNK, tokens), shard),
        out_shape=(
            jax.ShapeDtypeStruct((tokens, width), F32),
            jax.ShapeDtypeStruct((tokens, width), F32),
            jax.ShapeDtypeStruct((tokens, width), BF),
            jax.ShapeDtypeStruct((1, width), F32),
            piece,
            piece,
        ),
        grid_spec=pltpu.PrefetchScalarGridSpec(
            num_scalar_prefetch=1,
            grid=(2, steps),
            in_specs=[
                pl.BlockSpec((tokens, 2 * out_cols), whole, pipeline_mode=once),
                pl.BlockSpec((tokens, width), whole, pipeline_mode=once),
                pl.BlockSpec((1, width), whole, pipeline_mode=once),
                pl.BlockSpec((tokens, width), whole, pipeline_mode=once),
                pl.BlockSpec((width, out_cols), lambda t, j, c: (0, out_at), pipeline_mode=once),
                pl.BlockSpec((width, out_cols), lambda t, j, c: (1, out_at), pipeline_mode=once),
                pl.BlockSpec((width, wide), lambda t, j, c: (t, j)),
                pl.BlockSpec((width, wide), lambda t, j, c: (t, steps + j)),
                pl.BlockSpec((width, wide), lambda t, j, c: (t, 2 * steps + j)),
            ],
            out_specs=[
                pl.BlockSpec((tokens, width), whole, pipeline_mode=once),
                pl.BlockSpec((tokens, width), whole, pipeline_mode=once),
                pl.BlockSpec((tokens, width), whole, pipeline_mode=once),
                pl.BlockSpec((1, width), whole, pipeline_mode=once),
                piece_spec,
                piece_spec,
            ],
            scratch_shapes=[
                pltpu.VMEM((tokens, width), F32),
                pltpu.VMEM((tokens, width), BF),
                pltpu.VMEM((width, tokens), BF),
                pltpu.VMEM((width, tokens), BF),
                pltpu.VMEM((tokens, wide), BF),
                pltpu.VMEM((tokens, wide), BF),
                pltpu.VMEM((tokens, wide), BF),
                pltpu.VMEM((tokens, width), F32),
            ],
        ),
        compiler_params=pltpu.CompilerParams(
            dimension_semantics=("arbitrary", "arbitrary"), vmem_limit_bytes=56 << 20
        ),
        cost_estimate=pl.CostEstimate(
            flops=2 * tokens * width * (18 * hidden_cols + 2 * out_cols),
            transcendentals=2 * tokens * hidden_cols,
            bytes_accessed=weights.size * 2 + tokens * width * 16 + 12 * width * hidden_cols,
        ),
        name="feed_forward",
    )(core, heads_out, x_own, gain, cotangent, weights, weights, weights, weights, weights)


def weight_kernel(shard, core_ref, n1_ref, gqkv_ref, gattn_ref, heads_ref, keep_ref, send_ref):
    wide = gqkv_ref.shape[1] // 3
    for index in range(4):
        columns = slice(index * wide, (index + 1) * wide)
        if index < 3:
            grad = dot_tn(n1_ref[...], gqkv_ref[:, columns])
        else:
            grad = dot_tn(gattn_ref[...], heads_ref[...])
        split_rows(
            core_ref[0], shard, grad.astype(BF), keep_ref, send_ref, (slice(None), columns)
        )


def weight_gradients(core, n1, grad_qkv, grad_attn, heads_out, shard):
    tokens, model = n1.shape
    wide = heads_out.shape[1] // 2
    groups = model // (2 * shard)
    whole = lambda t, c: (0, 0)
    half = lambda t, c: (0, t)
    once = pl.Buffered(1)
    piece = jax.ShapeDtypeStruct((2, groups, shard, 4 * wide), BF)
    piece_spec = pl.BlockSpec((1, groups, shard, 4 * wide), lambda t, c: (t, 0, 0, 0))
    return pl.pallas_call(
        functools.partial(weight_kernel, shard),
        out_shape=(piece, piece),
        grid_spec=pltpu.PrefetchScalarGridSpec(
            num_scalar_prefetch=1,
            grid=(2,),
            in_specs=[
                pl.BlockSpec((tokens, model), whole, pipeline_mode=once),
                pl.BlockSpec((tokens, 3 * wide), half),
                pl.BlockSpec((tokens, model), whole, pipeline_mode=once),
                pl.BlockSpec((tokens, wide), half),
            ],
            out_specs=[piece_spec, piece_spec],
        ),
        compiler_params=pltpu.CompilerParams(
            dimension_semantics=("arbitrary",), vmem_limit_bytes=40 << 20
        ),
        cost_estimate=pl.CostEstimate(
            flops=16 * tokens * model * wide,
            transcendentals=0,
            bytes_accessed=tokens * (4 * model + 16 * wide) + 16 * model * wide,
        ),
        name="weight_gradients",
    )(core, n1, grad_qkv, grad_attn, heads_out)


def body(
    hidden_in,
    segment_ids,
    bucket_of,
    attn_gain,
    w_query,
    w_key,
    w_value,
    w_attn_out,
    bias_table,
    ffn_gain,
    w_gate,
    w_up,
    w_down,
    cotangent,
):
    micro, local_rows, half, width = hidden_in.shape
    rows = micro * local_rows
    seq = segment_ids.shape[2]
    shard = attn_gain.shape[0]
    dp_count = lax.axis_size("dp")
    tp_index = lax.axis_index("tp")
    left_side = tp_index == 0
    local_heads = bias_table.shape[1]
    buckets = bias_table.shape[0]
    head_cols = w_query.shape[1]
    hidden_cols = w_gate.shape[1]
    own_blocks = half // BLOCK
    length = half + BLOCK

    def halo_of(own):
        send = jnp.where(left_side, own[:, half - BLOCK :], own[:, :BLOCK])
        return swap(send, "tp", 0)

    gains = jnp.pad(jnp.stack([attn_gain, ffn_gain], axis=1), ((0, 0), (0, LANES - 2)))
    first_shard = jnp.concatenate([w_query, w_key, w_value, gains], axis=1)
    second_shard = jnp.concatenate([w_gate, w_up, w_down.T, w_attn_out.T], axis=1)
    cut = first_shard.shape[1] // (2 * LANES) * LANES
    second = lax.all_gather(second_shard, ("tp", "dp"), axis=0, tiled=True)
    x_own = hidden_in.reshape(rows, half, width)
    x_halo = halo_of(x_own)
    seg = segment_ids.reshape(rows, seq)
    seg_ext = lax.dynamic_slice_in_dim(seg, tp_index * (half - BLOCK), length, 1)
    seg_pad = jnp.pad(seg_ext, ((0, 0), (BLOCK, BLOCK)), constant_values=-1)
    seg_rows = jnp.broadcast_to(seg_pad[:, :, None], seg_pad.shape + (LANES,))
    seg_lanes = seg_pad.reshape(rows, length // BLOCK + 2, BLOCK)
    other_table = swap(bias_table, "tp", 0)
    table = jnp.where(
        left_side,
        jnp.concatenate([bias_table, other_table], axis=1),
        jnp.concatenate([other_table, bias_table], axis=1),
    )
    near = bucket_of[seq - 2 * BLOCK - 1 : seq + 2 * BLOCK - 1][::-1]
    onehot = (near[None, :] == jnp.arange(buckets, dtype=jnp.int32)[:, None]).astype(F32)
    per_offset = lax.dot_general(
        table, onehot, (((0,), (0,)), ((), ())), precision=HIGHEST_PREC, preferred_element_type=F32
    )
    bias = window_bias(per_offset)
    shift = tp_index.astype(jnp.int32)[None]
    core = (lax.axis_index("dp") & 1).astype(jnp.int32)[None]

    near_halves, (bias, x_halo) = gather_halves(first_shard, cut, (bias, x_halo))
    far_halves = [swap(value, *stage_groups()[2]) for value in near_halves]
    gain_at = near_halves[1].shape[-1] // 2 - LANES
    gain_rows = [h[1][..., gain_at : gain_at + 2] for h in (near_halves, far_halves)]
    own_first = core[0] == 0
    gain_rows = jnp.stack(
        [
            jnp.where(own_first, gain_rows[0], gain_rows[1]),
            jnp.where(own_first, gain_rows[1], gain_rows[0]),
        ],
        axis=1,
    )
    both_gains = gain_rows.reshape(width, 2).T.astype(F32)
    gain1, gain2 = both_gains[:1], both_gains[1:]

    heads_out, qkv, n1, part_a, part_b = attend_forward(
        jnp.concatenate([shift, core]),
        x_own,
        x_halo,
        gain1,
        near_halves,
        far_halves,
        seg_rows,
        seg_lanes,
        bias,
    )
    heads_flat = heads_out.reshape(rows * half, 2 * head_cols)

    cot_flat = cotangent.reshape(rows * half, width)
    block_out, grad_middle, grad_attn, grad_gain2, keep, send = feed_forward(
        core,
        heads_flat,
        x_own.reshape(rows * half, width),
        gain2,
        cot_flat,
        second,
        hidden_cols,
        shard,
    )
    grad_attn_rows = grad_attn.reshape(rows, half, width)
    grad_halo = halo_of(grad_attn_rows)

    far, near, cores = stage_groups()
    stages = [("tp", 0)] + dp_stages()[:-1]

    def both_cores(keep, send, split):
        terms = [
            value.reshape((2,) * len(stages) + value.shape[2:]) for value in (keep, swap(send, *cores))
        ]
        total = keep.shape[-1]
        ranges = ((0, split), (split, total - split))
        return [Scatter([Term(t, stages, *cut) for t in terms]) for cut in ranges]

    feed = both_cores(keep, send, hidden_cols // 2)
    others, (grad_attn_rows, grad_halo) = start_near(feed, near, 0, (grad_attn_rows, grad_halo))

    grad_qkv, diagonals = attend_backward(
        shift, qkv, grad_attn_rows, grad_halo, second, head_cols, seg_rows, seg_lanes, bias
    )
    (grad_qkv,) = end_near(feed, others, (grad_qkv,))
    if len(near[0]) > 1:
        others, (grad_qkv,) = start_near(feed, near, 1, (grad_qkv,))
    grad_qkv = grad_qkv.reshape(rows * half, grad_qkv.shape[-1])
    keep_w, send_w = weight_gradients(
        core, n1.reshape(rows * half, width), grad_qkv, grad_attn, heads_flat, shard
    )
    tail = both_cores(keep_w, send_w, 2 * head_cols)
    if len(near[0]) > 1:
        end_near(feed, others)
    for stage in far[1:][::-1]:
        far_stage(feed, stage)
    others, (grad_qkv,) = start_near(tail, near, 0, (grad_qkv,))
    grad_in, grad_gain1 = input_gradient(
        grad_qkv, part_a, part_b, x_own.reshape(rows * half, width), gain1, grad_middle
    )
    end_near(tail, others)
    if len(near[0]) > 1:
        others, _ = start_near(tail, near, 1)
        end_near(tail, others)
    for stage in far[:1]:
        far_stage(feed, stage)
    for stage in far[::-1]:
        far_stage(tail, stage)
    feed_sums = jnp.concatenate([s.total() for s in feed], axis=-1)
    sums_a, sums_b = [s.total() for s in tail]

    diagonals_turned = [jnp.roll(diagonals[:, s], 7 - s, axis=1) for s in range(8)]
    offset_sums = diagonals_turned[0]
    for step in range(1, 8):
        offset_sums = offset_sums + diagonals_turned[step]
    table_sum = lax.dot_general(
        onehot,
        offset_sums,
        (((1,), (1,)), ((), ())),
        precision=HIGHEST_PREC,
        preferred_element_type=F32,
    )
    small = jnp.concatenate([grad_gain1[0], grad_gain2[0], table_sum.reshape(-1)])
    small = sum_everywhere(small.reshape(-1, LANES)).reshape(-1)
    dp_start = lax.axis_index("dp") * shard
    sum_gain1 = lax.dynamic_slice_in_dim(small[:width], dp_start, shard)
    sum_gain2 = lax.dynamic_slice_in_dim(small[width : 2 * width], dp_start, shard)
    sum_table = small[2 * width :].reshape(buckets, 2 * local_heads)
    sum_table = lax.dynamic_slice_in_dim(sum_table, tp_index * local_heads, local_heads, 1)

    shape = (micro, local_rows, half, width)
    return (
        block_out.reshape(shape),
        grad_in.reshape(shape),
        sum_gain1,
        sums_a[:, :head_cols],
        sums_a[:, head_cols:],
        sums_b[:, :head_cols],
        sums_b[:, head_cols:].T,
        sum_table,
        sum_gain2,
        feed_sums[0],
        feed_sums[1],
        feed_sums[2].T,
    )


def solution(mesh):
    in_specs = (
        P(None, "dp", "tp", None),
        P(None, "dp", None),
        P(),
        P("dp"),
        P("dp", "tp"),
        P("dp", "tp"),
        P("dp", "tp"),
        P("tp", "dp"),
        P(None, "tp"),
        P("dp"),
        P("dp", "tp"),
        P("dp", "tp"),
        P("tp", "dp"),
        P(None, "dp", "tp", None),
    )
    out_specs = (
        P(None, "dp", "tp", None),
        P(None, "dp", "tp", None),
        P("dp"),
        P("dp", "tp"),
        P("dp", "tp"),
        P("dp", "tp"),
        P("tp", "dp"),
        P(None, "tp"),
        P("dp"),
        P("dp", "tp"),
        P("dp", "tp"),
        P("tp", "dp"),
    )
    return jax.shard_map(body, mesh=mesh, in_specs=in_specs, out_specs=out_specs, check_vma=False)
```

profile of v0, /device:TPU:0, one launch (start us, length us, event | category | flops | bytes accessed | tf_op | source)
XLA Modules:
  0.0 310.3 jit_solution(11771854460440980714)
XLA Ops:
  7.3 1.8 pad_maximum_fusion.5
  10.8 4.1 %collective-permute-start = (bf16[48,1280]{1,0:T(8,128)(2,1)S(1)}, bf16[48,1280]{1,0:T(8,128)(2,1)S(1)}, u32[]{:S(2)}, u32[]{:S(2)}) collective-permute-start(bf16[48,1280]{1,0:T(8,128)(2,1)S(1)} %fusion.27), channel_id=1, source_target_pairs={{0,16},{2,18},{4,20},{6,22},{8,24},{10,26},{12,28},{14,30},{16,0},... | collective-permute-start | bytes 368648 | tf_op jit(solution)/shard_map/ppermute | solution.py:26
  14.9 6.0 %collective-permute-done = bf16[48,1280]{1,0:T(8,128)(2,1)S(1)} collective-permute-done((bf16[48,1280]{1,0:T(8,128)(2,1)S(1)}, bf16[48,1280]{1,0:T(8,128)(2,1)S(1)}, u32[]{:S(2)}, u32[]{:S(2)}) %collective-permute-start) | collective-permute-done | bytes 122912 | tf_op jit(solution)/shard_map/ppermute | solution.py:26
  22.5 1.5 collective-permute-start.4
  24.0 9.1 %collective-permute-done.1 = bf16[2,48,1280]{2,1,0:T(8,128)(2,1)S(1)} collective-permute-done((bf16[2,48,1280]{2,1,0:T(8,128)(2,1)S(1)}, bf16[2,48,1280]{2,1,0:T(8,128)(2,1)S(1)}, u32[]{:S(2)}, u32[]{:S(2)}) %collective-permute-start.1) | collective-permute-done | bytes 245792 | tf_op jit(solution)/shard_map/ppermute | solution.py:26
  34.7 1.6 collective-permute-start.5
  38.0 4.3 %window_bias.1.bias_ref = f32[6,384,256]{2,1,0:T(8,128)} custom-call(f32[12,1,512]{2,1,0:T(1,128)} %broadcast_in_dim.19.turned_ref), custom_call_target="tpu_custom_call" | custom-call | tf_op jit(solution)/shard_map/window_bias/pallas_call | solution.py:580
  42.8 11.0 %collective-permute-done.3 = bf16[2,2,48,640]{3,2,0,1:T(8,128)(2,1)S(1)} collective-permute-done((bf16[2,2,48,640]{3,2,0,1:T(8,128)(2,1)S(1)}, bf16[2,2,48,640]{3,2,0,1:T(8,128)(2,1)S(1)}, u32[]{:S(2)}, u32[]{:S(2)}) %collective-permute-start.3) | collective-permute-done | bytes 245792 | tf_op jit(solution)/shard_map/ppermute | solution.py:26
  54.1 1.9 collective-permute-start.8
  55.9 10.5 %collective-permute-done.6 = bf16[2,2,48,1280]{3,2,0,1:T(8,128)(2,1)S(1)} collective-permute-done((bf16[2,2,48,1280]{3,2,0,1:T(8,128)(2,1)S(1)}, bf16[2,2,48,1280]{3,2,0,1:T(8,128)(2,1)S(1)}, u32[]{:S(2)}, u32[]{:S(2)}) %collective-permute-start.6) | collective-permute-done | bytes 491552 | tf_op jit(solution)/shard_map/ppermute | solution.py:26
  73.5 24.0 %attend_forward.1 = (bf16[2,512,768]{2,1,0:T(8,128)(2,1)}, bf16[2,640,2304]{2,1,0:T(8,128)(2,1)}, bf16[2,512,768]{2,1,0:T(8,128)(2,1)}, bf16[768,1280]{1,0:T(8,128)(2,1)}, bf16[768,1280]{1,0:T(8,128)(2,1)}) custom-call(s32[2]{0:T(128)S(1)} %pad_add_fusion.shift_ref, bf16[2,512,768]{2,1,0:T(8,128)(2,1)} %bitcast.288, ...), custom_call_target="tpu_custom_call" | custom-call | flops 6945767424 | bytes 15728640 | tf_op jit(solution)/shard_map/attend_forward/pallas_call | solution.py:323
  97.5 9.5 %all-gather.2.cloned.1.call-done.wo0_ref.wo1_ref.wg_ref.wu_ref.wd_ref = bf16[1536,3456]{1,0:T(8,128)(2,1)} async-done(((bf16[48,3456]{1,0:T(8,128)(2,1)}), bf16[1536,3456]{1,0:T(8,128)(2,1)}) %all-gather.2.cloned.1.call-update) | async-done | bytes 10616848 | tf_op jit(solution)/shard_map/all_gather | solution.py:859
  106.9 46.4 %feed_forward.1 = (f32[1024,768]{1,0:T(8,128)}, f32[1024,768]{1,0:T(8,128)}, bf16[1024,768]{1,0:T(8,128)(2,1)}, f32[1,768]{1,0:T(1,128)}, bf16[2,8,3,48,1024]{4,...) custom-call(s32[1]{0:T(128)} %bitcast.core_ref, bf16[1024,768]{1,0:T(8,128)(2,1)} %bitcast.296, ...), custom_call_target="tpu_custom_call" | custom-call | flops 30198988800 | bytes 32636928 | tf_op jit(solution)/shard_map/feed_forward/pallas_call | solution.py:718
  156.3 5.4 %collective-permute-done.10 = bf16[2,8,3,48,1024]{4,3,2,1,0:T(8,128)(2,1)} collective-permute-done((bf16[2,8,3,48,1024]{4,3,2,1,0:T(8,128)(2,1)}, bf16[2,8,3,48,1024]{4,3,2,1,0:T(8,128)(2,1)}, u32[]{:S(2)}, u32[]{:S(2)}) %collective-permute-start.10) | collective-permute-done | bytes 4718624 | tf_op jit(solution)/shard_map/ppermute | solution.py:26
  161.7 3.1 %fusion = bf16[2,2,2,3,48,512]{5,4,3,2,1,0:T(8,128)(2,1)} fusion(bf16[2,2,2,2,3,48,1024]{6,5,4,3,2,1,0:T(8,128)(2,1)} %bitcast.27, s32[]{:T(128)S(6)} %select_n.152, bf16[2,2,2,2,3,48,1024]{6,5,4,3,2,1,0:T(8,128)(2,1)} %bitcast.299), kind=kLoop, calls=%fused_computation.2 | loop fusion | flops 2359296 | bytes 3538948 | tf_op jit(solution)/shard_map/convert_element_type | solution.py:106
  164.8 2.0 fusion.1
  169.1 40.1 %attend_backward.1 = (bf16[2,512,2304]{2,1,0:T(8,128)(2,1)}, f32[12,8,512]{2,1,0:T(8,128)}) custom-call(s32[1]{0:T(128)} %bitcast.1.shift_ref, bf16[2,640,2304]{2,1,0:T(8,128)(2,1)} %get-tuple-element.58.qkv_ref, bf16[2,512,768]{2,1,0:T(8,128)(2,1)} %bitcast.293, bf16[2,128,768]{2,1,0:T(8,128)(2,1)} %copy-done.23, ...), custom_call_target="tpu_custom_call" | custom-call | flops 9059696640 | bytes 16908288 | tf_op jit(solution)/shard_map/attend_backward/pallas_call | solution.py:481
  209.3 3.7 %fusion.2 = (bf16[2,2,3,48,512]{4,3,2,1,0:T(8,128)(2,1)}, bf16[2,2,3,48,512]{4,3,2,1,0:T(8,128)(2,1)}) fusion(s32[]{:T(128)S(6)} %select_n.152, bf16[2,2,2,2,3,48,1024]{6,5,4,3,2,1,0:T(8,128)(2,1)} %bitcast.27, s32[]{:T(128)S(6)} %select_n.154, bf16[2,2,2,2,3,48,1024]{6,5,4,3,2,1,0:T(8,128)(2,1)} %bitcast.301, ...), kind=kLoop, calls=%fused_computation.5 | loop fusion | flops 3538944 | bytes 4718608 | tf_op jit(solution)/shard_map/convert_element_type | solution.py:106
  213.1 2.3 copy-done.9
  215.4 10.2 %weight_gradients.1 = (bf16[2,8,48,1536]{3,2,1,0:T(8,128)(2,1)S(1)}, bf16[2,8,48,1536]{3,2,1,0:T(8,128)(2,1)}) custom-call(s32[1]{0:T(128)} %bitcast.core_ref, bf16[1024,768]{1,0:T(8,128)(2,1)S(1)} %bitcast.298, bf16[1024,2304]{1,0:T(8,128)(2,1)S(1)} %bitcast.294, bf16[1024,768]{1,0:T(8,128)(2,1)S(1)} %copy-done.5, bf16[1024,768]{1,0:T(8,128)(2,1)S(1)} %bitcast.297), custom_call_target="tpu_custom_call" | custom-call | flops 4831838208 | bytes 14155776 | tf_op jit(solution)/shard_map/weight_gradients/pallas_call | solution.py:795
  232.6 9.1 %collective-permute-done.26 = bf16[2,2,3,48,512]{4,3,2,1,0:T(8,128)(2,1)} collective-permute-done((bf16[2,2,3,48,512]{4,3,2,1,0:T(8,128)(2,1)}, bf16[2,2,3,48,512]{4,3,2,1,0:T(8,128)(2,1)}, u32[]{:S(2)}, u32[]{:S(2)}) %collective-permute-start.26) | collective-permute-done | bytes 589856 | tf_op jit(solution)/shard_map/ppermute | solution.py:26
  242.6 2.0 fusion.7
  246.9 2.2 fusion.4
  253.5 1.9 copy-done.13
  255.3 1.5 copy-done.15
  256.9 7.3 %input_gradient.1 = (f32[1024,768]{1,0:T(8,128)}, f32[1,768]{1,0:T(1,128)S(1)}) custom-call(bf16[1024,2304]{1,0:T(8,128)(2,1)S(1)} %bitcast.295, bf16[768,1280]{1,0:T(8,128)(2,1)S(1)} %copy-done.14, bf16[768,1280]{1,0:T(8,128)(2,1)S(1)} %copy-done.15, bf16[1024,768]{1,0:T(8,128)(2,1)S(1)} %bitcast.291, f32[1,768]{1,0:T(1,128)S(1)} %get-tuple-element.165.gain_ref, ...), custom_call_target="tpu_custom_call" | custom-call | flops 3623878656 | bytes 16121856 | tf_op jit(solution)/shard_map/input_gradient/pallas_call | solution.py:543
  264.9 1.6 fusion.12
  269.2 1.5 fusion.9
  272.5 1.6 collective-permute-start.17
  281.6 5.6 %collective-permute-done.29 = bf16[3,48,1024]{2,1,0:T(8,128)(2,1)S(1)} collective-permute-done((bf16[3,48,1024]{2,1,0:T(8,128)(2,1)S(1)}, bf16[3,48,1024]{2,1,0:T(8,128)(2,1)S(1)}, u32[]{:S(2)}, u32[]{:S(2)}) %collective-permute-start.29) | collective-permute-done | bytes 294944 | tf_op jit(solution)/shard_map/ppermute | solution.py:26
  287.2 1.6 fusion.10
  293.8 7.7 %collective-permute-done.25 = bf16[48,1536]{1,0:T(8,128)(2,1)S(1)} collective-permute-done((bf16[48,1536]{1,0:T(8,128)(2,1)S(1)}, bf16[48,1536]{1,0:T(8,128)(2,1)S(1)}, u32[]{:S(2)}, u32[]{:S(2)}) %collective-permute-start.25) | collective-permute-done | bytes 147488 | tf_op jit(solution)/shard_map/ppermute | solution.py:26
  (169 shorter events, 53.7 us)
Async XLA Ops:
  7.2 60.4 %copy-start = (s32[2,1,1024]{2,1,0:T(1,128)S(1)}, s32[2,1,1024]{2,1,0:T(1,128)}, u32[]{:S(2)}) copy-start(s32[2,1,1024]{2,1,0:T(1,128)} %param.15) | copy-start | bytes 24580
  7.2 99.7 %all-gather.2.cloned.1.call-start = ((), (), s32[]{:S(2)}) async-start(), calls=%async_computation | async-start | bytes 10948608 | tf_op jit(solution)/shard_map/all_gather | solution.py:859
  10.8 10.1 %collective-permute-start = (bf16[48,1280]{1,0:T(8,128)(2,1)S(1)}, bf16[48,1280]{1,0:T(8,128)(2,1)S(1)}, u32[]{:S(2)}, u32[]{:S(2)}) collective-permute-start(bf16[48,1280]{1,0:T(8,128)(2,1)S(1)} %fusion.27), channel_id=1, source_target_pairs={{0,16},{2,18},{4,20},{6,22},{8,24},{10,26},{12,28},{14,30},{16,0},... | collective-permute-start | bytes 368648 | tf_op jit(solution)/shard_map/ppermute | solution.py:26
  21.7 11.4 %collective-permute-start.1 = (bf16[2,48,1280]{2,1,0:T(8,128)(2,1)S(1)}, bf16[2,48,1280]{2,1,0:T(8,128)(2,1)S(1)}, u32[]{:S(2)}, u32[]{:S(2)}) collective-permute-start(bf16[2,48,1280]{2,1,0:T(8,128)(2,1)S(1)} %pad_maximum_fusion.9), channel_id=1, source_target_pairs={{0,8},{2,10},{4,12},{6,14},{8,0},{10,2},{12,4},{14,6},{16,24},{18,... | collective-permute-start | bytes 737288 | tf_op jit(solution)/shard_map/ppermute | solution.py:26
  22.5 14.7 %collective-permute-start.4 = (f32[32,6]{0,1:T(8,128)S(1)}, f32[32,6]{0,1:T(8,128)S(1)}, u32[]{:S(2)}, u32[]{:S(2)}) collective-permute-start(f32[32,6]{0,1:T(8,128)S(1)} %copy-done.22), channel_id=1, source_target_pairs={{0,1},{1,0},{2,3},{3,2},{4,5},{5,4},{6,7},{7,6},{8,9},{9,8},{10,11... | collective-permute-start | bytes 2312 | tf_op jit(solution)/shard_map/ppermute | solution.py:26
  33.3 9.4 %collective-permute-start.2 = (bf16[2,2,48,640]{3,2,0,1:T(8,128)(2,1)S(1)}, bf16[2,2,48,640]{3,2,0,1:T(8,128)(2,1)S(1)}, u32[]{:S(2)}, u32[]{:S(2)}) collective-permute-start(bf16[2,2,48,640]{3,2,0,1:T(8,128)(2,1)S(1)} %get-tuple-element.144), channel_id=1, source_target_pairs={{0,4},{2,6},{4,0},{6,2},{8,12},{10,14},{12,8},{14,10},{16,20},{18,... | collective-permute-start | bytes 737288 | tf_op jit(solution)/shard_map/ppermute | solution.py:26
  34.7 19.3 %collective-permute-start.5 = (bf16[2,128,768]{2,1,0:T(8,128)(2,1)S(1)}, bf16[2,128,768]{2,1,0:T(8,128)(2,1)S(1)}, u32[]{:S(2)}, u32[]{:S(2)}) collective-permute-start(bf16[2,128,768]{2,1,0:T(8,128)(2,1)S(1)} %slice_select_fusion.1), channel_id=1, source_target_pairs={{0,1},{1,0},{2,3},{3,2},{4,5},{5,4},{6,7},{7,6},{8,9},{9,8},{10,11... | collective-permute-start | bytes 1179656 | tf_op jit(solution)/shard_map/ppermute | solution.py:26
  42.3 11.6 %collective-permute-start.3 = (bf16[2,2,48,640]{3,2,0,1:T(8,128)(2,1)S(1)}, bf16[2,2,48,640]{3,2,0,1:T(8,128)(2,1)S(1)}, u32[]{:S(2)}, u32[]{:S(2)}) collective-permute-start(bf16[2,2,48,640]{3,2,0,1:T(8,128)(2,1)S(1)} %get-tuple-element.143), channel_id=1, source_target_pairs={{0,1},{1,0},{2,3},{3,2},{4,5},{5,4},{6,7},{7,6},{8,9},{9,8},{10,11... | collective-permute-start | bytes 737288 | tf_op jit(solution)/shard_map/ppermute | solution.py:26
  54.0 12.4 %collective-permute-start.6 = (bf16[2,2,48,1280]{3,2,0,1:T(8,128)(2,1)S(1)}, bf16[2,2,48,1280]{3,2,0,1:T(8,128)(2,1)S(1)}, u32[]{:S(2)}, u32[]{:S(2)}) collective-permute-start(bf16[2,2,48,1280]{3,2,0,1:T(8,128)(2,1)S(1)} %pad_maximum_fusion.4), channel_id=1, source_target_pairs={{0,4},{2,6},{4,0},{6,2},{8,12},{10,14},{12,8},{14,10},{16,20},{18,... | collective-permute-start | bytes 1474568 | tf_op jit(solution)/shard_map/ppermute | solution.py:26
  54.1 12.7 %collective-permute-start.8 = (bf16[2,2,2,48,640]{4,3,0,1,2:T(8,128)(2,1)S(1)}, bf16[2,2,2,48,640]{4,3,0,1,2:T(8,128)(2,1)S(1)}, u32[]{:S(2)}, u32[]{:S(2)}) collective-permute-start(bf16[2,2,2,48,640]{4,3,0,1,2:T(8,128)(2,1)S(1)} %pad_maximum_fusion.3), channel_id=1, source_target_pairs={{0,1},{1,0},{2,3},{3,2},{4,5},{5,4},{6,7},{7,6},{8,9},{9,8},{10,11... | collective-permute-start | bytes 1474568 | tf_op jit(solution)/shard_map/ppermute | solution.py:26
  66.7 2.6 collective-permute-start.7
  67.0 4.2 %collective-permute-start.9 = (bf16[8,48,1280]{2,1,0:T(8,128)(2,1)S(1)}, bf16[8,48,1280]{2,1,0:T(8,128)(2,1)}, u32[]{:S(2)}, u32[]{:S(2)}) collective-permute-start(bf16[8,48,1280]{2,1,0:T(8,128)(2,1)S(1)} %bitcast.286), channel_id=1, source_target_pairs={{0,2},{2,0},{4,6},{6,4},{8,10},{10,8},{12,14},{14,12},{16,18},{18,... | collective-permute-start | bytes 2949128 | tf_op jit(solution)/shard_map/ppermute | solution.py:26
  153.4 8.3 %collective-permute-start.10 = (bf16[2,8,3,48,1024]{4,3,2,1,0:T(8,128)(2,1)}, bf16[2,8,3,48,1024]{4,3,2,1,0:T(8,128)(2,1)}, u32[]{:S(2)}, u32[]{:S(2)}) collective-permute-start(bf16[2,8,3,48,1024]{4,3,2,1,0:T(8,128)(2,1)} %get-tuple-element.54), channel_id=1, source_target_pairs={{0,2},{2,0},{4,6},{6,4},{8,10},{10,8},{12,14},{14,12},{16,18},{18,... | collective-permute-start | bytes 14155784 | tf_op jit(solution)/shard_map/ppermute | solution.py:26
  154.9 12.0 %collective-permute-start.11 = (bf16[2,128,768]{2,1,0:T(8,128)(2,1)S(1)}, bf16[2,128,768]{2,1,0:T(8,128)(2,1)S(1)}, u32[]{:S(2)}, u32[]{:S(2)}) collective-permute-start(bf16[2,128,768]{2,1,0:T(8,128)(2,1)S(1)} %slice_select_fusion), channel_id=1, source_target_pairs={{0,1},{1,0},{2,3},{3,2},{4,5},{5,4},{6,7},{7,6},{8,9},{9,8},{10,11... | collective-permute-start | bytes 1179656 | tf_op jit(solution)/shard_map/ppermute | solution.py:26
  166.9 42.4 %collective-permute-start.12 = (bf16[2,2,2,3,48,512]{5,4,3,2,1,0:T(8,128)(2,1)}, bf16[2,2,2,3,48,512]{5,4,3,2,1,0:T(8,128)(2,1)S(1)}, u32[]{:S(2)}, u32[]{:S(2)}) collective-permute-start(bf16[2,2,2,3,48,512]{5,4,3,2,1,0:T(8,128)(2,1)} %fusion), channel_id=1, source_target_pairs={{0,4},{2,6},{4,0},{6,2},{8,12},{10,14},{12,8},{14,10},{16,20},{18,... | collective-permute-start | bytes 3538952 | tf_op jit(solution)/shard_map/ppermute | solution.py:26
  168.3 40.9 %collective-permute-start.13 = (bf16[2,2,2,3,48,512]{5,4,3,0,2,1:T(8,128)(2,1)S(1)}, bf16[2,2,2,3,48,512]{5,4,3,0,2,1:T(8,128)(2,1)S(1)}, u32[]{:S(2)}, u32[]{:S(2)}) collective-permute-start(bf16[2,2,2,3,48,512]{5,4,3,0,2,1:T(8,128)(2,1)S(1)} %copy.104), channel_id=1, source_target_pairs={{0,1},{1,0},{2,3},{3,2},{4,5},{5,4},{6,7},{7,6},{8,9},{9,8},{10,11... | collective-permute-start | bytes 3538952 | tf_op jit(solution)/shard_map/ppermute | solution.py:26
  225.6 21.3 %collective-permute-start.14 = (bf16[2,8,48,1536]{3,2,1,0:T(8,128)(2,1)}, bf16[2,8,48,1536]{3,2,1,0:T(8,128)(2,1)}, u32[]{:S(2)}, u32[]{:S(2)}) collective-permute-start(bf16[2,8,48,1536]{3,2,1,0:T(8,128)(2,1)} %get-tuple-element.67), channel_id=1, source_target_pairs={{0,2},{2,0},{4,6},{6,4},{8,10},{10,8},{12,14},{14,12},{16,18},{18,... | collective-permute-start | bytes 7077896 | tf_op jit(solution)/shard_map/ppermute | solution.py:26
  225.6 16.1 %collective-permute-start.26 = (bf16[2,2,3,48,512]{4,3,2,1,0:T(8,128)(2,1)}, bf16[2,2,3,48,512]{4,3,2,1,0:T(8,128)(2,1)}, u32[]{:S(2)}, u32[]{:S(2)}) collective-permute-start(bf16[2,2,3,48,512]{4,3,2,1,0:T(8,128)(2,1)} %get-tuple-element.78), channel_id=1, source_target_pairs={{0,1},{1,0},{2,3},{3,2},{4,5},{5,4},{6,7},{7,6},{8,9},{9,8},{10,11... | collective-permute-start | bytes 1769480 | tf_op jit(solution)/shard_map/ppermute | solution.py:26
  226.8 15.8 %collective-permute-start.27 = (bf16[2,2,3,48,512]{4,3,2,1,0:T(8,128)(2,1)}, bf16[2,2,3,48,512]{4,3,2,1,0:T(8,128)(2,1)}, u32[]{:S(2)}, u32[]{:S(2)}) collective-permute-start(bf16[2,2,3,48,512]{4,3,2,1,0:T(8,128)(2,1)} %get-tuple-element.79), channel_id=1, source_target_pairs={{0,4},{2,6},{4,0},{6,2},{8,12},{10,14},{12,8},{14,10},{16,20},{18,... | collective-permute-start | bytes 1769480 | tf_op jit(solution)/shard_map/ppermute | solution.py:26
  245.5 19.4 %collective-permute-start.28 = (bf16[2,3,48,1024]{3,2,1,0:T(8,128)(2,1)}, bf16[2,3,48,1024]{3,2,1,0:T(8,128)(2,1)}, u32[]{:S(2)}, u32[]{:S(2)}) collective-permute-start(bf16[2,3,48,1024]{3,2,1,0:T(8,128)(2,1)} %pad_maximum_fusion.2), channel_id=1, source_target_pairs={{0,8},{2,10},{4,12},{6,14},{8,0},{10,2},{12,4},{14,6},{16,24},{18,... | collective-permute-start | bytes 1769480 | tf_op jit(solution)/shard_map/ppermute | solution.py:26
  250.4 18.8 %collective-permute-start.20 = (bf16[2,2,2,48,768]{4,3,2,1,0:T(8,128)(2,1)}, bf16[2,2,2,48,768]{4,3,2,1,0:T(8,128)(2,1)}, u32[]{:S(2)}, u32[]{:S(2)}) collective-permute-start(bf16[2,2,2,48,768]{4,3,2,1,0:T(8,128)(2,1)} %fusion.4), channel_id=1, source_target_pairs={{0,4},{2,6},{4,0},{6,2},{8,12},{10,14},{12,8},{14,10},{16,20},{18,... | collective-permute-start | bytes 1769480 | tf_op jit(solution)/shard_map/ppermute | solution.py:26
  252.1 17.2 %collective-permute-start.22 = (bf16[2,2,2,48,768]{4,3,0,2,1:T(8,128)(2,1)}, bf16[2,2,2,48,768]{4,3,0,2,1:T(8,128)(2,1)}, u32[]{:S(2)}, u32[]{:S(2)}) collective-permute-start(bf16[2,2,2,48,768]{4,3,0,2,1:T(8,128)(2,1)} %copy.120), channel_id=1, source_target_pairs={{0,1},{1,0},{2,3},{3,2},{4,5},{5,4},{6,7},{7,6},{8,9},{9,8},{10,11... | collective-permute-start | bytes 1769480 | tf_op jit(solution)/shard_map/ppermute | solution.py:26
  264.2 3.7 %collective-permute-start.15 = (f32[15,128]{1,0:T(8,128)S(1)}, f32[15,128]{1,0:T(8,128)S(1)}, u32[]{:S(2)}, u32[]{:S(2)}) collective-permute-start(f32[15,128]{1,0:T(8,128)S(1)} %maximum_bitcast_fusion), channel_id=1, source_target_pairs={{0,1},{1,0},{2,3},{3,2},{4,5},{5,4},{6,7},{7,6},{8,9},{9,8},{10,11... | collective-permute-start | bytes 23048 | tf_op jit(solution)/shard_map/ppermute | solution.py:26
  267.9 4.6 %collective-permute-start.16 = (f32[15,128]{1,0:T(8,128)S(1)}, f32[15,128]{1,0:T(8,128)S(1)}, u32[]{:S(2)}, u32[]{:S(2)}) collective-permute-start(f32[15,128]{1,0:T(8,128)S(1)} %fusion.71), channel_id=1, source_target_pairs={{0,16},{2,18},{4,20},{6,22},{8,24},{10,26},{12,28},{14,30},{16,0},... | collective-permute-start | bytes 23048 | tf_op jit(solution)/shard_map/ppermute | solution.py:26
  270.7 6.8 %collective-permute-start.21 = (bf16[2,2,48,768]{3,2,1,0:T(8,128)(2,1)S(1)}, bf16[2,2,48,768]{3,2,1,0:T(8,128)(2,1)S(1)}, u32[]{:S(2)}, u32[]{:S(2)}) collective-permute-start(bf16[2,2,48,768]{3,2,1,0:T(8,128)(2,1)S(1)} %get-tuple-element.130), channel_id=1, source_target_pairs={{0,1},{1,0},{2,3},{3,2},{4,5},{5,4},{6,7},{7,6},{8,9},{9,8},{10,11... | collective-permute-start | bytes 884744 | tf_op jit(solution)/shard_map/ppermute | solution.py:26
  271.2 6.8 %collective-permute-start.23 = (bf16[2,2,48,768]{3,2,1,0:T(8,128)(2,1)S(1)}, bf16[2,2,48,768]{3,2,1,0:T(8,128)(2,1)S(1)}, u32[]{:S(2)}, u32[]{:S(2)}) collective-permute-start(bf16[2,2,48,768]{3,2,1,0:T(8,128)(2,1)S(1)} %get-tuple-element.131), channel_id=1, source_target_pairs={{0,4},{2,6},{4,0},{6,2},{8,12},{10,14},{12,8},{14,10},{16,20},{18,... | collective-permute-start | bytes 884744 | tf_op jit(solution)/shard_map/ppermute | solution.py:26
  272.5 3.7 %collective-permute-start.17 = (f32[15,128]{1,0:T(8,128)S(1)}, f32[15,128]{1,0:T(8,128)S(1)}, u32[]{:S(2)}, u32[]{:S(2)}) collective-permute-start(f32[15,128]{1,0:T(8,128)S(1)} %fusion.73), channel_id=1, source_target_pairs={{0,8},{2,10},{4,12},{6,14},{8,0},{10,2},{12,4},{14,6},{16,24},{18,... | collective-permute-start | bytes 23048 | tf_op jit(solution)/shard_map/ppermute | solution.py:26
  274.1 13.1 %collective-permute-start.29 = (bf16[3,48,1024]{2,1,0:T(8,128)(2,1)S(1)}, bf16[3,48,1024]{2,1,0:T(8,128)(2,1)S(1)}, u32[]{:S(2)}, u32[]{:S(2)}) collective-permute-start(bf16[3,48,1024]{2,1,0:T(8,128)(2,1)S(1)} %pad_maximum_fusion.7), channel_id=1, source_target_pairs={{0,16},{2,18},{4,20},{6,22},{8,24},{10,26},{12,28},{14,30},{16,0},... | collective-permute-start | bytes 884744 | tf_op jit(solution)/shard_map/ppermute | solution.py:26
  276.2 12.6 %collective-permute-start.18 = (f32[15,128]{1,0:T(8,128)S(1)}, f32[15,128]{1,0:T(8,128)S(1)}, u32[]{:S(2)}, u32[]{:S(2)}) collective-permute-start(f32[15,128]{1,0:T(8,128)S(1)} %add.250), channel_id=1, source_target_pairs={{0,4},{2,6},{4,0},{6,2},{8,12},{10,14},{12,8},{14,10},{16,20},{18,... | collective-permute-start | bytes 23048 | tf_op jit(solution)/shard_map/ppermute | solution.py:26
  280.1 11.1 %collective-permute-start.24 = (bf16[2,48,1536]{2,1,0:T(8,128)(2,1)}, bf16[2,48,1536]{2,1,0:T(8,128)(2,1)}, u32[]{:S(2)}, u32[]{:S(2)}) collective-permute-start(bf16[2,48,1536]{2,1,0:T(8,128)(2,1)} %pad_maximum_fusion.6), channel_id=1, source_target_pairs={{0,8},{2,10},{4,12},{6,14},{8,0},{10,2},{12,4},{14,6},{16,24},{18,... | collective-permute-start | bytes 884744 | tf_op jit(solution)/shard_map/ppermute | solution.py:26
  288.8 1.2 collective-permute-start.19
  292.5 9.0 %collective-permute-start.25 = (bf16[48,1536]{1,0:T(8,128)(2,1)S(1)}, bf16[48,1536]{1,0:T(8,128)(2,1)S(1)}, u32[]{:S(2)}, u32[]{:S(2)}) collective-permute-start(bf16[48,1536]{1,0:T(8,128)(2,1)S(1)} %pad_maximum_fusion.11), channel_id=1, source_target_pairs={{0,16},{2,18},{4,20},{6,22},{8,24},{10,26},{12,28},{14,30},{16,0},... | collective-permute-start | bytes 442376 | tf_op jit(solution)/shard_map/ppermute | solution.py:26
  (23 other events, 191.1 us)
Sparse Core Ops, SparseCore 0:
  11.5 95.4 all-gather.1
where the time goes:
time: 311 us; the launch traced here: 310 us
  Pallas kernels  132 us (42%)
  waiting for transfers between devices  80.1 us (26%)
  other arithmetic  32.4 us (10%)
  starting transfers between devices  30.7 us (10%)
  local copies, waits for them, and re-layouts  19.3 us (6%)
  between operations  14.6 us (5%)
    ppermute x30, waiting for transfers between devices, swap(): return lax.ppermute(value, axis, [(i, i ^ 1 << bit) for i in range(count)])  70.6 us
    pallas_call x1, Pallas kernels, feed_forward(): pl.pallas_call(functools.partial(feed_kernel, min(FEED_CHUNK, tokens), sh...  46.4 us
    pallas_call x1, Pallas kernels, attend_backward(): pl.pallas_call(functools.partial(attend_back_kernel, pairs, last, own_blo...  40.1 us
    ppermute x30, starting transfers between devices, swap(): return lax.ppermute(value, axis, [(i, i ^ 1 << bit) for i in range(count)])  30.6 us
    pallas_call x1, Pallas kernels, attend_forward(): pl.pallas_call(functools.partial(attend_kernel, pairs, last), out_shape=(...  24 us
    convert_element_type x10, other arithmetic, split(): return send.astype(BF)  20.1 us
    pallas_call x1, Pallas kernels, weight_gradients(): pl.pallas_call(functools.partial(weight_kernel, shard), out_shape=(piece,...  10.2 us
    all_gather x1, waiting for transfers between devices, body(): second = lax.all_gather(second_shard, ('tp', 'dp'), axis=0, tiled=True)  9.5 us
  transfers between devices with their start and end apart: 31, of which 17 were waited for; matrix products, arithmetic and copies ran while one was open for 11% of the time, Pallas kernels for 24%

commit v1 on v0

--- a/solution.py
+++ b/solution.py
@@ -24,6 +24,10 @@
 def swap(value, axis, bit):
     count = lax.axis_size(axis)
     return lax.ppermute(value, axis, [(i, i ^ (1 << bit)) for i in range(count)])
+
+
+def swap_flat(value, axis, bit):
+    return swap(value.reshape(-1, value.shape[-1]), axis, bit).reshape(value.shape)
 
 
 def own_bit(axis, bit):
@@ -63,12 +67,39 @@
         piece, have = merge(piece, have, stage)
     halves = [(piece[..., :cut], have), (piece[..., cut:], have)]
     for step in range(len(orders[0])):
-        if step == len(orders[0]) - 1:
-            values, before_last = tie([h[0] for h in halves], before_last)
-            halves = [(v, h[1]) for v, h in zip(values, halves)]
-        halves = [merge(*half, order[step]) for half, order in zip(halves, orders)]
+        done = merge(*halves[0], orders[0][step])
+        if step == 0:
+            (value, first), before_last = tie([halves[1][0], done[0]], before_last)
+            halves[1], done = (value, halves[1][1]), (first, done[1])
+        halves = [done, merge(*halves[1], orders[1][step])]
     shape = (-1, piece.shape[-2])
     return [h[0].reshape(shape + h[0].shape[-1:]) for h in halves], before_last
+
+
+def flips(group):
+    chosen = [()]
+    for stage in reversed(group):
+        chosen += [c + (stage,) for c in chosen]
+    return chosen[1:]
+
+
+def swap_with(value, flip):
+    flat = value.reshape(-1, value.shape[-1])
+    across = sum(1 << bit for axis, bit in flip if axis == "tp")
+    along = sum(1 << bit for axis, bit in flip if axis == "dp")
+    if not across:
+        axes, pairs = "dp", [(i, i ^ along) for i in range(lax.axis_size("dp"))]
+    elif not along:
+        axes, pairs = "tp", [(i, i ^ across) for i in range(lax.axis_size("tp"))]
+    else:
+        count = lax.axis_size("tp")
+        axes = ("dp", "tp")
+        pairs = [
+            (i * count + j, (i ^ along) * count + (j ^ across))
+            for i in range(lax.axis_size("dp"))
+            for j in range(count)
+        ]
+    return lax.ppermute(flat, axes, pairs).reshape(value.shape)
 
 
 class Term:
@@ -76,17 +107,16 @@
         self.array, self.stages, self.first = array, list(stages), first
         self.count = array.shape[-1] if count is None else count
 
-    def part(self, done, stage, index):
+    def part(self, fixed, flip):
         starts, sizes, kept = [], [], []
-        for dim, own in enumerate(self.stages):
-            if own == stage:
-                starts.append(index)
-            elif own in done:
-                starts.append(own_bit(*own))
+        for stage in self.stages:
+            if stage in fixed:
+                starts.append(1 - own_bit(*stage) if stage in flip else own_bit(*stage))
+                sizes.append(1)
             else:
                 starts.append(0)
+                sizes.append(2)
                 kept.append(2)
-            sizes.append(1 if own == stage or own in done else 2)
         rest = self.array.shape[len(self.stages) : -1]
         starts += [0] * len(rest) + [self.first]
         sizes += list(rest) + [self.count]
@@ -99,49 +129,62 @@
         self.terms, self.done = terms, []
         self.stages = list(terms[0].stages)
 
-    def split(self, stage):
-        self.stages.remove(stage)
-        send = sum(t.part(self.done, stage, 1 - own_bit(*stage)).astype(F32) for t in self.terms)
-        self.done = self.done + [stage]
-        return send.astype(BF)
+    def sends(self, group):
+        self.done = self.done + list(group)
+        self.stages = [s for s in self.stages if s not in group]
+        return [
+            sum(t.part(self.done, flip).astype(F32) for t in self.terms).astype(BF)
+            for flip in flips(group)
+        ]
 
     def add(self, array, first=0, count=None):
         self.terms.append(Term(array, self.stages, first, count))
 
     def total(self):
-        return sum(t.part(self.done, None, 0).astype(F32) for t in self.terms)
-
-
-def start_near(scatters, orders, step, later=()):
-    sends = [s.split(order[step]) for s, order in zip(scatters, orders)]
+        return sum(t.part(self.done, ()).astype(F32) for t in self.terms)
+
+
+def start_sends(scatters, groups, later=()):
+    sends = [s.sends(group) for s, group in zip(scatters, groups)]
+    count = len(sends[0])
+    if later:
+        flat, later = tie([x for part in sends for x in part], later)
+        sends = [flat[i * count : (i + 1) * count] for i in range(len(scatters))]
+    others = [
+        [swap_with(x, flip) for x, flip in zip(part, flips(group))]
+        for part, group in zip(sends, groups)
+    ]
+    return others, later
+
+
+def end_sends(scatters, others, later=()):
+    count = len(others[0])
+    flat = [x for part in others for x in part]
+    if later:
+        flat, later = tie(flat, later)
+    for index, scatter in enumerate(scatters):
+        for other in flat[index * count : (index + 1) * count]:
+            scatter.add(other)
+    return later
+
+
+def start_joint(scatters, group, later=()):
+    sends = [jnp.concatenate(parts, axis=-1) for parts in zip(*[s.sends(group) for s in scatters])]
     if later:
         sends, later = tie(sends, later)
-    return [swap(send, *order[step]) for send, order in zip(sends, orders)], later
-
-
-def end_near(scatters, others, later=()):
+    return [swap_with(x, flip) for x, flip in zip(sends, flips(group))], later
+
+
+def end_joint(scatters, others, later=()):
     if later:
         others, later = tie(others, later)
-    for scatter, other in zip(scatters, others):
-        scatter.add(other)
+    for other in others:
+        at = 0
+        for scatter in scatters:
+            count = scatter.terms[0].count
+            scatter.add(other, at, count)
+            at += count
     return later
-
-
-def far_stage(scatters, stage, later=()):
-    send = jnp.concatenate([s.split(stage) for s in scatters], axis=-1)
-    if later:
-        (send,), later = tie([send], later)
-    other = swap(send, *stage)
-    wide = other.shape[-1] // len(scatters)
-    for index, scatter in enumerate(scatters):
-        scatter.add(other, index * wide, wide)
-    return later
-
-
-def sum_everywhere(value):
-    for axis, bit in [("tp", 0)] + dp_stages():
-        value = value + swap(value, axis, bit)
-    return value
 
 
 def inverse_rms(values):
@@ -377,7 +420,7 @@
     third = [block_sum[step * BLOCK : (step + 1) * BLOCK] for step in range(3)]
     cur = jnp.concatenate([third[2], third[1], third[0], jnp.zeros((BLOCK, BLOCK), F32)], axis=1)
     count = BLOCK // 2
-    while count >= 8:
+    while count >= 1:
         cur = cur[count:] + pltpu.roll(cur[:count], count, 1)
         count //= 2
     return cur
@@ -391,8 +434,7 @@
     qkv_ref,
     grad_ref,
     halo_ref,
-    wo0_ref,
-    wo1_ref,
+    wo_ref,
     segr_ref,
     segl_ref,
     bias_ref,
@@ -412,13 +454,10 @@
     @pl.when(block == 0)
     def _():
         acc_ref[...] = jnp.zeros_like(acc_ref)
-        wide = wo0_ref.shape[1]
         own = pl.ds(pl.multiple_of(shift * BLOCK, BLOCK), own_blocks * BLOCK)
+        heads_s[own, :] = grad_ref[0]
         other = place_of((1 - shift) * own_blocks)
-        for half, ref in enumerate((wo0_ref, wo1_ref)):
-            columns = slice(half * wide, (half + 1) * wide)
-            heads_s[own, columns] = dot_nn(grad_ref[0], ref[...]).astype(BF)
-            heads_s[other, columns] = dot_nn(halo_ref[0], ref[...]).astype(BF)
+        heads_s[other, :] = dot_nn(halo_ref[0], wo_ref[...]).astype(BF)
 
     @pl.when(jnp.logical_and(block == 0, row == 0))
     def _():
@@ -463,43 +502,42 @@
 
 
 def attend_backward(
-    shift, qkv, grad_attn, grad_halo, weights, out_cols, seg_rows, seg_lanes, bias
+    shift, qkv, grad_heads, grad_halo, out_weight, seg_rows, seg_lanes, bias
 ):
     rows, length, width = qkv.shape
-    half, model = grad_attn.shape[1:]
+    half, cols = grad_heads.shape[1:]
+    model = grad_halo.shape[2]
     own_blocks = half // BLOCK
     pairs = bias.shape[0]
     last = length // BLOCK - 1
     steps = rows * (last + 1) * pairs
-    out_at = weights.shape[1] // out_cols - 1
     once = pl.Buffered(1)
     cost = pl.CostEstimate(
-        flops=steps * 20 * BLOCK * 3 * BLOCK * LANES + 4 * rows * length * model * out_cols,
+        flops=steps * 120 * BLOCK * 3 * BLOCK * LANES + 2 * rows * BLOCK * model * cols,
         transcendentals=steps * 6 * BLOCK * BLOCK,
-        bytes_accessed=qkv.size * 4 + grad_attn.size * 2 + bias.size * 4 + model * out_cols * 4,
+        bytes_accessed=qkv.size * 4 + grad_heads.size * 2 + bias.size * 4 + model * cols * 2,
     )
     return pl.pallas_call(
         functools.partial(attend_back_kernel, pairs, last, own_blocks),
         out_shape=(
             jax.ShapeDtypeStruct((rows, half, width), BF),
-            jax.ShapeDtypeStruct((2 * pairs, 8, 4 * BLOCK), F32),
+            jax.ShapeDtypeStruct((2 * pairs, 1, 4 * BLOCK), F32),
         ),
         grid_spec=pltpu.PrefetchScalarGridSpec(
             num_scalar_prefetch=1,
             grid=(rows, last + 1),
             in_specs=[
                 pl.BlockSpec((1, length, width), lambda r, i, s: (r, 0, 0)),
-                pl.BlockSpec((1, half, model), lambda r, i, s: (r, 0, 0)),
+                pl.BlockSpec((1, half, cols), lambda r, i, s: (r, 0, 0)),
                 pl.BlockSpec((1, BLOCK, model), lambda r, i, s: (r, 0, 0)),
-                pl.BlockSpec((model, out_cols), lambda r, i, s: (0, out_at), pipeline_mode=once),
-                pl.BlockSpec((model, out_cols), lambda r, i, s: (1, out_at), pipeline_mode=once),
+                pl.BlockSpec((model, cols), lambda r, i, s: (0, 0), pipeline_mode=once),
                 pl.BlockSpec((1,) + seg_rows.shape[1:], lambda r, i, s: (r, 0, 0)),
                 pl.BlockSpec((1,) + seg_lanes.shape[1:], lambda r, i, s: (r, 0, 0)),
                 pl.BlockSpec(bias.shape, lambda r, i, s: (0, 0, 0), pipeline_mode=once),
             ],
             out_specs=[
                 pl.BlockSpec((1, half, width), lambda r, i, s: (r, 0, 0)),
-                pl.BlockSpec((2 * pairs, 8, 4 * BLOCK), lambda r, i, s: (0, 0, 0)),
+                pl.BlockSpec((2 * pairs, 1, 4 * BLOCK), lambda r, i, s: (0, 0, 0)),
             ],
             scratch_shapes=[
                 pltpu.VMEM((length, pairs * LANES), BF),
@@ -512,22 +550,16 @@
         ),
         cost_estimate=cost,
         name="attend_backward",
-    )(shift, qkv, grad_attn, grad_halo, weights, weights, seg_rows, seg_lanes, bias)
-
-
-def input_kernel(grad_ref, wa_ref, wb_ref, x_ref, gain_ref, gmid_ref, out_ref, ggain_ref):
+    )(shift, qkv, grad_heads, grad_halo, out_weight, seg_rows, seg_lanes, bias)
+
+
+def input_kernel(grad_ref, wa_ref, wb_ref, x_ref, gain_ref, gmid_ref, out_ref):
     grad_n1 = None
     for ref, start, at, used in column_pieces(wa_ref, wb_ref):
         part = dot_nt(grad_ref[:, at : at + used], ref[:, start : start + used])
         grad_n1 = part if grad_n1 is None else grad_n1 + part
     x = x_ref[...].astype(F32)
     r1 = inverse_rms(x)
-
-    @pl.when(pl.program_id(0) == 0)
-    def _():
-        ggain_ref[...] = jnp.zeros_like(ggain_ref)
-
-    ggain_ref[...] += jnp.sum(grad_n1 * x * r1, axis=0, keepdims=True)
     scaled = grad_n1 * gain_ref[...]
     inner = jnp.mean(scaled * x, axis=-1, keepdims=True)
     out_ref[...] = gmid_ref[...] + r1 * scaled - x * (r1 * r1 * r1 * inner)
@@ -542,10 +574,7 @@
     whole = lambda i: (0, 0)
     return pl.pallas_call(
         input_kernel,
-        out_shape=(
-            jax.ShapeDtypeStruct((tokens, model), F32),
-            jax.ShapeDtypeStruct((1, model), F32),
-        ),
+        out_shape=jax.ShapeDtypeStruct((tokens, model), F32),
         grid=(tokens // chunk,),
         in_specs=[
             pl.BlockSpec((chunk, width), here),
@@ -555,14 +584,12 @@
             pl.BlockSpec((1, model), whole, pipeline_mode=once),
             pl.BlockSpec((chunk, model), here),
         ],
-        out_specs=[pl.BlockSpec((chunk, model), here), pl.BlockSpec((1, model), whole)],
+        out_specs=pl.BlockSpec((chunk, model), here),
         compiler_params=pltpu.CompilerParams(
             dimension_semantics=("arbitrary",), vmem_limit_bytes=40 << 20
         ),
         cost_estimate=pl.CostEstimate(
-            flops=2 * tokens * width * model,
-            transcendentals=tokens,
-            bytes_accessed=tokens * (2 * width + 10 * model) + 2 * width * model,
+            flops=tokens * model, transcendentals=tokens, bytes_accessed=tokens
         ),
         name="input_gradient",
     )(grad_qkv, part_a, part_b, x_own, gain, grad_middle)
@@ -627,6 +654,7 @@
     ggain_ref,
     keep_ref,
     send_ref,
+    wo_ref,
     mid_s,
     n2_s,
     n2t_s,
@@ -650,6 +678,9 @@
 
     @pl.when(step == 0)
     def _():
+        wo_ref[:, :half] = wo0_ref[...]
+        wo_ref[:, half:] = wo1_ref[...]
+
         def work(place):
             middle = x_ref[place, :].astype(F32)
             middle = middle + dot_nt(heads_ref[place, :half], wo0_ref[...])
@@ -724,6 +755,7 @@
             jax.ShapeDtypeStruct((1, width), F32),
             piece,
             piece,
+            jax.ShapeDtypeStruct((width, 2 * out_cols), BF),
         ),
         grid_spec=pltpu.PrefetchScalarGridSpec(
             num_scalar_prefetch=1,
@@ -746,6 +778,7 @@
                 pl.BlockSpec((1, width), whole, pipeline_mode=once),
                 piece_spec,
                 piece_spec,
+                pl.BlockSpec((width, 2 * out_cols), whole, pipeline_mode=once),
             ],
             scratch_shapes=[
                 pltpu.VMEM((tokens, width), F32),
@@ -770,28 +803,97 @@
     )(core, heads_out, x_own, gain, cotangent, weights, weights, weights, weights, weights)
 
 
-def weight_kernel(shard, core_ref, n1_ref, gqkv_ref, gattn_ref, heads_ref, keep_ref, send_ref):
+def split_rows_at(own_core, half, shard, grad, keep_ref, send_ref, columns):
+    for core in range(2):
+        first, second = (keep_ref, send_ref) if core == 0 else (send_ref, keep_ref)
+
+        @pl.when(own_core == core)
+        def _():
+            for group in range(grad.shape[0] // (2 * shard)):
+                start = group * 2 * shard
+                first[half, group, :, columns] = grad[start : start + shard]
+                second[half, group, :, columns] = grad[start + shard : start + 2 * shard]
+
+
+def weight_kernel(
+    shard,
+    core_ref,
+    n1_ref,
+    gqkv_ref,
+    gout_ref,
+    wa_ref,
+    wb_ref,
+    gain_ref,
+    ggain_ref,
+    diag_ref,
+    onehot_ref,
+    keep_ref,
+    send_ref,
+    gain_s,
+):
+    model = n1_ref.shape[1]
     wide = gqkv_ref.shape[1] // 3
+    half = pl.program_id(0)
+
+    @pl.when(half == 0)
+    def _():
+        gain_s[...] = jnp.zeros_like(gain_s)
+
+    wide_a, wide_b = wa_ref.shape[1] // 2, wb_ref.shape[1] // 2
     for index in range(4):
         columns = slice(index * wide, (index + 1) * wide)
         if index < 3:
             grad = dot_tn(n1_ref[...], gqkv_ref[:, columns])
+            for at in range(index * wide, (index + 1) * wide, LANES):
+                if at < wide_a:
+                    weight = wa_ref[:, lanes_of(half * wide_a + at)]
+                else:
+                    weight = wb_ref[:, lanes_of(half * wide_b + at - wide_a)]
+                here = at - index * wide
+                gain_s[...] += weight.astype(F32) * grad[:, here : here + LANES]
         else:
-            grad = dot_tn(gattn_ref[...], heads_ref[...])
-        split_rows(
-            core_ref[0], shard, grad.astype(BF), keep_ref, send_ref, (slice(None), columns)
+            grad = gout_ref[...]
+        split_rows_at(core_ref[0], half, shard, grad.astype(BF), keep_ref, send_ref, columns)
+
+    @pl.when(half == 1)
+    def _():
+        ggain1 = jnp.sum(gain_s[...].T, axis=0, keepdims=True) / gain_ref[...]
+        table = lax.dot_general(
+            diag_ref[...],
+            onehot_ref[...],
+            (((1,), (1,)), ((), ())),
+            precision=HIGHEST_PREC,
+            preferred_element_type=F32,
         )
-
-
-def weight_gradients(core, n1, grad_qkv, grad_attn, heads_out, shard):
+        rows = []
+        for value in (ggain1, ggain_ref[...]):
+            rows += [value[:, at : at + LANES] for at in range(0, model, LANES)]
+        table = jnp.concatenate(
+            [table, jnp.zeros((table.shape[0], LANES - table.shape[1]), F32)], axis=1
+        )
+        small = jnp.concatenate(rows + [table], axis=0).astype(BF)
+        for ref in (keep_ref, send_ref):
+            ref[:, :, :, 4 * wide :] = jnp.zeros(ref.shape[:3] + (ref.shape[3] - 4 * wide,), BF)
+            for at in range(0, small.shape[0], shard):
+                lines = small[at : at + shard]
+                place = slice(4 * wide + at // shard * LANES, 4 * wide + (at // shard + 1) * LANES)
+                for side in range(2):
+                    for group in range(ref.shape[1]):
+                        ref[side, group, : lines.shape[0], place] = lines
+
+
+def weight_gradients(
+    core, n1, grad_qkv, grad_out_w, part_a, part_b, gain, grad_gain2, diagonals, onehot, shard
+):
     tokens, model = n1.shape
-    wide = heads_out.shape[1] // 2
+    wide = grad_out_w.shape[1] // 2
     groups = model // (2 * shard)
     whole = lambda t, c: (0, 0)
     half = lambda t, c: (0, t)
     once = pl.Buffered(1)
-    piece = jax.ShapeDtypeStruct((2, groups, shard, 4 * wide), BF)
-    piece_spec = pl.BlockSpec((1, groups, shard, 4 * wide), lambda t, c: (t, 0, 0, 0))
+    lines = 2 * model // LANES + diagonals.shape[0]
+    piece = jax.ShapeDtypeStruct((2, groups, shard, 4 * wide + pl.cdiv(lines, shard) * LANES), BF)
+    piece_spec = pl.BlockSpec(piece.shape, lambda t, c: (0, 0, 0, 0), pipeline_mode=once)
     return pl.pallas_call(
         functools.partial(weight_kernel, shard),
         out_shape=(piece, piece),
@@ -801,21 +903,38 @@
             in_specs=[
                 pl.BlockSpec((tokens, model), whole, pipeline_mode=once),
                 pl.BlockSpec((tokens, 3 * wide), half),
-                pl.BlockSpec((tokens, model), whole, pipeline_mode=once),
-                pl.BlockSpec((tokens, wide), half),
+                pl.BlockSpec((model, wide), half),
+                pl.BlockSpec(part_a.shape, whole, pipeline_mode=once),
+                pl.BlockSpec(part_b.shape, whole, pipeline_mode=once),
+                pl.BlockSpec(gain.shape, whole, pipeline_mode=once),
+                pl.BlockSpec(grad_gain2.shape, whole, pipeline_mode=once),
+                pl.BlockSpec(diagonals.shape, whole, pipeline_mode=once),
+                pl.BlockSpec(onehot.shape, whole, pipeline_mode=once),
             ],
             out_specs=[piece_spec, piece_spec],
+            scratch_shapes=[pltpu.VMEM((model, LANES), F32)],
         ),
         compiler_params=pltpu.CompilerParams(
             dimension_semantics=("arbitrary",), vmem_limit_bytes=40 << 20
         ),
         cost_estimate=pl.CostEstimate(
-            flops=16 * tokens * model * wide,
+            flops=tokens * model,
             transcendentals=0,
-            bytes_accessed=tokens * (4 * model + 16 * wide) + 16 * model * wide,
+            bytes_accessed=tokens,
         ),
         name="weight_gradients",
-    )(core, n1, grad_qkv, grad_attn, heads_out)
+    )(
+        core,
+        n1,
+        grad_qkv,
+        grad_out_w,
+        part_a,
+        part_b,
+        gain,
+        grad_gain2,
+        diagonals,
+        onehot,
+    )
 
 
 def body(
@@ -908,7 +1027,7 @@
     heads_flat = heads_out.reshape(rows * half, 2 * head_cols)
 
     cot_flat = cotangent.reshape(rows * half, width)
-    block_out, grad_middle, grad_attn, grad_gain2, keep, send = feed_forward(
+    block_out, grad_middle, grad_attn, grad_gain2, keep, send, out_weight = feed_forward(
         core,
         heads_flat,
         x_own.reshape(rows * half, width),
@@ -920,69 +1039,86 @@
     )
     grad_attn_rows = grad_attn.reshape(rows, half, width)
     grad_halo = halo_of(grad_attn_rows)
+    grad_out_w = dot_tn(grad_attn, heads_flat).astype(BF)
+    grad_heads = dot_nn(grad_attn, out_weight).astype(BF).reshape(heads_out.shape)
 
     far, near, cores = stage_groups()
+    far_groups = [far[max(i - 2, 0) : i] for i in range(len(far), 0, -2)]
     stages = [("tp", 0)] + dp_stages()[:-1]
-
-    def both_cores(keep, send, split):
+    twice = len(near[0]) > 1
+
+    def both_cores(keep, send, cuts):
         terms = [
-            value.reshape((2,) * len(stages) + value.shape[2:]) for value in (keep, swap(send, *cores))
+            value.reshape((2,) * len(stages) + value.shape[2:])
+            for value in (keep, swap_with(send, (cores,)))
         ]
-        total = keep.shape[-1]
-        ranges = ((0, split), (split, total - split))
-        return [Scatter([Term(t, stages, *cut) for t in terms]) for cut in ranges]
-
-    feed = both_cores(keep, send, hidden_cols // 2)
-    others, (grad_attn_rows, grad_halo) = start_near(feed, near, 0, (grad_attn_rows, grad_halo))
+        ends = cuts[1:] + [keep.shape[-1]]
+        return [Scatter([Term(t, stages, c, e - c) for t in terms]) for c, e in zip(cuts, ends)]
+
+    feed = both_cores(keep, send, [0])
+    others, (grad_heads, grad_halo, grad_out_w) = start_sends(
+        feed, [near[0]], (grad_heads, grad_halo, grad_out_w)
+    )
 
     grad_qkv, diagonals = attend_backward(
-        shift, qkv, grad_attn_rows, grad_halo, second, head_cols, seg_rows, seg_lanes, bias
-    )
-    (grad_qkv,) = end_near(feed, others, (grad_qkv,))
-    if len(near[0]) > 1:
-        others, (grad_qkv,) = start_near(feed, near, 1, (grad_qkv,))
+        shift, qkv, grad_heads, grad_halo, out_weight, seg_rows, seg_lanes, bias
+    )
     grad_qkv = grad_qkv.reshape(rows * half, grad_qkv.shape[-1])
     keep_w, send_w = weight_gradients(
-        core, n1.reshape(rows * half, width), grad_qkv, grad_attn, heads_flat, shard
-    )
-    tail = both_cores(keep_w, send_w, 2 * head_cols)
-    if len(near[0]) > 1:
-        end_near(feed, others)
-    for stage in far[1:][::-1]:
-        far_stage(feed, stage)
-    others, (grad_qkv,) = start_near(tail, near, 0, (grad_qkv,))
-    grad_in, grad_gain1 = input_gradient(
+        core,
+        n1.reshape(rows * half, width),
+        grad_qkv,
+        grad_out_w,
+        part_a,
+        part_b,
+        gain1,
+        grad_gain2,
+        diagonals[:, 0],
+        onehot,
+        shard,
+    )
+    keep_w, send_w = end_sends(feed, others, (keep_w, send_w))
+    tail = both_cores(keep_w, send_w, [0, 2 * head_cols])
+    late = list(far)
+    waiting = []
+    if late:
+        waiting, (tail[0].terms[0].array,) = start_joint(
+            feed, [late.pop()], (tail[0].terms[0].array,)
+        )
+    others, (grad_qkv,) = start_sends(tail, [order[:1] for order in near], (grad_qkv,))
+    grad_in = input_gradient(
         grad_qkv, part_a, part_b, x_own.reshape(rows * half, width), gain1, grad_middle
     )
-    end_near(tail, others)
-    if len(near[0]) > 1:
-        others, _ = start_near(tail, near, 1)
-        end_near(tail, others)
-    for stage in far[:1]:
-        far_stage(feed, stage)
-    for stage in far[::-1]:
-        far_stage(tail, stage)
+    if waiting:
+        waiting, (grad_in,) = tie(waiting, (grad_in,))
+        end_joint(feed, waiting)
+    while late:
+        waiting, (grad_in,) = start_joint(feed, [late.pop()], (grad_in,))
+        if late:
+            end_joint(feed, waiting)
+    (grad_in,) = end_sends(tail, others, (grad_in,))
+    if twice:
+        others, _ = start_sends(tail, [order[1:] for order in near])
+        end_sends(tail, others)
+    for index, group in enumerate(far_groups):
+        others, _ = start_joint(tail, group)
+        if index == 0 and len(far) > 1:
+            waiting, others = tie(waiting, others)
+            end_joint(feed, waiting)
+        end_joint(tail, others)
     feed_sums = jnp.concatenate([s.total() for s in feed], axis=-1)
     sums_a, sums_b = [s.total() for s in tail]
 
-    diagonals_turned = [jnp.roll(diagonals[:, s], 7 - s, axis=1) for s in range(8)]
-    offset_sums = diagonals_turned[0]
-    for step in range(1, 8):
-        offset_sums = offset_sums + diagonals_turned[step]
-    table_sum = lax.dot_general(
-        onehot,
-        offset_sums,
-        (((1,), (1,)), ((), ())),
-        precision=HIGHEST_PREC,
-        preferred_element_type=F32,
-    )
-    small = jnp.concatenate([grad_gain1[0], grad_gain2[0], table_sum.reshape(-1)])
-    small = sum_everywhere(small.reshape(-1, LANES)).reshape(-1)
+    small = sums_b[:, 2 * head_cols :]
+    small = jnp.concatenate(
+        [small[:, at : at + LANES] for at in range(0, small.shape[1], LANES)], axis=0
+    )
+    lines = width // LANES
     dp_start = lax.axis_index("dp") * shard
-    sum_gain1 = lax.dynamic_slice_in_dim(small[:width], dp_start, shard)
-    sum_gain2 = lax.dynamic_slice_in_dim(small[width : 2 * width], dp_start, shard)
-    sum_table = small[2 * width :].reshape(buckets, 2 * local_heads)
-    sum_table = lax.dynamic_slice_in_dim(sum_table, tp_index * local_heads, local_heads, 1)
+    sum_gain1 = lax.dynamic_slice_in_dim(small[:lines].reshape(-1), dp_start, shard)
+    sum_gain2 = lax.dynamic_slice_in_dim(small[lines : 2 * lines].reshape(-1), dp_start, shard)
+    sum_table = small[2 * lines : 2 * lines + 2 * local_heads, :buckets]
+    sum_table = lax.dynamic_slice_in_dim(sum_table, tp_index * local_heads, local_heads, 0).T
 
     shape = (micro, local_rows, half, width)
     return (
@@ -992,7 +1128,7 @@
         sums_a[:, :head_cols],
         sums_a[:, head_cols:],
         sums_b[:, :head_cols],
-        sums_b[:, head_cols:].T,
+        sums_b[:, head_cols : 2 * head_cols].T,
         sum_table,
         sum_gain2,
         feed_sums[0],

time: 311 us -> 299 us (0.961)
  waiting for transfers between devices: 80.1 us -> 66.1 us
  matrix products: 1.05 us -> 5.55 us
    ppermute x30 -> x11, waiting for transfers between devices: 70.6 us -> 36.6 us  [swap(): return lax.ppermute(value, axis, [(i, i ^ 1 << bit) for i in range(count)])]
    ppermute x0 -> x14, waiting for transfers between devices: none -> 20.4 us  [swap_with(): return lax.ppermute(flat, axes, pairs).reshape(value.shape)]
    ppermute x0 -> x14, starting transfers between devices: none -> 15.7 us  [swap_with(): return lax.ppermute(flat, axes, pairs).reshape(value.shape)]
    ppermute x30 -> x11, starting transfers between devices: 30.6 us -> 15 us  [swap(): return lax.ppermute(value, axis, [(i, i ^ 1 << bit) for i in range(count)])]
    dot_general x1 -> x2, matrix products: 0.9 us -> 5.4 us  [the longest x1 2.88 us: dot_tn(): lax.dot_general(left, right, (((0,), (0,)), ((), ())), preferred_element_...]
    add x7 -> x5, other arithmetic: 2.88 us -> 6.16 us  [the longest x3 3.86 us: total(): return sum((t.part(self.done, ()).astype(F32) for t in self.terms))]
    convert_element_type x10, other arithmetic: 20.1 us -> 16.8 us  [the longest x9 16.8 us: sends(): sum((t.part(self.done, flip).astype(F32) for t in self.terms)).astype(BF)]
    unnamed x51 -> x57, local copies, waits for them, and re-layouts: 9.33 us -> 10.9 us
  transfers between devices with their start and end apart: 31 -> 26, of which waited for: 17 -> 12; matrix products, arithmetic and copies ran while one was open for 11% -> 12% of each run, Pallas kernels for 24% -> 28%
where the time goes in v1:
time: 299 us; the launch traced here: 298 us
  Pallas kernels  132 us (44%)
  waiting for transfers between devices  66.1 us (22%)
  starting transfers between devices  30.8 us (10%)
  other arithmetic  29.3 us (10%)
  local copies, waits for them, and re-layouts  19.8 us (7%)
  between operations  14.5 us (5%)
  matrix products  5.55 us (2%)
    pallas_call x1, Pallas kernels, feed_forward(): pl.pallas_call(functools.partial(feed_kernel, min(FEED_CHUNK, tokens), sh...  47.5 us
    pallas_call x1, Pallas kernels, attend_backward(): pl.pallas_call(functools.partial(attend_back_kernel, pairs, last, own_blo...  39.9 us
    ppermute x11, waiting for transfers between devices, swap(): return lax.ppermute(value, axis, [(i, i ^ 1 << bit) for i in range(count)])  36.6 us
    pallas_call x1, Pallas kernels, attend_forward(): pl.pallas_call(functools.partial(attend_kernel, pairs, last), out_shape=(...  24 us
    ppermute x14, waiting for transfers between devices, swap_with(): return lax.ppermute(flat, axes, pairs).reshape(value.shape)  20.4 us
    convert_element_type x9, other arithmetic, sends(): sum((t.part(self.done, flip).astype(F32) for t in self.terms)).astype(BF)  16.8 us
    ppermute x14, starting transfers between devices, swap_with(): return lax.ppermute(flat, axes, pairs).reshape(value.shape)  15.7 us
    ppermute x11, starting transfers between devices, swap(): return lax.ppermute(value, axis, [(i, i ^ 1 << bit) for i in range(count)])  15 us
  transfers between devices with their start and end apart: 26, of which 12 were waited for; matrix products, arithmetic and copies ran while one was open for 12% of the time, Pallas kernels for 28%

profile of v1, /device:TPU:0, one launch (start us, length us, event | category | flops | bytes accessed | tf_op | source)
XLA Modules:
  0.0 298.2 jit_solution(4228767677844242534)
XLA Ops:
  7.3 1.8 pad_maximum_fusion.4
  10.8 4.1 %collective-permute-start = (bf16[48,1280]{1,0:T(8,128)(2,1)S(1)}, bf16[48,1280]{1,0:T(8,128)(2,1)S(1)}, u32[]{:S(2)}, u32[]{:S(2)}) collective-permute-start(bf16[48,1280]{1,0:T(8,128)(2,1)S(1)} %fusion.24), channel_id=1, source_target_pairs={{0,16},{2,18},{4,20},{6,22},{8,24},{10,26},{12,28},{14,30},{16,0},... | collective-permute-start | bytes 368648 | tf_op jit(solution)/shard_map/ppermute | solution.py:26
  14.9 6.0 %collective-permute-done = bf16[48,1280]{1,0:T(8,128)(2,1)S(1)} collective-permute-done((bf16[48,1280]{1,0:T(8,128)(2,1)S(1)}, bf16[48,1280]{1,0:T(8,128)(2,1)S(1)}, u32[]{:S(2)}, u32[]{:S(2)}) %collective-permute-start) | collective-permute-done | bytes 122912 | tf_op jit(solution)/shard_map/ppermute | solution.py:26
  24.0 9.1 %collective-permute-done.1 = bf16[2,48,1280]{2,1,0:T(8,128)(2,1)S(1)} collective-permute-done((bf16[2,48,1280]{2,1,0:T(8,128)(2,1)S(1)}, bf16[2,48,1280]{2,1,0:T(8,128)(2,1)S(1)}, u32[]{:S(2)}, u32[]{:S(2)}) %collective-permute-start.1) | collective-permute-done | bytes 245792 | tf_op jit(solution)/shard_map/ppermute | solution.py:26
  34.7 1.6 collective-permute-start.4
  38.0 4.3 %window_bias.1.bias_ref = f32[6,384,256]{2,1,0:T(8,128)} custom-call(f32[12,1,512]{2,1,0:T(1,128)} %broadcast_in_dim.19.turned_ref), custom_call_target="tpu_custom_call" | custom-call | tf_op jit(solution)/shard_map/window_bias/pallas_call | solution.py:607
  43.8 1.8 collective-permute-start.5
  45.5 10.3 %collective-permute-done.5 = bf16[2,2,48,640]{3,2,0,1:T(8,128)(2,1)S(1)} collective-permute-done((bf16[2,2,48,640]{3,2,0,1:T(8,128)(2,1)S(1)}, bf16[2,2,48,640]{3,2,0,1:T(8,128)(2,1)S(1)}, u32[]{:S(2)}, u32[]{:S(2)}) %collective-permute-start.5) | collective-permute-done | bytes 245792 | tf_op jit(solution)/shard_map/ppermute | solution.py:26
  57.6 8.8 %collective-permute-done.6 = bf16[2,2,48,1280]{3,2,0,1:T(8,128)(2,1)S(1)} collective-permute-done((bf16[2,2,48,1280]{3,2,0,1:T(8,128)(2,1)S(1)}, bf16[2,2,48,1280]{3,2,0,1:T(8,128)(2,1)S(1)}, u32[]{:S(2)}, u32[]{:S(2)}) %collective-permute-start.6) | collective-permute-done | bytes 491552 | tf_op jit(solution)/shard_map/ppermute | solution.py:26
  73.5 24.0 %attend_forward.1 = (bf16[2,512,768]{2,1,0:T(8,128)(2,1)}, bf16[2,640,2304]{2,1,0:T(8,128)(2,1)}, bf16[2,512,768]{2,1,0:T(8,128)(2,1)}, bf16[768,1280]{1,0:T(8,128)(2,1)}, bf16[768,1280]{1,0:T(8,128)(2,1)}) custom-call(s32[2]{0:T(128)S(1)} %pad_add_fusion.shift_ref, bf16[2,512,768]{2,1,0:T(8,128)(2,1)} %bitcast.218, ...), custom_call_target="tpu_custom_call" | custom-call | flops 6945767424 | bytes 15728640 | tf_op jit(solution)/shard_map/attend_forward/pallas_call | solution.py:366
  97.5 9.1 %all-gather.2.cloned.1.call-done.wo0_ref.wo1_ref.wg_ref.wu_ref.wd_ref = bf16[1536,3456]{1,0:T(8,128)(2,1)} async-done(((bf16[48,3456]{1,0:T(8,128)(2,1)}), bf16[1536,3456]{1,0:T(8,128)(2,1)}) %all-gather.2.cloned.1.call-update) | async-done | bytes 10616848 | tf_op jit(solution)/shard_map/all_gather | solution.py:978
  106.6 47.5 %feed_forward.1 = (f32[1024,768]{1,0:T(8,128)}, f32[1024,768]{1,0:T(8,128)}, bf16[1024,768]{1,0:T(8,128)(2,1)}, f32[1,768]{1,0:T(1,128)}, bf16[2,8,3,48,1024]{4,...) custom-call(s32[1]{0:T(128)} %bitcast.core_ref, bf16[1024,768]{1,0:T(8,128)(2,1)} %bitcast.261, ...), custom_call_target="tpu_custom_call" | custom-call | flops 30198988800 | bytes 32636928 | tf_op jit(solution)/shard_map/feed_forward/pallas_call | solution.py:749
  157.2 2.9 convolution_convert_fusion.1.gout_ref
  160.1 2.5 convolution_convert_fusion
  162.6 4.7 %fusion.2 = (bf16[2,2,3,48,1024]{4,3,2,1,0:T(8,128)(2,1)S(1)}, bf16[2,2,3,48,1024]{4,3,2,1,0:T(8,128)(2,1)}, bf16[2,2,3,48,1024]{4,3,2,1,0:T(8,128)(2,1)}) fusion(bf16[2,2,2,2,3,48,1024]{6,5,4,3,2,1,0:T(8,128)(2,1)} %bitcast.27, s32[]{:T(128)S(6)} %select_n.153, s32[]{:T(128)S(6)} %select_n.154, bf16[2,2,2,2,3,48,1024]{6,5,4,3,2,1,0:T(8,128)(2,1)S(1)} %bitcast.242, ...), kind=kLoop, calls=%fused_computation.8 | loop fusion | flops 7077888 | bytes 10616848 | tf_op jit(solution)/shard_map/convert_element_type | solution.py:136
  170.8 39.9 %attend_backward.1 = (bf16[2,512,2304]{2,1,0:T(8,128)(2,1)}, f32[12,1,512]{2,1,0:T(1,128)}) custom-call(s32[1]{0:T(128)} %bitcast.1.shift_ref, bf16[2,640,2304]{2,1,0:T(8,128)(2,1)} %get-tuple-element.73.qkv_ref, bf16[2,512,768]{2,1,0:T(8,128)(2,1)} %bitcast.263, bf16[2,128,768]{2,1,0:T(8,128)(2,1)} %copy-done.22, ...), custom_call_target="tpu_custom_call" | custom-call | flops 45600473088 | bytes 16908288 | tf_op jit(solution)/shard_map/attend_backward/pallas_call | solution.py:520
  211.4 10.1 %weight_gradients.1 = (bf16[2,8,48,1664]{3,2,1,0:T(8,128)(2,1)S(1)}, bf16[2,8,48,1664]{3,2,1,0:T(8,128)(2,1)}) custom-call(s32[1]{0:T(128)} %bitcast.core_ref, bf16[1024,768]{1,0:T(8,128)(2,1)S(1)} %bitcast.230, bf16[1024,2304]{1,0:T(8,128)(2,1)} %bitcast.216, bf16[768,768]{1,0:T(8,128)(2,1)S(1)} %convolution_convert_fusion.1.gout_ref, ...), custom_call_target="tpu_custom_call" | custom-call | flops 786432 | bytes 1024 | tf_op jit(solution)/shard_map/weight_gradients/pallas_call | solution.py:897
  223.2 3.3 %fusion.3 = bf16[2,3,48,1024]{3,2,1,0:T(8,128)(2,1)} fusion(s32[]{:T(128)S(6)} %select_n.151, bf16[2,2,2,2,3,48,1024]{6,5,4,3,2,1,0:T(8,128)(2,1)} %bitcast.27, s32[]{:T(128)S(6)} %select_n.150, s32[]{:T(128)S(6)} %select_n.152, bf16[2,2,2,2,3,48,1024]{6,5,4,3,2,1,0:T(8,128)(2,1)} %bitcast.237, bf16[2,2,3,48,1024]{4,3,2,1,0:T(8,128)(2,1)} %bitcast.35, ...), kind=kLoop, calls=%fused_computation.10 | loop fusion | flops 2949120 | bytes 3538956 | tf_op jit(solution)/shard_map/convert_element_type | solution.py:136
  228.3 2.2 fusion.6
  230.5 2.1 fusion.4
  234.6 2.3 copy-done.2
  238.5 1.9 copy-done.8
  240.4 6.5 %input_gradient.1 = f32[1024,768]{1,0:T(8,128)} custom-call(bf16[1024,2304]{1,0:T(8,128)(2,1)S(1)} %bitcast.217, bf16[768,1280]{1,0:T(8,128)(2,1)S(1)} %copy-done.3, bf16[768,1280]{1,0:T(8,128)(2,1)S(1)} %copy-done.5, bf16[1024,768]{1,0:T(8,128)(2,1)S(1)} %bitcast.221, f32[1,768]{1,0:T(1,128)S(1)} %get-tuple-element.177.gain_ref, f32[1024,768]{1,0:T(8,128)S(1)} %copy-done.8), custom_call_target="tpu_custom_call" | custom-call | flops 786432 | bytes 1024 | tf_op jit(solution)/shard_map/input_gradient/pallas_call | solution.py:575
  246.8 1.7 fusion.9
  255.3 1.8 collective-permute-start.20
  257.0 3.4 %collective-permute-done.21 = bf16[192,768]{1,0:T(8,128)(2,1)S(1)} collective-permute-done((bf16[192,768]{1,0:T(8,128)(2,1)S(1)}, bf16[192,768]{1,0:T(8,128)(2,1)S(1)}, u32[]{:S(2)}, u32[]{:S(2)}) %collective-permute-start.21) | collective-permute-done | bytes 294944 | tf_op jit(solution)/shard_map/ppermute | solution.py:102
  261.8 1.9 collective-permute-done.19
  265.1 1.8 collective-permute-start.24
  268.0 1.7 collective-permute-start.22
  269.7 8.5 %collective-permute-done.20 = bf16[144,1024]{1,0:T(8,128)(2,1)S(1)} collective-permute-done((bf16[144,1024]{1,0:T(8,128)(2,1)S(1)}, bf16[144,1024]{1,0:T(8,128)(2,1)S(1)}, u32[]{:S(2)}, u32[]{:S(2)}) %collective-permute-start.20) | collective-permute-done | bytes 294944 | tf_op jit(solution)/shard_map/ppermute | solution.py:102
  278.2 6.0 %collective-permute-done.23 = bf16[48,1664]{1,0:T(8,128)(2,1)S(1)} collective-permute-done((bf16[48,1664]{1,0:T(8,128)(2,1)S(1)}, bf16[48,1664]{1,0:T(8,128)(2,1)S(1)}, u32[]{:S(2)}, u32[]{:S(2)}) %collective-permute-start.23) | collective-permute-done | bytes 159776 | tf_op jit(solution)/shard_map/ppermute | solution.py:102
  286.3 1.8 fusion.7
  (149 shorter events, 48.5 us)
Async XLA Ops:
  7.2 60.5 %copy-start = (s32[2,1,1024]{2,1,0:T(1,128)S(1)}, s32[2,1,1024]{2,1,0:T(1,128)}, u32[]{:S(2)}) copy-start(s32[2,1,1024]{2,1,0:T(1,128)} %param.15) | copy-start | bytes 24580
  7.2 99.4 %all-gather.2.cloned.1.call-start = ((), (), s32[]{:S(2)}) async-start(), calls=%async_computation | async-start | bytes 10948608 | tf_op jit(solution)/shard_map/all_gather | solution.py:978
  10.8 10.1 %collective-permute-start = (bf16[48,1280]{1,0:T(8,128)(2,1)S(1)}, bf16[48,1280]{1,0:T(8,128)(2,1)S(1)}, u32[]{:S(2)}, u32[]{:S(2)}) collective-permute-start(bf16[48,1280]{1,0:T(8,128)(2,1)S(1)} %fusion.24), channel_id=1, source_target_pairs={{0,16},{2,18},{4,20},{6,22},{8,24},{10,26},{12,28},{14,30},{16,0},... | collective-permute-start | bytes 368648 | tf_op jit(solution)/shard_map/ppermute | solution.py:26
  21.7 11.4 %collective-permute-start.1 = (bf16[2,48,1280]{2,1,0:T(8,128)(2,1)S(1)}, bf16[2,48,1280]{2,1,0:T(8,128)(2,1)S(1)}, u32[]{:S(2)}, u32[]{:S(2)}) collective-permute-start(bf16[2,48,1280]{2,1,0:T(8,128)(2,1)S(1)} %pad_maximum_fusion.6), channel_id=1, source_target_pairs={{0,8},{2,10},{4,12},{6,14},{8,0},{10,2},{12,4},{14,6},{16,24},{18,... | collective-permute-start | bytes 737288 | tf_op jit(solution)/shard_map/ppermute | solution.py:26
  22.5 14.7 %collective-permute-start.3 = (f32[32,6]{0,1:T(8,128)S(1)}, f32[32,6]{0,1:T(8,128)S(1)}, u32[]{:S(2)}, u32[]{:S(2)}) collective-permute-start(f32[32,6]{0,1:T(8,128)S(1)} %copy-done.21), channel_id=1, source_target_pairs={{0,1},{1,0},{2,3},{3,2},{4,5},{5,4},{6,7},{7,6},{8,9},{9,8},{10,11... | collective-permute-start | bytes 2312 | tf_op jit(solution)/shard_map/ppermute | solution.py:26
  33.3 9.0 %collective-permute-start.2 = (bf16[2,2,48,640]{3,2,0,1:T(8,128)(2,1)S(1)}, bf16[2,2,48,640]{3,2,0,1:T(8,128)(2,1)S(1)}, u32[]{:S(2)}, u32[]{:S(2)}) collective-permute-start(bf16[2,2,48,640]{3,2,0,1:T(8,128)(2,1)S(1)} %get-tuple-element.164), channel_id=1, source_target_pairs={{0,4},{2,6},{4,0},{6,2},{8,12},{10,14},{12,8},{14,10},{16,20},{18,... | collective-permute-start | bytes 737288 | tf_op jit(solution)/shard_map/ppermute | solution.py:26
  34.7 9.0 %collective-permute-start.4 = (bf16[2,128,768]{2,1,0:T(8,128)(2,1)S(1)}, bf16[2,128,768]{2,1,0:T(8,128)(2,1)S(1)}, u32[]{:S(2)}, u32[]{:S(2)}) collective-permute-start(bf16[2,128,768]{2,1,0:T(8,128)(2,1)S(1)} %slice_select_fusion.1), channel_id=1, source_target_pairs={{0,1},{1,0},{2,3},{3,2},{4,5},{5,4},{6,7},{7,6},{8,9},{9,8},{10,11... | collective-permute-start | bytes 1179656 | tf_op jit(solution)/shard_map/ppermute | solution.py:26
  43.8 12.0 %collective-permute-start.5 = (bf16[2,2,48,640]{3,2,0,1:T(8,128)(2,1)S(1)}, bf16[2,2,48,640]{3,2,0,1:T(8,128)(2,1)S(1)}, u32[]{:S(2)}, u32[]{:S(2)}) collective-permute-start(bf16[2,2,48,640]{3,2,0,1:T(8,128)(2,1)S(1)} %get-tuple-element.60), channel_id=1, source_target_pairs={{0,1},{1,0},{2,3},{3,2},{4,5},{5,4},{6,7},{7,6},{8,9},{9,8},{10,11... | collective-permute-start | bytes 737288 | tf_op jit(solution)/shard_map/ppermute | solution.py:26
  55.9 10.5 %collective-permute-start.6 = (bf16[2,2,48,1280]{3,2,0,1:T(8,128)(2,1)S(1)}, bf16[2,2,48,1280]{3,2,0,1:T(8,128)(2,1)S(1)}, u32[]{:S(2)}, u32[]{:S(2)}) collective-permute-start(bf16[2,2,48,1280]{3,2,0,1:T(8,128)(2,1)S(1)} %pad_maximum_fusion.3), channel_id=1, source_target_pairs={{0,4},{2,6},{4,0},{6,2},{8,12},{10,14},{12,8},{14,10},{16,20},{18,... | collective-permute-start | bytes 1474568 | tf_op jit(solution)/shard_map/ppermute | solution.py:26
  57.2 9.6 %collective-permute-start.8 = (bf16[2,2,2,48,640]{4,3,0,1,2:T(8,128)(2,1)S(1)}, bf16[2,2,2,48,640]{4,3,0,1,2:T(8,128)(2,1)S(1)}, u32[]{:S(2)}, u32[]{:S(2)}) collective-permute-start(bf16[2,2,2,48,640]{4,3,0,1,2:T(8,128)(2,1)S(1)} %pad_maximum_fusion.2), channel_id=1, source_target_pairs={{0,1},{1,0},{2,3},{3,2},{4,5},{5,4},{6,7},{7,6},{8,9},{9,8},{10,11... | collective-permute-start | bytes 1474568 | tf_op jit(solution)/shard_map/ppermute | solution.py:26
  66.8 2.6 collective-permute-start.7
  67.1 4.2 %collective-permute-start.9 = (bf16[8,48,1280]{2,1,0:T(8,128)(2,1)S(1)}, bf16[8,48,1280]{2,1,0:T(8,128)(2,1)}, u32[]{:S(2)}, u32[]{:S(2)}) collective-permute-start(bf16[8,48,1280]{2,1,0:T(8,128)(2,1)S(1)} %bitcast.234), channel_id=1, source_target_pairs={{0,2},{2,0},{4,6},{6,4},{8,10},{10,8},{12,14},{14,12},{16,18},{18,... | collective-permute-start | bytes 2949128 | tf_op jit(solution)/shard_map/ppermute | solution.py:26
  106.6 47.8 %copy-start.20 = (s32[512]{0:T(512)S(1)}, s32[512]{0:T(512)}, u32[]{:S(2)}) copy-start(s32[512]{0:T(512)} %copy-done.19) | copy-start | bytes 6148
  106.6 50.5 %copy-start.23 = (bf16[2,512,768]{2,1,0:T(8,128)(2,1)S(1)}, bf16[2,512,768]{2,1,0:T(8,128)(2,1)}, u32[]{:S(2)}) copy-start(bf16[2,512,768]{2,1,0:T(8,128)(2,1)} %get-tuple-element.63) | copy-start | bytes 4718596
  154.1 8.5 %collective-permute-start.10 = (bf16[2304,1024]{1,0:T(8,128)(2,1)}, bf16[2304,1024]{1,0:T(8,128)(2,1)}, u32[]{:S(2)}, u32[]{:S(2)}) collective-permute-start(bf16[2304,1024]{1,0:T(8,128)(2,1)} %bitcast.256), channel_id=1, source_target_pairs={{0,2},{2,0},{4,6},{6,4},{8,10},{10,8},{12,14},{14,12},{16,18},{18,... | collective-permute-start | bytes 14155784 | tf_op jit(solution)/shard_map/ppermute | solution.py:102
  155.7 11.6 %collective-permute-start.11 = (bf16[2,128,768]{2,1,0:T(8,128)(2,1)S(1)}, bf16[2,128,768]{2,1,0:T(8,128)(2,1)S(1)}, u32[]{:S(2)}, u32[]{:S(2)}) collective-permute-start(bf16[2,128,768]{2,1,0:T(8,128)(2,1)S(1)} %slice_select_fusion), channel_id=1, source_target_pairs={{0,1},{1,0},{2,3},{3,2},{4,5},{5,4},{6,7},{7,6},{8,9},{9,8},{10,11... | collective-permute-start | bytes 1179656 | tf_op jit(solution)/shard_map/ppermute | solution.py:26
  167.3 55.8 %collective-permute-start.12 = (bf16[576,1024]{1,0:T(8,128)(2,1)}, bf16[576,1024]{1,0:T(8,128)(2,1)}, u32[]{:S(2)}, u32[]{:S(2)}) collective-permute-start(bf16[576,1024]{1,0:T(8,128)(2,1)} %bitcast.34), channel_id=1, source_target_pairs={{0,1},{1,0},{2,3},{3,2},{4,5},{5,4},{6,7},{7,6},{8,9},{9,8},{10,11... | collective-permute-start | bytes 3538952 | tf_op jit(solution)/shard_map/ppermute | solution.py:102
  168.6 54.5 %collective-permute-start.13 = (bf16[576,1024]{1,0:T(8,128)(2,1)}, bf16[576,1024]{1,0:T(8,128)(2,1)}, u32[]{:S(2)}, u32[]{:S(2)}) collective-permute-start(bf16[576,1024]{1,0:T(8,128)(2,1)} %bitcast.36), channel_id=1, source_target_pairs={{0,4},{2,6},{4,0},{6,2},{8,12},{10,14},{12,8},{14,10},{16,20},{18,... | collective-permute-start | bytes 3538952 | tf_op jit(solution)/shard_map/ppermute | solution.py:102
  169.3 53.8 %collective-permute-start.14 = (bf16[576,1024]{1,0:T(8,128)(2,1)S(1)}, bf16[576,1024]{1,0:T(8,128)(2,1)}, u32[]{:S(2)}, u32[]{:S(2)}) collective-permute-start(bf16[576,1024]{1,0:T(8,128)(2,1)S(1)} %bitcast.244), channel_id=1, source_target_pairs={{0,5},{1,4},{2,7},{3,6},{4,1},{5,0},{6,3},{7,2},{8,13},{9,12},{10,... | collective-permute-start | bytes 3538952 | tf_op jit(solution)/shard_map/ppermute | solution.py:102
  170.8 40.6 %copy-start.4 = (bf16[768,1280]{1,0:T(8,128)(2,1)S(1)}, bf16[768,1280]{1,0:T(8,128)(2,1)}, u32[]{:S(2)}) copy-start(bf16[768,1280]{1,0:T(8,128)(2,1)} %get-tuple-element.79.wb_ref) | copy-start | bytes 5898244
  170.8 40.6 %copy-start.11 = (bf16[2,512,768]{2,1,0:T(8,128)(2,1)S(1)}, bf16[2,512,768]{2,1,0:T(8,128)(2,1)}, u32[]{:S(2)}) copy-start(bf16[2,512,768]{2,1,0:T(8,128)(2,1)} %get-tuple-element.72) | copy-start | bytes 4718596
  170.8 40.6 %copy-start.16 = (f32[1,768]{1,0:T(1,128)S(1)}, f32[1,768]{1,0:T(1,128)}, u32[]{:S(2)}) copy-start(f32[1,768]{1,0:T(1,128)} %get-tuple-element.80.ggain_ref) | copy-start | bytes 9220
  223.1 5.2 %collective-permute-start.15 = (bf16[768,1664]{1,0:T(8,128)(2,1)}, bf16[768,1664]{1,0:T(8,128)(2,1)}, u32[]{:S(2)}, u32[]{:S(2)}) collective-permute-start(bf16[768,1664]{1,0:T(8,128)(2,1)} %bitcast.46), channel_id=1, source_target_pairs={{0,2},{2,0},{4,6},{6,4},{8,10},{10,8},{12,14},{14,12},{16,18},{18,... | collective-permute-start | bytes 7667720 | tf_op jit(solution)/shard_map/ppermute | solution.py:102
  226.5 20.3 %collective-permute-start.18 = (bf16[288,1024]{1,0:T(8,128)(2,1)}, bf16[288,1024]{1,0:T(8,128)(2,1)}, u32[]{:S(2)}, u32[]{:S(2)}) collective-permute-start(bf16[288,1024]{1,0:T(8,128)(2,1)} %bitcast.58), channel_id=1, source_target_pairs={{0,8},{2,10},{4,12},{6,14},{8,0},{10,2},{12,4},{14,6},{16,24},{18,... | collective-permute-start | bytes 1769480 | tf_op jit(solution)/shard_map/ppermute | solution.py:102
  232.6 18.2 %collective-permute-start.17 = (bf16[384,896]{1,0:T(8,128)(2,1)}, bf16[384,896]{1,0:T(8,128)(2,1)}, u32[]{:S(2)}, u32[]{:S(2)}) collective-permute-start(bf16[384,896]{1,0:T(8,128)(2,1)} %bitcast.52), channel_id=1, source_target_pairs={{0,1},{1,0},{2,3},{3,2},{4,5},{5,4},{6,7},{7,6},{8,9},{9,8},{10,11... | collective-permute-start | bytes 2064392 | tf_op jit(solution)/shard_map/ppermute | solution.py:102
  233.9 17.0 %collective-permute-start.16 = (bf16[384,768]{1,0:T(8,128)(2,1)}, bf16[384,768]{1,0:T(8,128)(2,1)}, u32[]{:S(2)}, u32[]{:S(2)}) collective-permute-start(bf16[384,768]{1,0:T(8,128)(2,1)} %bitcast.50), channel_id=1, source_target_pairs={{0,4},{2,6},{4,0},{6,2},{8,12},{10,14},{12,8},{14,10},{16,20},{18,... | collective-permute-start | bytes 1769480 | tf_op jit(solution)/shard_map/ppermute | solution.py:102
  251.9 8.6 %collective-permute-start.21 = (bf16[192,768]{1,0:T(8,128)(2,1)S(1)}, bf16[192,768]{1,0:T(8,128)(2,1)S(1)}, u32[]{:S(2)}, u32[]{:S(2)}) collective-permute-start(bf16[192,768]{1,0:T(8,128)(2,1)S(1)} %fusion.8), channel_id=1, source_target_pairs={{0,1},{1,0},{2,3},{3,2},{4,5},{5,4},{6,7},{7,6},{8,9},{9,8},{10,11... | collective-permute-start | bytes 884744 | tf_op jit(solution)/shard_map/ppermute | solution.py:102
  254.4 9.3 %collective-permute-start.19 = (bf16[192,896]{1,0:T(8,128)(2,1)S(1)}, bf16[192,896]{1,0:T(8,128)(2,1)S(1)}, u32[]{:S(2)}, u32[]{:S(2)}) collective-permute-start(bf16[192,896]{1,0:T(8,128)(2,1)S(1)} %fusion.5), channel_id=1, source_target_pairs={{0,4},{2,6},{4,0},{6,2},{8,12},{10,14},{12,8},{14,10},{16,20},{18,... | collective-permute-start | bytes 1032200 | tf_op jit(solution)/shard_map/ppermute | solution.py:102
  255.3 22.9 %collective-permute-start.20 = (bf16[144,1024]{1,0:T(8,128)(2,1)S(1)}, bf16[144,1024]{1,0:T(8,128)(2,1)S(1)}, u32[]{:S(2)}, u32[]{:S(2)}) collective-permute-start(bf16[144,1024]{1,0:T(8,128)(2,1)S(1)} %bitcast.249), channel_id=1, source_target_pairs={{0,16},{2,18},{4,20},{6,22},{8,24},{10,26},{12,28},{14,30},{16,0},... | collective-permute-start | bytes 884744 | tf_op jit(solution)/shard_map/ppermute | solution.py:102
  265.1 13.1 %collective-permute-start.24 = (bf16[48,1664]{1,0:T(8,128)(2,1)S(1)}, bf16[48,1664]{1,0:T(8,128)(2,1)S(1)}, u32[]{:S(2)}, u32[]{:S(2)}) collective-permute-start(bf16[48,1664]{1,0:T(8,128)(2,1)S(1)} %pad_maximum_fusion.9), channel_id=1, source_target_pairs={{0,24},{2,26},{4,28},{6,30},{8,16},{10,18},{12,20},{14,22},{16,8},... | collective-permute-start | bytes 479240 | tf_op jit(solution)/shard_map/ppermute | solution.py:102
  266.9 17.2 %collective-permute-start.23 = (bf16[48,1664]{1,0:T(8,128)(2,1)S(1)}, bf16[48,1664]{1,0:T(8,128)(2,1)S(1)}, u32[]{:S(2)}, u32[]{:S(2)}) collective-permute-start(bf16[48,1664]{1,0:T(8,128)(2,1)S(1)} %pad_maximum_fusion.8), channel_id=1, source_target_pairs={{0,16},{2,18},{4,20},{6,22},{8,24},{10,26},{12,28},{14,30},{16,0},... | collective-permute-start | bytes 479240 | tf_op jit(solution)/shard_map/ppermute | solution.py:102
  268.0 16.2 %collective-permute-start.22 = (bf16[48,1664]{1,0:T(8,128)(2,1)S(1)}, bf16[48,1664]{1,0:T(8,128)(2,1)S(1)}, u32[]{:S(2)}, u32[]{:S(2)}) collective-permute-start(bf16[48,1664]{1,0:T(8,128)(2,1)S(1)} %pad_maximum_fusion.7), channel_id=1, source_target_pairs={{0,8},{2,10},{4,12},{6,14},{8,0},{10,2},{12,4},{14,6},{16,24},{18,... | collective-permute-start | bytes 479240 | tf_op jit(solution)/shard_map/ppermute | solution.py:102
  (21 other events, 183.6 us)
Sparse Core Ops, SparseCore 0:
  11.5 95.0 all-gather.1

commit v2 on v1

--- a/solution.py
+++ b/solution.py
@@ -13,6 +13,7 @@
 BLOCK = 128
 LANES = 128
 FEED_CHUNK = 1024
+EDGE_CHUNK = 256
 BF = jnp.bfloat16
 F32 = jnp.float32
 
@@ -309,7 +310,7 @@
 
         def own(index, carry):
             value = normed(x_ref[0, place_of(index), :])
-            n1_ref[0, place_of(index), :] = value
+            n1_ref[0, :, place_of(index)] = value.T
             n1_s[place_of(index + shift), :] = value
             return carry
 
@@ -368,7 +369,7 @@
         out_shape=(
             jax.ShapeDtypeStruct((rows, half, pairs * LANES), BF),
             jax.ShapeDtypeStruct((rows, length, width), BF),
-            jax.ShapeDtypeStruct((rows, half, model), BF),
+            jax.ShapeDtypeStruct((rows, model, half), BF),
             jax.ShapeDtypeStruct((model, widths[0]), BF),
             jax.ShapeDtypeStruct((model, widths[1]), BF),
         ),
@@ -390,7 +391,7 @@
             out_specs=[
                 pl.BlockSpec((1, BLOCK, pairs * LANES), lambda r, i, s: (r, i, 0)),
                 pl.BlockSpec((1, length, width), lambda r, i, s: (r, 0, 0)),
-                pl.BlockSpec((1, half, model), lambda r, i, s: (r, 0, 0)),
+                pl.BlockSpec((1, model, half), lambda r, i, s: (r, 0, 0)),
                 pl.BlockSpec((model, widths[0]), lambda r, i, s: (0, 0), pipeline_mode=once),
                 pl.BlockSpec((model, widths[1]), lambda r, i, s: (0, 0), pipeline_mode=once),
             ],
@@ -520,7 +521,7 @@
     return pl.pallas_call(
         functools.partial(attend_back_kernel, pairs, last, own_blocks),
         out_shape=(
-            jax.ShapeDtypeStruct((rows, half, width), BF),
+            pltpu.HBM((rows, half, width), BF),
             jax.ShapeDtypeStruct((2 * pairs, 1, 4 * BLOCK), F32),
         ),
         grid_spec=pltpu.PrefetchScalarGridSpec(
@@ -546,7 +547,7 @@
             ],
         ),
         compiler_params=pltpu.CompilerParams(
-            dimension_semantics=("arbitrary", "arbitrary"), vmem_limit_bytes=56 << 20
+            dimension_semantics=("arbitrary", "arbitrary"), vmem_limit_bytes=38 << 20
         ),
         cost_estimate=cost,
         name="attend_backward",
@@ -586,7 +587,7 @@
         ],
         out_specs=pl.BlockSpec((chunk, model), here),
         compiler_params=pltpu.CompilerParams(
-            dimension_semantics=("arbitrary",), vmem_limit_bytes=40 << 20
+            dimension_semantics=("arbitrary",), vmem_limit_bytes=60 << 20
         ),
         cost_estimate=pl.CostEstimate(
             flops=tokens * model, transcendentals=tokens, bytes_accessed=tokens
@@ -669,12 +670,14 @@
     final = pl.num_programs(0) * pl.num_programs(1) - 1
     half = heads_ref.shape[1] // 2
 
-    def for_chunks(work):
+    def for_chunks(work, count):
         def one(index, carry):
-            work(pl.ds(pl.multiple_of(index * chunk, chunk), chunk))
+            work(pl.ds(pl.multiple_of(index * count, count), count))
             return carry
 
-        lax.fori_loop(0, tokens // chunk, one, 0)
+        lax.fori_loop(0, tokens // count, one, 0)
+
+    edge = min(EDGE_CHUNK, tokens)
 
     @pl.when(step == 0)
     def _():
@@ -691,9 +694,9 @@
             n2_s[place, :] = normed
             n2t_s[:, place] = normed.T
             cott_s[:, place] = cot_ref[place, :].T
-            gn2_s[place, :] = jnp.zeros((chunk, width), F32)
-
-        for_chunks(work)
+            gn2_s[place, :] = jnp.zeros((edge, width), F32)
+
+        for_chunks(work, edge)
 
     def work(place):
         n2, cot = n2_s[place, :], cot_ref[place, :]
@@ -709,7 +712,7 @@
         out_ref[place, :] += dot_nt(hidden, wd_ref[...])
         gn2_s[place, :] += dot_nt(grad_gate, wg_ref[...]) + dot_nt(grad_up, wu_ref[...])
 
-    for_chunks(work)
+    for_chunks(work, chunk)
 
     def store(kind, grad):
         split_rows(core_ref[0], shard, grad.astype(BF), keep_ref, send_ref, (kind,))
@@ -732,7 +735,7 @@
             gmid_ref[place, :] = grad
             gattn_ref[place, :] = grad.astype(BF)
 
-        for_chunks(work)
+        for_chunks(work, edge)
 
 
 def feed_forward(core, heads_out, x_own, gain, cotangent, weights, hidden_cols, shard):
@@ -831,7 +834,7 @@
     send_ref,
     gain_s,
 ):
-    model = n1_ref.shape[1]
+    rows, model, length = n1_ref.shape
     wide = gqkv_ref.shape[1] // 3
     half = pl.program_id(0)
 
@@ -843,7 +846,10 @@
     for index in range(4):
         columns = slice(index * wide, (index + 1) * wide)
         if index < 3:
-            grad = dot_tn(n1_ref[...], gqkv_ref[:, columns])
+            grad = sum(
+                dot_nn(n1_ref[row], gqkv_ref[row * length : (row + 1) * length, columns])
+                for row in range(rows)
+            )
             for at in range(index * wide, (index + 1) * wide, LANES):
                 if at < wide_a:
                     weight = wa_ref[:, lanes_of(half * wide_a + at)]
@@ -885,14 +891,15 @@
 def weight_gradients(
     core, n1, grad_qkv, grad_out_w, part_a, part_b, gain, grad_gain2, diagonals, onehot, shard
 ):
-    tokens, model = n1.shape
+    rows, model, length = n1.shape
+    tokens = rows * length
     wide = grad_out_w.shape[1] // 2
     groups = model // (2 * shard)
     whole = lambda t, c: (0, 0)
     half = lambda t, c: (0, t)
     once = pl.Buffered(1)
     lines = 2 * model // LANES + diagonals.shape[0]
-    piece = jax.ShapeDtypeStruct((2, groups, shard, 4 * wide + pl.cdiv(lines, shard) * LANES), BF)
+    piece = pltpu.HBM((2, groups, shard, 4 * wide + pl.cdiv(lines, shard) * LANES), BF)
     piece_spec = pl.BlockSpec(piece.shape, lambda t, c: (0, 0, 0, 0), pipeline_mode=once)
     return pl.pallas_call(
         functools.partial(weight_kernel, shard),
@@ -901,7 +908,7 @@
             num_scalar_prefetch=1,
             grid=(2,),
             in_specs=[
-                pl.BlockSpec((tokens, model), whole, pipeline_mode=once),
+                pl.BlockSpec(n1.shape, lambda t, c: (0, 0, 0), pipeline_mode=once),
                 pl.BlockSpec((tokens, 3 * wide), half),
                 pl.BlockSpec((model, wide), half),
                 pl.BlockSpec(part_a.shape, whole, pipeline_mode=once),
@@ -1064,9 +1071,10 @@
         shift, qkv, grad_heads, grad_halo, out_weight, seg_rows, seg_lanes, bias
     )
     grad_qkv = grad_qkv.reshape(rows * half, grad_qkv.shape[-1])
+    grad_qkv = pltpu.with_memory_space_constraint(grad_qkv, pltpu.HBM)
     keep_w, send_w = weight_gradients(
         core,
-        n1.reshape(rows * half, width),
+        n1,
         grad_qkv,
         grad_out_w,
         part_a,
@@ -1079,34 +1087,27 @@
     )
     keep_w, send_w = end_sends(feed, others, (keep_w, send_w))
     tail = both_cores(keep_w, send_w, [0, 2 * head_cols])
-    late = list(far)
     waiting = []
-    if late:
+    for group in far_groups:
+        end_joint(feed, waiting)
         waiting, (tail[0].terms[0].array,) = start_joint(
-            feed, [late.pop()], (tail[0].terms[0].array,)
+            feed, group, (tail[0].terms[0].array,)
         )
     others, (grad_qkv,) = start_sends(tail, [order[:1] for order in near], (grad_qkv,))
     grad_in = input_gradient(
         grad_qkv, part_a, part_b, x_own.reshape(rows * half, width), gain1, grad_middle
     )
-    if waiting:
-        waiting, (grad_in,) = tie(waiting, (grad_in,))
-        end_joint(feed, waiting)
-    while late:
-        waiting, (grad_in,) = start_joint(feed, [late.pop()], (grad_in,))
-        if late:
-            end_joint(feed, waiting)
     (grad_in,) = end_sends(tail, others, (grad_in,))
     if twice:
         others, _ = start_sends(tail, [order[1:] for order in near])
+        flat, (last,) = tie(list(waiting) + others[0], others[1])
+        waiting, others = flat[: len(waiting)], [flat[len(waiting) :], [last]]
         end_sends(tail, others)
-    for index, group in enumerate(far_groups):
+    end_joint(feed, waiting)
+    feed_sums = jnp.concatenate([s.total() for s in feed], axis=-1)
+    for group in far_groups:
         others, _ = start_joint(tail, group)
-        if index == 0 and len(far) > 1:
-            waiting, others = tie(waiting, others)
-            end_joint(feed, waiting)
         end_joint(tail, others)
-    feed_sums = jnp.concatenate([s.total() for s in feed], axis=-1)
     sums_a, sums_b = [s.total() for s in tail]
 
     small = sums_b[:, 2 * head_cols :]

time: 299 us -> 290 us (0.970)
  local copies, waits for them, and re-layouts: 19.8 us -> 12 us
  waiting for transfers between devices: 66.1 us -> 62.7 us
    unnamed x57 -> x49, local copies, waits for them, and re-layouts: 10.9 us -> 3.06 us
    all_gather x1, waiting for transfers between devices: 9.1 us -> 4.6 us  [body(): second = lax.all_gather(second_shard, ('tp', 'dp'), axis=0, tiled=True)]
    pallas_call x1, Pallas kernels: 39.9 us -> 35.5 us  [attend_backward(): pl.pallas_call(functools.partial(attend_back_kernel, pairs, last, own_blo...]
    pallas_call x1, Pallas kernels: 6.46 us -> 10 us  [input_gradient(): pl.pallas_call(input_kernel, out_shape=jax.ShapeDtypeStruct((tokens, mode...]
    convert_element_type x9 -> x8, other arithmetic: 16.8 us -> 14.7 us  [sends(): sum((t.part(self.done, flip).astype(F32) for t in self.terms)).astype(BF)]
    ppermute x14 -> x15, starting transfers between devices: 15.7 us -> 17.7 us  [swap_with(): return lax.ppermute(flat, axes, pairs).reshape(value.shape)]
    ppermute x14 -> x15, waiting for transfers between devices: 20.4 us -> 21.9 us  [swap_with(): return lax.ppermute(flat, axes, pairs).reshape(value.shape)]
  transfers between devices with their start and end apart: 26 -> 27, of which waited for: 12 -> 15; matrix products, arithmetic and copies ran while one was open for 12% -> 11% of each run, Pallas kernels for 28% -> 29%
where the time goes in v2:
time: 290 us; the launch traced here: 289 us
  Pallas kernels  133 us (46%)
  waiting for transfers between devices  62.7 us (22%)
  starting transfers between devices  32.3 us (11%)
  other arithmetic  30 us (10%)
  between operations  14.5 us (5%)
  local copies, waits for them, and re-layouts  12 us (4%)
  matrix products  4.53 us (2%)
    pallas_call x1, Pallas kernels, feed_forward(): pl.pallas_call(functools.partial(feed_kernel, min(FEED_CHUNK, tokens), sh...  48.1 us
    ppermute x11, waiting for transfers between devices, swap(): return lax.ppermute(value, axis, [(i, i ^ 1 << bit) for i in range(count)])  36.1 us
    pallas_call x1, Pallas kernels, attend_backward(): pl.pallas_call(functools.partial(attend_back_kernel, pairs, last, own_blo...  35.5 us
    pallas_call x1, Pallas kernels, attend_forward(): pl.pallas_call(functools.partial(attend_kernel, pairs, last), out_shape=(...  24.1 us
    ppermute x15, waiting for transfers between devices, swap_with(): return lax.ppermute(flat, axes, pairs).reshape(value.shape)  21.9 us
    ppermute x15, starting transfers between devices, swap_with(): return lax.ppermute(flat, axes, pairs).reshape(value.shape)  17.7 us
    convert_element_type x8, other arithmetic, sends(): sum((t.part(self.done, flip).astype(F32) for t in self.terms)).astype(BF)  14.7 us
    ppermute x11, starting transfers between devices, swap(): return lax.ppermute(value, axis, [(i, i ^ 1 << bit) for i in range(count)])  14.5 us
  transfers between devices with their start and end apart: 27, of which 15 were waited for; matrix products, arithmetic and copies ran while one was open for 11% of the time, Pallas kernels for 29%

profile of v2, /device:TPU:0, one launch (start us, length us, event | category | flops | bytes accessed | tf_op | source)
XLA Modules:
  0.0 288.6 jit_solution(14377309483441071109)
XLA Ops:
  7.3 1.9 pad_maximum_fusion.4
  10.8 4.1 %collective-permute-start = (bf16[48,1280]{1,0:T(8,128)(2,1)S(1)}, bf16[48,1280]{1,0:T(8,128)(2,1)S(1)}, u32[]{:S(2)}, u32[]{:S(2)}) collective-permute-start(bf16[48,1280]{1,0:T(8,128)(2,1)S(1)} %fusion.27), channel_id=1, source_target_pairs={{0,16},{2,18},{4,20},{6,22},{8,24},{10,26},{12,28},{14,30},{16,0},... | collective-permute-start | bytes 368648 | tf_op jit(solution)/shard_map/ppermute | solution.py:27
  14.9 6.0 %collective-permute-done = bf16[48,1280]{1,0:T(8,128)(2,1)S(1)} collective-permute-done((bf16[48,1280]{1,0:T(8,128)(2,1)S(1)}, bf16[48,1280]{1,0:T(8,128)(2,1)S(1)}, u32[]{:S(2)}, u32[]{:S(2)}) %collective-permute-start) | collective-permute-done | bytes 122912 | tf_op jit(solution)/shard_map/ppermute | solution.py:27
  22.5 1.5 collective-permute-start.3
  24.0 9.2 %collective-permute-done.1 = bf16[2,48,1280]{2,1,0:T(8,128)(2,1)S(1)} collective-permute-done((bf16[2,48,1280]{2,1,0:T(8,128)(2,1)S(1)}, bf16[2,48,1280]{2,1,0:T(8,128)(2,1)S(1)}, u32[]{:S(2)}, u32[]{:S(2)}) %collective-permute-start.1) | collective-permute-done | bytes 245792 | tf_op jit(solution)/shard_map/ppermute | solution.py:27
  33.4 1.5 collective-permute-start.2
  35.0 1.6 collective-permute-start.4
  38.2 4.2 %window_bias.1.bias_ref = f32[6,384,256]{2,1,0:T(8,128)} custom-call(f32[12,1,512]{2,1,0:T(1,128)} %broadcast_in_dim.19.turned_ref), custom_call_target="tpu_custom_call" | custom-call | tf_op jit(solution)/shard_map/window_bias/pallas_call | solution.py:608
  44.4 1.7 collective-permute-start.5
  46.1 9.0 %collective-permute-done.5 = bf16[2,2,48,640]{3,2,0,1:T(8,128)(2,1)S(1)} collective-permute-done((bf16[2,2,48,640]{3,2,0,1:T(8,128)(2,1)S(1)}, bf16[2,2,48,640]{3,2,0,1:T(8,128)(2,1)S(1)}, u32[]{:S(2)}, u32[]{:S(2)}) %collective-permute-start.5) | collective-permute-done | bytes 245792 | tf_op jit(solution)/shard_map/ppermute | solution.py:27
  56.8 9.3 %collective-permute-done.6 = bf16[2,2,48,1280]{3,2,0,1:T(8,128)(2,1)S(1)} collective-permute-done((bf16[2,2,48,1280]{3,2,0,1:T(8,128)(2,1)S(1)}, bf16[2,2,48,1280]{3,2,0,1:T(8,128)(2,1)S(1)}, u32[]{:S(2)}, u32[]{:S(2)}) %collective-permute-start.6) | collective-permute-done | bytes 491552 | tf_op jit(solution)/shard_map/ppermute | solution.py:27
  71.3 1.4 collective-permute-done.9.a_other_ref
  74.9 24.1 %attend_forward.1 = (bf16[2,512,768]{2,1,0:T(8,128)(2,1)}, bf16[2,640,2304]{2,1,0:T(8,128)(2,1)}, bf16[2,768,512]{2,1,0:T(8,128)(2,1)}, bf16[768,1280]{1,0:T(8,128)(2,1)}, bf16[768,1280]{1,0:T(8,128)(2,1)}) custom-call(s32[2]{0:T(128)S(1)} %pad_add_fusion.shift_ref, bf16[2,512,768]{2,1,0:T(8,128)(2,1)} %bitcast.238, ...), custom_call_target="tpu_custom_call" | custom-call | flops 6945767424 | bytes 15728640 | tf_op jit(solution)/shard_map/attend_forward/pallas_call | solution.py:367
  98.9 4.6 %all-gather.2.cloned.1.call-done.wo0_ref.wo1_ref.wg_ref.wu_ref.wd_ref = bf16[1536,3456]{1,0:T(8,128)(2,1)} async-done(((bf16[48,3456]{1,0:T(8,128)(2,1)}), bf16[1536,3456]{1,0:T(8,128)(2,1)}) %all-gather.2.cloned.1.call-update) | async-done | bytes 10616848 | tf_op jit(solution)/shard_map/all_gather | solution.py:985
  103.5 48.1 %feed_forward.1 = (f32[1024,768]{1,0:T(8,128)}, f32[1024,768]{1,0:T(8,128)}, bf16[1024,768]{1,0:T(8,128)(2,1)}, f32[1,768]{1,0:T(1,128)}, bf16[2,8,3,48,1024]{4,...) custom-call(s32[1]{0:T(128)} %bitcast.core_ref, bf16[1024,768]{1,0:T(8,128)(2,1)} %bitcast.269, ...), custom_call_target="tpu_custom_call" | custom-call | flops 30198988800 | bytes 32636928 | tf_op jit(solution)/shard_map/feed_forward/pallas_call | solution.py:752
  153.2 1.6 collective-permute-start.11
  154.8 3.0 %convolution_convert_fusion.1.gout_ref = bf16[768,768]{1,0:T(8,128)(2,1)S(1)} fusion(bf16[1024,768]{1,0:T(8,128)(2,1)} %get-tuple-element.66, bf16[1024,768]{1,0:T(8,128)(2,1)S(1)} %bitcast.270), kind=kOutput, calls=%fused_computation.4 | convolution fusion | flops 1208549376 | bytes 4325376 | tf_op jit(solution)/shard_map/dot_general | solution.py:238
  160.1 3.9 %fusion.2 = (bf16[2,2,3,48,1024]{4,3,2,1,0:T(8,128)(2,1)S(1)}, bf16[2,2,3,48,1024]{4,3,2,1,0:T(8,128)(2,1)S(1)}, bf16[2,2,3,48,1024]{4,3,2,1,0:T(8,128)(2,1)S(1)}) fusion(bf16[2,2,2,2,3,48,1024]{6,5,4,3,2,1,0:T(8,128)(2,1)} %bitcast.27, s32[]{:T(128)S(6)} %select_n.154, s32[]{:T(128)S(6)} %select_n.155, bf16[2,2,2,2,3,48,1024]{6,5,4,3,2,1,0:T(8,128)(2,1)S(1)} %bitcast.237, ...), kind=kLoop, calls=%fused_computation.8 | loop fusion | flops 7077888 | bytes 10616848 | tf_op jit(solution)/shard_map/convert_element_type | solution.py:137
  164.5 1.6 collective-permute-start.12
  168.0 35.5 %attend_backward.1 = (bf16[2,512,2304]{2,1,0:T(8,128)(2,1)}, f32[12,1,512]{2,1,0:T(1,128)S(1)}) custom-call(s32[1]{0:T(128)} %bitcast.1.shift_ref, bf16[2,640,2304]{2,1,0:T(8,128)(2,1)S(1)} %bitcast.230, bf16[2,512,768]{2,1,0:T(8,128)(2,1)S(1)} %bitcast.228, bf16[2,128,768]{2,1,0:T(8,128)(2,1)S(1)} %collective-permute-done.11.halo_ref, ...), custom_call_target="tpu_custom_call" | custom-call | flops 45600473088 | bytes 16908288 | tf_op jit(solution)/shard_map/attend_backward/pallas_call | solution.py:521
  203.5 10.8 %weight_gradients.1 = (bf16[2,8,48,1664]{3,2,1,0:T(8,128)(2,1)}, bf16[2,8,48,1664]{3,2,1,0:T(8,128)(2,1)}) custom-call(s32[1]{0:T(128)} %bitcast.core_ref, bf16[2,768,512]{2,1,0:T(8,128)(2,1)S(1)} %copy-done.5, bf16[1024,2304]{1,0:T(8,128)(2,1)} %bitcast.231, bf16[768,768]{1,0:T(8,128)(2,1)S(1)} %convolution_convert_fusion.1.gout_ref, ...), custom_call_target="tpu_custom_call" | custom-call | flops 786432 | bytes 1024 | tf_op jit(solution)/shard_map/weight_gradients/pallas_call | solution.py:904
  214.3 4.5 %collective-permute-done.14 = bf16[576,1024]{1,0:T(8,128)(2,1)} collective-permute-done((bf16[576,1024]{1,0:T(8,128)(2,1)S(1)}, bf16[576,1024]{1,0:T(8,128)(2,1)}, u32[]{:S(2)}, u32[]{:S(2)}) %collective-permute-start.14) | collective-permute-done | bytes 1179680 | tf_op jit(solution)/shard_map/ppermute | solution.py:103
  218.9 4.0 %fusion.10 = (bf16[3,48,1024]{2,1,0:T(8,128)(2,1)}, bf16[3,48,1024]{2,1,0:T(8,128)(2,1)}, bf16[3,48,1024]{2,1,0:T(8,128)(2,1)}) fusion(bf16[2,2,3,48,1024]{4,3,2,1,0:T(8,128)(2,1)} %bitcast.39, s32[]{:T(128)S(6)} %select_n.157, s32[]{:T(128)S(6)} %select_n.152, bf16[2,2,3,48,1024]{4,3,2,1,0:T(8,128)(2,1)} %bitcast.37, ...), kind=kLoop, calls=%fused_computation.26 | loop fusion | flops 4423680 | bytes 5308440 | tf_op jit(solution)/shard_map/convert_element_type | solution.py:137
  225.3 2.1 fusion.5
  229.5 2.4 collective-permute-start.18
  234.3 10.0 %input_gradient.1 = f32[1024,768]{1,0:T(8,128)} custom-call(bf16[1024,2304]{1,0:T(8,128)(2,1)} %bitcast.232, bf16[768,1280]{1,0:T(8,128)(2,1)} %get-tuple-element.77.wa_ref, bf16[768,1280]{1,0:T(8,128)(2,1)} %get-tuple-element.78.wb_ref, bf16[1024,768]{1,0:T(8,128)(2,1)} %bitcast.240, f32[1,768]{1,0:T(1,128)} %copy-done.6, ...), custom_call_target="tpu_custom_call" | custom-call | flops 786432 | bytes 1024 | tf_op jit(solution)/shard_map/input_gradient/pallas_call | solution.py:576
  251.0 4.7 %collective-permute-done.19 = bf16[144,1024]{1,0:T(8,128)(2,1)} collective-permute-done((bf16[144,1024]{1,0:T(8,128)(2,1)}, bf16[144,1024]{1,0:T(8,128)(2,1)}, u32[]{:S(2)}, u32[]{:S(2)}) %collective-permute-start.19) | collective-permute-done | bytes 294944 | tf_op jit(solution)/shard_map/ppermute | solution.py:103
  255.7 2.4 collective-permute-done.21
  260.7 2.8 collective-permute-start.23
  264.5 1.7 collective-permute-start.25
  266.1 1.9 fusion.8
  268.8 8.4 %collective-permute-done.24 = bf16[48,1664]{1,0:T(8,128)(2,1)S(1)} collective-permute-done((bf16[48,1664]{1,0:T(8,128)(2,1)S(1)}, bf16[48,1664]{1,0:T(8,128)(2,1)S(1)}, u32[]{:S(2)}, u32[]{:S(2)}) %collective-permute-start.24) | collective-permute-done | bytes 159776 | tf_op jit(solution)/shard_map/ppermute | solution.py:103
  (143 shorter events, 44.7 us)
Async XLA Ops:
  7.2 61.4 %copy-start = (s32[2,1,1024]{2,1,0:T(1,128)S(1)}, s32[2,1,1024]{2,1,0:T(1,128)}, u32[]{:S(2)}) copy-start(s32[2,1,1024]{2,1,0:T(1,128)} %param.15) | copy-start | bytes 24580
  7.2 96.3 %all-gather.2.cloned.1.call-start = ((), (), s32[]{:S(2)}) async-start(), calls=%async_computation | async-start | bytes 10948608 | tf_op jit(solution)/shard_map/all_gather | solution.py:985
  10.8 10.1 %collective-permute-start = (bf16[48,1280]{1,0:T(8,128)(2,1)S(1)}, bf16[48,1280]{1,0:T(8,128)(2,1)S(1)}, u32[]{:S(2)}, u32[]{:S(2)}) collective-permute-start(bf16[48,1280]{1,0:T(8,128)(2,1)S(1)} %fusion.27), channel_id=1, source_target_pairs={{0,16},{2,18},{4,20},{6,22},{8,24},{10,26},{12,28},{14,30},{16,0},... | collective-permute-start | bytes 368648 | tf_op jit(solution)/shard_map/ppermute | solution.py:27
  21.7 11.5 %collective-permute-start.1 = (bf16[2,48,1280]{2,1,0:T(8,128)(2,1)S(1)}, bf16[2,48,1280]{2,1,0:T(8,128)(2,1)S(1)}, u32[]{:S(2)}, u32[]{:S(2)}) collective-permute-start(bf16[2,48,1280]{2,1,0:T(8,128)(2,1)S(1)} %pad_maximum_fusion.6), channel_id=1, source_target_pairs={{0,8},{2,10},{4,12},{6,14},{8,0},{10,2},{12,4},{14,6},{16,24},{18,... | collective-permute-start | bytes 737288 | tf_op jit(solution)/shard_map/ppermute | solution.py:27
  22.5 14.9 %collective-permute-start.3 = (f32[32,6]{0,1:T(8,128)S(1)}, f32[32,6]{0,1:T(8,128)S(1)}, u32[]{:S(2)}, u32[]{:S(2)}) collective-permute-start(f32[32,6]{0,1:T(8,128)S(1)} %copy-done.17), channel_id=1, source_target_pairs={{0,1},{1,0},{2,3},{3,2},{4,5},{5,4},{6,7},{7,6},{8,9},{9,8},{10,11... | collective-permute-start | bytes 2312 | tf_op jit(solution)/shard_map/ppermute | solution.py:27
  33.4 9.1 %collective-permute-start.2 = (bf16[2,2,48,640]{3,2,0,1:T(8,128)(2,1)S(1)}, bf16[2,2,48,640]{3,2,0,1:T(8,128)(2,1)}, u32[]{:S(2)}, u32[]{:S(2)}) collective-permute-start(bf16[2,2,48,640]{3,2,0,1:T(8,128)(2,1)S(1)} %get-tuple-element.165), channel_id=1, source_target_pairs={{0,4},{2,6},{4,0},{6,2},{8,12},{10,14},{12,8},{14,10},{16,20},{18,... | collective-permute-start | bytes 737288 | tf_op jit(solution)/shard_map/ppermute | solution.py:27
  35.0 9.4 %collective-permute-start.4 = (bf16[2,128,768]{2,1,0:T(8,128)(2,1)S(1)}, bf16[2,128,768]{2,1,0:T(8,128)(2,1)S(1)}, u32[]{:S(2)}, u32[]{:S(2)}) collective-permute-start(bf16[2,128,768]{2,1,0:T(8,128)(2,1)S(1)} %slice_select_fusion.1), channel_id=1, source_target_pairs={{0,1},{1,0},{2,3},{3,2},{4,5},{5,4},{6,7},{7,6},{8,9},{9,8},{10,11... | collective-permute-start | bytes 1179656 | tf_op jit(solution)/shard_map/ppermute | solution.py:27
  44.4 10.7 %collective-permute-start.5 = (bf16[2,2,48,640]{3,2,0,1:T(8,128)(2,1)S(1)}, bf16[2,2,48,640]{3,2,0,1:T(8,128)(2,1)S(1)}, u32[]{:S(2)}, u32[]{:S(2)}) collective-permute-start(bf16[2,2,48,640]{3,2,0,1:T(8,128)(2,1)S(1)} %get-tuple-element.59), channel_id=1, source_target_pairs={{0,1},{1,0},{2,3},{3,2},{4,5},{5,4},{6,7},{7,6},{8,9},{9,8},{10,11... | collective-permute-start | bytes 737288 | tf_op jit(solution)/shard_map/ppermute | solution.py:27
  55.2 10.9 %collective-permute-start.6 = (bf16[2,2,48,1280]{3,2,0,1:T(8,128)(2,1)S(1)}, bf16[2,2,48,1280]{3,2,0,1:T(8,128)(2,1)S(1)}, u32[]{:S(2)}, u32[]{:S(2)}) collective-permute-start(bf16[2,2,48,1280]{3,2,0,1:T(8,128)(2,1)S(1)} %pad_maximum_fusion.3), channel_id=1, source_target_pairs={{0,4},{2,6},{4,0},{6,2},{8,12},{10,14},{12,8},{14,10},{16,20},{18,... | collective-permute-start | bytes 1474568 | tf_op jit(solution)/shard_map/ppermute | solution.py:27
  56.1 11.0 %collective-permute-start.8 = (bf16[2,2,2,48,640]{4,3,0,1,2:T(8,128)(2,1)}, bf16[2,2,2,48,640]{4,3,0,1,2:T(8,128)(2,1)S(1)}, u32[]{:S(2)}, u32[]{:S(2)}) collective-permute-start(bf16[2,2,2,48,640]{4,3,0,1,2:T(8,128)(2,1)} %pad_maximum_fusion.2), channel_id=1, source_target_pairs={{0,1},{1,0},{2,3},{3,2},{4,5},{5,4},{6,7},{7,6},{8,9},{9,8},{10,11... | collective-permute-start | bytes 1474568 | tf_op jit(solution)/shard_map/ppermute | solution.py:27
  66.4 2.9 collective-permute-start.7
  68.5 4.2 %collective-permute-start.9 = (bf16[8,48,1280]{2,1,0:T(8,128)(2,1)S(1)}, bf16[8,48,1280]{2,1,0:T(8,128)(2,1)}, u32[]{:S(2)}, u32[]{:S(2)}) collective-permute-start(bf16[8,48,1280]{2,1,0:T(8,128)(2,1)S(1)} %bitcast.225), channel_id=1, source_target_pairs={{0,2},{2,0},{4,6},{6,4},{8,10},{10,8},{12,14},{14,12},{16,18},{18,... | collective-permute-start | bytes 2949128 | tf_op jit(solution)/shard_map/ppermute | solution.py:27
  71.3 132.2 %copy-start.6 = (f32[1,768]{1,0:T(1,128)}, f32[1,768]{1,0:T(1,128)S(1)}, u32[]{:S(2)}) copy-start(f32[1,768]{1,0:T(1,128)S(1)} %get-tuple-element.178.gain_ref) | copy-start | bytes 9220
  103.5 48.4 %copy-start.16 = (s32[512]{0:T(512)S(1)}, s32[512]{0:T(512)}, u32[]{:S(2)}) copy-start(s32[512]{0:T(512)} %copy-done.15) | copy-start | bytes 6148
  103.5 51.3 %copy-start.18 = (bf16[2,512,768]{2,1,0:T(8,128)(2,1)S(1)}, bf16[2,512,768]{2,1,0:T(8,128)(2,1)}, u32[]{:S(2)}) copy-start(bf16[2,512,768]{2,1,0:T(8,128)(2,1)} %get-tuple-element.62) | copy-start | bytes 4718596
  151.6 8.3 %collective-permute-start.10 = (bf16[2304,1024]{1,0:T(8,128)(2,1)}, bf16[2304,1024]{1,0:T(8,128)(2,1)}, u32[]{:S(2)}, u32[]{:S(2)}) collective-permute-start(bf16[2304,1024]{1,0:T(8,128)(2,1)} %bitcast.263), channel_id=1, source_target_pairs={{0,2},{2,0},{4,6},{6,4},{8,10},{10,8},{12,14},{14,12},{16,18},{18,... | collective-permute-start | bytes 14155784 | tf_op jit(solution)/shard_map/ppermute | solution.py:103
  153.2 11.3 %collective-permute-start.11 = (bf16[2,128,768]{2,1,0:T(8,128)(2,1)S(1)}, bf16[2,128,768]{2,1,0:T(8,128)(2,1)S(1)}, u32[]{:S(2)}, u32[]{:S(2)}) collective-permute-start(bf16[2,128,768]{2,1,0:T(8,128)(2,1)S(1)} %slice_select_fusion), channel_id=1, source_target_pairs={{0,1},{1,0},{2,3},{3,2},{4,5},{5,4},{6,7},{7,6},{8,9},{9,8},{10,11... | collective-permute-start | bytes 1179656 | tf_op jit(solution)/shard_map/ppermute | solution.py:27
  164.5 49.8 %collective-permute-start.12 = (bf16[576,1024]{1,0:T(8,128)(2,1)S(1)}, bf16[576,1024]{1,0:T(8,128)(2,1)}, u32[]{:S(2)}, u32[]{:S(2)}) collective-permute-start(bf16[576,1024]{1,0:T(8,128)(2,1)S(1)} %bitcast.253), channel_id=1, source_target_pairs={{0,1},{1,0},{2,3},{3,2},{4,5},{5,4},{6,7},{7,6},{8,9},{9,8},{10,11... | collective-permute-start | bytes 3538952 | tf_op jit(solution)/shard_map/ppermute | solution.py:103
  166.0 48.3 %collective-permute-start.13 = (bf16[576,1024]{1,0:T(8,128)(2,1)S(1)}, bf16[576,1024]{1,0:T(8,128)(2,1)}, u32[]{:S(2)}, u32[]{:S(2)}) collective-permute-start(bf16[576,1024]{1,0:T(8,128)(2,1)S(1)} %bitcast.252), channel_id=1, source_target_pairs={{0,4},{2,6},{4,0},{6,2},{8,12},{10,14},{12,8},{14,10},{16,20},{18,... | collective-permute-start | bytes 3538952 | tf_op jit(solution)/shard_map/ppermute | solution.py:103
  166.7 52.1 %collective-permute-start.14 = (bf16[576,1024]{1,0:T(8,128)(2,1)S(1)}, bf16[576,1024]{1,0:T(8,128)(2,1)}, u32[]{:S(2)}, u32[]{:S(2)}) collective-permute-start(bf16[576,1024]{1,0:T(8,128)(2,1)S(1)} %bitcast.251), channel_id=1, source_target_pairs={{0,5},{1,4},{2,7},{3,6},{4,1},{5,0},{6,3},{7,2},{8,13},{9,12},{10,... | collective-permute-start | bytes 3538952 | tf_op jit(solution)/shard_map/ppermute | solution.py:103
  168.0 35.5 %copy-start.2 = (bf16[768,1280]{1,0:T(8,128)(2,1)S(1)}, bf16[768,1280]{1,0:T(8,128)(2,1)}, u32[]{:S(2)}) copy-start(bf16[768,1280]{1,0:T(8,128)(2,1)} %get-tuple-element.77.wa_ref) | copy-start | bytes 5898244
  218.9 5.2 %collective-permute-start.15 = (bf16[768,1664]{1,0:T(8,128)(2,1)}, bf16[768,1664]{1,0:T(8,128)(2,1)}, u32[]{:S(2)}, u32[]{:S(2)}) collective-permute-start(bf16[768,1664]{1,0:T(8,128)(2,1)} %bitcast.264), channel_id=1, source_target_pairs={{0,2},{2,0},{4,6},{6,4},{8,10},{10,8},{12,14},{14,12},{16,18},{18,... | collective-permute-start | bytes 7667720 | tf_op jit(solution)/shard_map/ppermute | solution.py:103
  227.4 19.0 %collective-permute-start.17 = (bf16[384,896]{1,0:T(8,128)(2,1)S(1)}, bf16[384,896]{1,0:T(8,128)(2,1)}, u32[]{:S(2)}, u32[]{:S(2)}) collective-permute-start(bf16[384,896]{1,0:T(8,128)(2,1)S(1)} %bitcast.254), channel_id=1, source_target_pairs={{0,1},{1,0},{2,3},{3,2},{4,5},{5,4},{6,7},{7,6},{8,9},{9,8},{10,11... | collective-permute-start | bytes 2064392 | tf_op jit(solution)/shard_map/ppermute | solution.py:103
  228.7 17.7 %collective-permute-start.16 = (bf16[384,768]{1,0:T(8,128)(2,1)}, bf16[384,768]{1,0:T(8,128)(2,1)}, u32[]{:S(2)}, u32[]{:S(2)}) collective-permute-start(bf16[384,768]{1,0:T(8,128)(2,1)} %bitcast.57), channel_id=1, source_target_pairs={{0,4},{2,6},{4,0},{6,2},{8,12},{10,14},{12,8},{14,10},{16,20},{18,... | collective-permute-start | bytes 1769480 | tf_op jit(solution)/shard_map/ppermute | solution.py:103
  229.5 21.5 %collective-permute-start.18 = (bf16[144,1024]{1,0:T(8,128)(2,1)}, bf16[144,1024]{1,0:T(8,128)(2,1)S(1)}, u32[]{:S(2)}, u32[]{:S(2)}) collective-permute-start(bf16[144,1024]{1,0:T(8,128)(2,1)} %bitcast.65), channel_id=1, source_target_pairs={{0,8},{2,10},{4,12},{6,14},{8,0},{10,2},{12,4},{14,6},{16,24},{18,... | collective-permute-start | bytes 884744 | tf_op jit(solution)/shard_map/ppermute | solution.py:103
  231.9 23.8 %collective-permute-start.19 = (bf16[144,1024]{1,0:T(8,128)(2,1)}, bf16[144,1024]{1,0:T(8,128)(2,1)}, u32[]{:S(2)}, u32[]{:S(2)}) collective-permute-start(bf16[144,1024]{1,0:T(8,128)(2,1)} %bitcast.67), channel_id=1, source_target_pairs={{0,16},{2,18},{4,20},{6,22},{8,24},{10,26},{12,28},{14,30},{16,0},... | collective-permute-start | bytes 884744 | tf_op jit(solution)/shard_map/ppermute | solution.py:103
  232.9 22.8 %collective-permute-start.20 = (bf16[144,1024]{1,0:T(8,128)(2,1)}, bf16[144,1024]{1,0:T(8,128)(2,1)}, u32[]{:S(2)}, u32[]{:S(2)}) collective-permute-start(bf16[144,1024]{1,0:T(8,128)(2,1)} %bitcast.69), channel_id=1, source_target_pairs={{0,24},{2,26},{4,28},{6,30},{8,16},{10,18},{12,20},{14,22},{16,8},... | collective-permute-start | bytes 884744 | tf_op jit(solution)/shard_map/ppermute | solution.py:103
  247.5 10.6 %collective-permute-start.22 = (bf16[192,896]{1,0:T(8,128)(2,1)S(1)}, bf16[192,896]{1,0:T(8,128)(2,1)S(1)}, u32[]{:S(2)}, u32[]{:S(2)}) collective-permute-start(bf16[192,896]{1,0:T(8,128)(2,1)S(1)} %fusion.4), channel_id=1, source_target_pairs={{0,4},{2,6},{4,0},{6,2},{8,12},{10,14},{12,8},{14,10},{16,20},{18,... | collective-permute-start | bytes 1032200 | tf_op jit(solution)/shard_map/ppermute | solution.py:103
  250.2 7.9 %collective-permute-start.21 = (bf16[192,768]{1,0:T(8,128)(2,1)}, bf16[192,768]{1,0:T(8,128)(2,1)}, u32[]{:S(2)}, u32[]{:S(2)}) collective-permute-start(bf16[192,768]{1,0:T(8,128)(2,1)} %fusion.9), channel_id=1, source_target_pairs={{0,1},{1,0},{2,3},{3,2},{4,5},{5,4},{6,7},{7,6},{8,9},{9,8},{10,11... | collective-permute-start | bytes 884744 | tf_op jit(solution)/shard_map/ppermute | solution.py:103
  260.7 8.1 %collective-permute-start.23 = (bf16[48,1664]{1,0:T(8,128)(2,1)S(1)}, bf16[48,1664]{1,0:T(8,128)(2,1)S(1)}, u32[]{:S(2)}, u32[]{:S(2)}) collective-permute-start(bf16[48,1664]{1,0:T(8,128)(2,1)S(1)} %pad_maximum_fusion.7), channel_id=1, source_target_pairs={{0,8},{2,10},{4,12},{6,14},{8,0},{10,2},{12,4},{14,6},{16,24},{18,... | collective-permute-start | bytes 479240 | tf_op jit(solution)/shard_map/ppermute | solution.py:103
  263.6 13.6 %collective-permute-start.24 = (bf16[48,1664]{1,0:T(8,128)(2,1)S(1)}, bf16[48,1664]{1,0:T(8,128)(2,1)S(1)}, u32[]{:S(2)}, u32[]{:S(2)}) collective-permute-start(bf16[48,1664]{1,0:T(8,128)(2,1)S(1)} %pad_maximum_fusion.8), channel_id=1, source_target_pairs={{0,16},{2,18},{4,20},{6,22},{8,24},{10,26},{12,28},{14,30},{16,0},... | collective-permute-start | bytes 479240 | tf_op jit(solution)/shard_map/ppermute | solution.py:103
  264.5 12.7 %collective-permute-start.25 = (bf16[48,1664]{1,0:T(8,128)(2,1)S(1)}, bf16[48,1664]{1,0:T(8,128)(2,1)S(1)}, u32[]{:S(2)}, u32[]{:S(2)}) collective-permute-start(bf16[48,1664]{1,0:T(8,128)(2,1)S(1)} %pad_maximum_fusion.9), channel_id=1, source_target_pairs={{0,24},{2,26},{4,28},{6,30},{8,16},{10,18},{12,20},{14,22},{16,8},... | collective-permute-start | bytes 479240 | tf_op jit(solution)/shard_map/ppermute | solution.py:103
  (18 other events, 225.0 us)
Sparse Core Ops, SparseCore 0:
  10.9 92.5 all-gather.1

commit v3 on v2

--- a/solution.py
+++ b/solution.py
@@ -12,7 +12,7 @@
 HIGHEST_PREC = lax.Precision.HIGHEST
 BLOCK = 128
 LANES = 128
-FEED_CHUNK = 1024
+FEED_CHUNK = 512
 EDGE_CHUNK = 256
 BF = jnp.bfloat16
 F32 = jnp.float32
@@ -64,13 +64,18 @@
 def gather_halves(piece, cut, before_last):
     far, orders, _ = stage_groups()
     have = []
-    for stage in far:
+    bias, halo = before_last
+    for index, stage in enumerate(far):
+        if index == len(far) - 1:
+            (piece,), (halo,) = tie([piece], [halo])
         piece, have = merge(piece, have, stage)
+    (piece,), (bias,) = tie([piece], [bias])
+    before_last = (bias, halo)
     halves = [(piece[..., :cut], have), (piece[..., cut:], have)]
     for step in range(len(orders[0])):
         done = merge(*halves[0], orders[0][step])
         if step == 0:
-            (value, first), before_last = tie([halves[1][0], done[0]], before_last)
+            (value,), (first,) = tie([halves[1][0]], [done[0]])
             halves[1], done = (value, halves[1][1]), (first, done[1])
         halves = [done, merge(*halves[1], orders[1][step])]
     shape = (-1, piece.shape[-2])
@@ -663,7 +668,6 @@
     hid_s,
     gg_s,
     gu_s,
-    gn2_s,
 ):
     tokens, width = x_ref.shape
     step = pl.program_id(0) * pl.num_programs(1) + pl.program_id(1)
@@ -694,25 +698,29 @@
             n2_s[place, :] = normed
             n2t_s[:, place] = normed.T
             cott_s[:, place] = cot_ref[place, :].T
-            gn2_s[place, :] = jnp.zeros((edge, width), F32)
+            gmid_ref[place, :] = jnp.zeros((edge, width), F32)
 
         for_chunks(work, edge)
 
-    def work(place):
-        n2, cot = n2_s[place, :], cot_ref[place, :]
-        act, slope = gelu_parts(dot_nn(n2, wg_ref[...]))
-        up = dot_nn(n2, wu_ref[...])
-        grad_hidden = dot_nn(cot, wd_ref[...])
-        hidden = (act * up).astype(BF)
-        grad_gate = (grad_hidden * up * slope).astype(BF)
-        grad_up = (grad_hidden * act).astype(BF)
-        hid_s[place, :] = hidden
-        gg_s[place, :] = grad_gate
-        gu_s[place, :] = grad_up
+    places = [pl.ds(at, chunk) for at in range(0, tokens, chunk)]
+    products = [
+        (
+            dot_nn(n2_s[place, :], wg_ref[...]),
+            dot_nn(n2_s[place, :], wu_ref[...]),
+            dot_nn(cot_ref[place, :], wd_ref[...]),
+        )
+        for place in places
+    ]
+    lows = []
+    for place, (gate, up, grad_hidden) in zip(places, products):
+        act, slope = gelu_parts(gate)
+        low = (act * up, grad_hidden * up * slope, grad_hidden * act)
+        lows.append([value.astype(BF) for value in low])
+        for ref, value in zip((hid_s, gg_s, gu_s), lows[-1]):
+            ref[place, :] = value
+    for place, (hidden, grad_gate, grad_up) in zip(places, lows):
         out_ref[place, :] += dot_nt(hidden, wd_ref[...])
-        gn2_s[place, :] += dot_nt(grad_gate, wg_ref[...]) + dot_nt(grad_up, wu_ref[...])
-
-    for_chunks(work, chunk)
+        gmid_ref[place, :] += dot_nt(grad_gate, wg_ref[...]) + dot_nt(grad_up, wu_ref[...])
 
     def store(kind, grad):
         split_rows(core_ref[0], shard, grad.astype(BF), keep_ref, send_ref, (kind,))
@@ -726,7 +734,7 @@
         ggain_ref[...] = jnp.zeros_like(ggain_ref)
 
         def work(place):
-            middle, grad_n2 = mid_s[place, :], gn2_s[place, :]
+            middle, grad_n2 = mid_s[place, :], gmid_ref[place, :]
             r2 = inverse_rms(middle)
             ggain_ref[...] += jnp.sum(grad_n2 * middle * r2, axis=0, keepdims=True)
             scaled = grad_n2 * gain_ref[...]
@@ -791,11 +799,10 @@
                 pltpu.VMEM((tokens, wide), BF),
                 pltpu.VMEM((tokens, wide), BF),
                 pltpu.VMEM((tokens, wide), BF),
-                pltpu.VMEM((tokens, width), F32),
             ],
         ),
         compiler_params=pltpu.CompilerParams(
-            dimension_semantics=("arbitrary", "arbitrary"), vmem_limit_bytes=56 << 20
+            dimension_semantics=("arbitrary", "arbitrary"), vmem_limit_bytes=53 << 20
         ),
         cost_estimate=pl.CostEstimate(
             flops=2 * tokens * width * (18 * hidden_cols + 2 * out_cols),

time: 290 us -> 288 us (level)
  transfers between devices with their start and end apart: 27 -> 27, of which waited for: 15 -> 17; matrix products, arithmetic and copies ran while one was open for 11% -> 10% of each run, Pallas kernels for 29% -> 29%
where the time goes in v3:
time: 288 us; the launch traced here: 287 us
  Pallas kernels  131 us (45%)
  waiting for transfers between devices  63.4 us (22%)
  starting transfers between devices  32.2 us (11%)
  other arithmetic  29.3 us (10%)
  between operations  14.6 us (5%)
  local copies, waits for them, and re-layouts  11.4 us (4%)
  matrix products  4.54 us (2%)
    pallas_call x1, Pallas kernels, feed_forward(): pl.pallas_call(functools.partial(feed_kernel, min(FEED_CHUNK, tokens), sh...  46.9 us
    ppermute x11, waiting for transfers between devices, swap(): return lax.ppermute(value, axis, [(i, i ^ 1 << bit) for i in range(count)])  38 us
    pallas_call x1, Pallas kernels, attend_backward(): pl.pallas_call(functools.partial(attend_back_kernel, pairs, last, own_blo...  35.5 us
    pallas_call x1, Pallas kernels, attend_forward(): pl.pallas_call(functools.partial(attend_kernel, pairs, last), out_shape=(...  24 us
    ppermute x15, waiting for transfers between devices, swap_with(): return lax.ppermute(flat, axes, pairs).reshape(value.shape)  21.1 us
    ppermute x15, starting transfers between devices, swap_with(): return lax.ppermute(flat, axes, pairs).reshape(value.shape)  16.9 us
    ppermute x11, starting transfers between devices, swap(): return lax.ppermute(value, axis, [(i, i ^ 1 << bit) for i in range(count)])  15.3 us
    convert_element_type x8, other arithmetic, sends(): sum((t.part(self.done, flip).astype(F32) for t in self.terms)).astype(BF)  14.7 us
  transfers between devices with their start and end apart: 27, of which 17 were waited for; matrix products, arithmetic and copies ran while one was open for 10% of the time, Pallas kernels for 29%

profile of v3, /device:TPU:0, one launch (start us, length us, event | category | flops | bytes accessed | tf_op | source)
XLA Modules:
  0.0 286.7 jit_solution(6691369181289932666)
XLA Ops:
  7.3 1.8 pad_maximum_fusion.5
  10.7 4.1 %collective-permute-start = (bf16[48,1280]{1,0:T(8,128)(2,1)S(1)}, bf16[48,1280]{1,0:T(8,128)(2,1)S(1)}, u32[]{:S(2)}, u32[]{:S(2)}) collective-permute-start(bf16[48,1280]{1,0:T(8,128)(2,1)S(1)} %fusion.26), channel_id=1, source_target_pairs={{0,16},{2,18},{4,20},{6,22},{8,24},{10,26},{12,28},{14,30},{16,0},... | collective-permute-start | bytes 368648 | tf_op jit(solution)/shard_map/ppermute | solution.py:27
  16.0 1.6 collective-permute-start.1
  17.6 3.2 %collective-permute-done = bf16[48,1280]{1,0:T(8,128)(2,1)S(1)} collective-permute-done((bf16[48,1280]{1,0:T(8,128)(2,1)S(1)}, bf16[48,1280]{1,0:T(8,128)(2,1)S(1)}, u32[]{:S(2)}, u32[]{:S(2)}) %collective-permute-start) | collective-permute-done | bytes 122912 | tf_op jit(solution)/shard_map/ppermute | solution.py:27
  20.9 8.1 %collective-permute-done.1.halo_ref = bf16[2,128,768]{2,1,0:T(8,128)(2,1)S(1)} collective-permute-done((bf16[2,128,768]{2,1,0:T(8,128)(2,1)S(1)}, bf16[2,128,768]{2,1,0:T(8,128)(2,1)S(1)}, u32[]{:S(2)}, u32[]{:S(2)}) %collective-permute-start.1) | collective-permute-done | bytes 393248 | tf_op jit(solution)/shard_map/ppermute | solution.py:27
  29.0 1.6 collective-permute-start.2
  34.9 4.2 %window_bias.1.bias_ref = f32[6,384,256]{2,1,0:T(8,128)} custom-call(f32[12,1,512]{2,1,0:T(1,128)} %broadcast_in_dim.19.turned_ref), custom_call_target="tpu_custom_call" | custom-call | tf_op jit(solution)/shard_map/window_bias/pallas_call | solution.py:613
  39.3 1.6 collective-permute-start.4
  40.9 6.1 %collective-permute-done.4 = bf16[2,2,48,640]{3,2,0,1:T(8,128)(2,1)S(1)} collective-permute-done((bf16[2,2,48,640]{3,2,0,1:T(8,128)(2,1)S(1)}, bf16[2,2,48,640]{3,2,0,1:T(8,128)(2,1)S(1)}, u32[]{:S(2)}, u32[]{:S(2)}) %collective-permute-start.4) | collective-permute-done | bytes 245792 | tf_op jit(solution)/shard_map/ppermute | solution.py:27
  48.9 6.6 %collective-permute-done.5 = bf16[2,2,48,640]{3,2,0,1:T(8,128)(2,1)S(1)} collective-permute-done((bf16[2,2,48,640]{3,2,0,1:T(8,128)(2,1)S(1)}, bf16[2,2,48,640]{3,2,0,1:T(8,128)(2,1)S(1)}, u32[]{:S(2)}, u32[]{:S(2)}) %collective-permute-start.5) | collective-permute-done | bytes 245792 | tf_op jit(solution)/shard_map/ppermute | solution.py:27
  57.8 9.3 %collective-permute-done.6 = bf16[2,2,48,1280]{3,2,0,1:T(8,128)(2,1)S(1)} collective-permute-done((bf16[2,2,48,1280]{3,2,0,1:T(8,128)(2,1)S(1)}, bf16[2,2,48,1280]{3,2,0,1:T(8,128)(2,1)S(1)}, u32[]{:S(2)}, u32[]{:S(2)}) %collective-permute-start.6) | collective-permute-done | bytes 491552 | tf_op jit(solution)/shard_map/ppermute | solution.py:27
  76.3 24.0 %attend_forward.1 = (bf16[2,512,768]{2,1,0:T(8,128)(2,1)}, bf16[2,640,2304]{2,1,0:T(8,128)(2,1)}, bf16[2,768,512]{2,1,0:T(8,128)(2,1)}, bf16[768,1280]{1,0:T(8,128)(2,1)}, bf16[768,1280]{1,0:T(8,128)(2,1)}) custom-call(s32[2]{0:T(128)S(1)} %pad_add_fusion.shift_ref, bf16[2,512,768]{2,1,0:T(8,128)(2,1)} %bitcast.239, ...), custom_call_target="tpu_custom_call" | custom-call | flops 6945767424 | bytes 15728640 | tf_op jit(solution)/shard_map/attend_forward/pallas_call | solution.py:372
  100.3 4.2 %all-gather.2.cloned.1.call-done.wo0_ref.wo1_ref.wg_ref.wu_ref.wd_ref = bf16[1536,3456]{1,0:T(8,128)(2,1)} async-done(((bf16[48,3456]{1,0:T(8,128)(2,1)}), bf16[1536,3456]{1,0:T(8,128)(2,1)}) %all-gather.2.cloned.1.call-update) | async-done | bytes 10616848 | tf_op jit(solution)/shard_map/all_gather | solution.py:992
  104.5 46.9 %feed_forward.1 = (f32[1024,768]{1,0:T(8,128)}, f32[1024,768]{1,0:T(8,128)}, bf16[1024,768]{1,0:T(8,128)(2,1)}, f32[1,768]{1,0:T(1,128)S(1)}, bf16[2,8,3,48,1024...) custom-call(s32[1]{0:T(128)} %bitcast.core_ref, bf16[1024,768]{1,0:T(8,128)(2,1)} %bitcast.269, ...), custom_call_target="tpu_custom_call" | custom-call | flops 30198988800 | bytes 32636928 | tf_op jit(solution)/shard_map/feed_forward/pallas_call | solution.py:760
  152.9 1.6 collective-permute-start.11
  154.5 3.0 %convolution_convert_fusion.1.gout_ref = bf16[768,768]{1,0:T(8,128)(2,1)S(1)} fusion(bf16[1024,768]{1,0:T(8,128)(2,1)} %get-tuple-element.70, bf16[1024,768]{1,0:T(8,128)(2,1)S(1)} %bitcast.270), kind=kOutput, calls=%fused_computation.4 | convolution fusion | flops 1208549376 | bytes 4325376 | tf_op jit(solution)/shard_map/dot_general | solution.py:243
  159.9 3.9 %fusion.2 = (bf16[2,2,3,48,1024]{4,3,2,1,0:T(8,128)(2,1)S(1)}, bf16[2,2,3,48,1024]{4,3,2,1,0:T(8,128)(2,1)S(1)}, bf16[2,2,3,48,1024]{4,3,2,1,0:T(8,128)(2,1)S(1)}) fusion(bf16[2,2,2,2,3,48,1024]{6,5,4,3,2,1,0:T(8,128)(2,1)} %bitcast.27, s32[]{:T(128)S(6)} %select_n.154, s32[]{:T(128)S(6)} %select_n.155, bf16[2,2,2,2,3,48,1024]{6,5,4,3,2,1,0:T(8,128)(2,1)S(1)} %bitcast.237, ...), kind=kLoop, calls=%fused_computation.8 | loop fusion | flops 7077888 | bytes 10616848 | tf_op jit(solution)/shard_map/convert_element_type | solution.py:142
  164.3 1.5 collective-permute-start.12
  167.8 35.5 %attend_backward.1 = (bf16[2,512,2304]{2,1,0:T(8,128)(2,1)}, f32[12,1,512]{2,1,0:T(1,128)S(1)}) custom-call(s32[1]{0:T(128)} %bitcast.1.shift_ref, bf16[2,640,2304]{2,1,0:T(8,128)(2,1)S(1)} %bitcast.230, bf16[2,512,768]{2,1,0:T(8,128)(2,1)S(1)} %bitcast.228, bf16[2,128,768]{2,1,0:T(8,128)(2,1)S(1)} %collective-permute-done.11.halo_ref, ...), custom_call_target="tpu_custom_call" | custom-call | flops 45600473088 | bytes 16908288 | tf_op jit(solution)/shard_map/attend_backward/pallas_call | solution.py:526
  203.3 10.8 %weight_gradients.1 = (bf16[2,8,48,1664]{3,2,1,0:T(8,128)(2,1)}, bf16[2,8,48,1664]{3,2,1,0:T(8,128)(2,1)}) custom-call(s32[1]{0:T(128)} %bitcast.core_ref, bf16[2,768,512]{2,1,0:T(8,128)(2,1)S(1)} %copy-done.5, bf16[1024,2304]{1,0:T(8,128)(2,1)} %bitcast.231, bf16[768,768]{1,0:T(8,128)(2,1)S(1)} %convolution_convert_fusion.1.gout_ref, ...), custom_call_target="tpu_custom_call" | custom-call | flops 786432 | bytes 1024 | tf_op jit(solution)/shard_map/weight_gradients/pallas_call | solution.py:911
  214.0 4.4 %collective-permute-done.14 = bf16[576,1024]{1,0:T(8,128)(2,1)} collective-permute-done((bf16[576,1024]{1,0:T(8,128)(2,1)S(1)}, bf16[576,1024]{1,0:T(8,128)(2,1)}, u32[]{:S(2)}, u32[]{:S(2)}) %collective-permute-start.14) | collective-permute-done | bytes 1179680 | tf_op jit(solution)/shard_map/ppermute | solution.py:108
  218.4 4.0 %fusion.10 = (bf16[3,48,1024]{2,1,0:T(8,128)(2,1)}, bf16[3,48,1024]{2,1,0:T(8,128)(2,1)}, bf16[3,48,1024]{2,1,0:T(8,128)(2,1)}) fusion(bf16[2,2,3,48,1024]{4,3,2,1,0:T(8,128)(2,1)} %bitcast.39, s32[]{:T(128)S(6)} %select_n.157, s32[]{:T(128)S(6)} %select_n.152, bf16[2,2,3,48,1024]{4,3,2,1,0:T(8,128)(2,1)} %bitcast.37, ...), kind=kLoop, calls=%fused_computation.26 | loop fusion | flops 4423680 | bytes 5308440 | tf_op jit(solution)/shard_map/convert_element_type | solution.py:142
  224.8 2.1 fusion.5
  226.9 1.6 collective-permute-start.17
  231.3 2.0 collective-permute-start.20
  233.3 10.0 %input_gradient.1 = f32[1024,768]{1,0:T(8,128)} custom-call(bf16[1024,2304]{1,0:T(8,128)(2,1)} %bitcast.232, bf16[768,1280]{1,0:T(8,128)(2,1)} %get-tuple-element.81.wa_ref, bf16[768,1280]{1,0:T(8,128)(2,1)} %get-tuple-element.82.wb_ref, bf16[1024,768]{1,0:T(8,128)(2,1)} %bitcast.241, f32[1,768]{1,0:T(1,128)} %copy-done.6, ...), custom_call_target="tpu_custom_call" | custom-call | flops 786432 | bytes 1024 | tf_op jit(solution)/shard_map/input_gradient/pallas_call | solution.py:581
  246.6 1.6 collective-permute-start.22
  250.5 3.5 %collective-permute-done.19 = bf16[144,1024]{1,0:T(8,128)(2,1)} collective-permute-done((bf16[144,1024]{1,0:T(8,128)(2,1)}, bf16[144,1024]{1,0:T(8,128)(2,1)}, u32[]{:S(2)}, u32[]{:S(2)}) %collective-permute-start.19) | collective-permute-done | bytes 294944 | tf_op jit(solution)/shard_map/ppermute | solution.py:108
  253.9 3.7 %collective-permute-done.21 = bf16[192,768]{1,0:T(8,128)(2,1)} collective-permute-done((bf16[192,768]{1,0:T(8,128)(2,1)}, bf16[192,768]{1,0:T(8,128)(2,1)}, u32[]{:S(2)}, u32[]{:S(2)}) %collective-permute-start.21) | collective-permute-done | bytes 294944 | tf_op jit(solution)/shard_map/ppermute | solution.py:108
  262.7 2.1 collective-permute-start.25
  264.9 1.9 fusion.8
  267.6 7.7 %collective-permute-done.24 = bf16[48,1664]{1,0:T(8,128)(2,1)S(1)} collective-permute-done((bf16[48,1664]{1,0:T(8,128)(2,1)S(1)}, bf16[48,1664]{1,0:T(8,128)(2,1)S(1)}, u32[]{:S(2)}, u32[]{:S(2)}) %collective-permute-start.24) | collective-permute-done | bytes 159776 | tf_op jit(solution)/shard_map/ppermute | solution.py:108
  (146 shorter events, 47.9 us)
Async XLA Ops:
  7.2 62.4 %copy-start = (s32[2,1,1024]{2,1,0:T(1,128)S(1)}, s32[2,1,1024]{2,1,0:T(1,128)}, u32[]{:S(2)}) copy-start(s32[2,1,1024]{2,1,0:T(1,128)} %param.15) | copy-start | bytes 24580
  7.2 97.3 %all-gather.2.cloned.1.call-start = ((), (), s32[]{:S(2)}) async-start(), calls=%async_computation | async-start | bytes 10948608 | tf_op jit(solution)/shard_map/all_gather | solution.py:992
  10.7 10.1 %collective-permute-start = (bf16[48,1280]{1,0:T(8,128)(2,1)S(1)}, bf16[48,1280]{1,0:T(8,128)(2,1)S(1)}, u32[]{:S(2)}, u32[]{:S(2)}) collective-permute-start(bf16[48,1280]{1,0:T(8,128)(2,1)S(1)} %fusion.26), channel_id=1, source_target_pairs={{0,16},{2,18},{4,20},{6,22},{8,24},{10,26},{12,28},{14,30},{16,0},... | collective-permute-start | bytes 368648 | tf_op jit(solution)/shard_map/ppermute | solution.py:27
  16.0 13.0 %collective-permute-start.1 = (bf16[2,128,768]{2,1,0:T(8,128)(2,1)S(1)}, bf16[2,128,768]{2,1,0:T(8,128)(2,1)S(1)}, u32[]{:S(2)}, u32[]{:S(2)}) collective-permute-start(bf16[2,128,768]{2,1,0:T(8,128)(2,1)S(1)} %slice_select_fusion.1), channel_id=1, source_target_pairs={{0,1},{1,0},{2,3},{3,2},{4,5},{5,4},{6,7},{7,6},{8,9},{9,8},{10,11... | collective-permute-start | bytes 1179656 | tf_op jit(solution)/shard_map/ppermute | solution.py:27
  29.0 10.2 %collective-permute-start.2 = (bf16[2,48,1280]{2,1,0:T(8,128)(2,1)S(1)}, bf16[2,48,1280]{2,1,0:T(8,128)(2,1)S(1)}, u32[]{:S(2)}, u32[]{:S(2)}) collective-permute-start(bf16[2,48,1280]{2,1,0:T(8,128)(2,1)S(1)} %pad_maximum_fusion.6), channel_id=1, source_target_pairs={{0,8},{2,10},{4,12},{6,14},{8,0},{10,2},{12,4},{14,6},{16,24},{18,... | collective-permute-start | bytes 737288 | tf_op jit(solution)/shard_map/ppermute | solution.py:27
  30.6 3.6 %collective-permute-start.3 = (f32[32,6]{0,1:T(8,128)S(1)}, f32[32,6]{0,1:T(8,128)S(1)}, u32[]{:S(2)}, u32[]{:S(2)}) collective-permute-start(f32[32,6]{0,1:T(8,128)S(1)} %copy-done.18), channel_id=1, source_target_pairs={{0,1},{1,0},{2,3},{3,2},{4,5},{5,4},{6,7},{7,6},{8,9},{9,8},{10,11... | collective-permute-start | bytes 2312 | tf_op jit(solution)/shard_map/ppermute | solution.py:27
  39.3 7.7 %collective-permute-start.4 = (bf16[2,2,48,640]{3,2,0,1:T(8,128)(2,1)S(1)}, bf16[2,2,48,640]{3,2,0,1:T(8,128)(2,1)S(1)}, u32[]{:S(2)}, u32[]{:S(2)}) collective-permute-start(bf16[2,2,48,640]{3,2,0,1:T(8,128)(2,1)S(1)} %slice.71), channel_id=1, source_target_pairs={{0,4},{2,6},{4,0},{6,2},{8,12},{10,14},{12,8},{14,10},{16,20},{18,... | collective-permute-start | bytes 737288 | tf_op jit(solution)/shard_map/ppermute | solution.py:27
  48.0 7.6 %collective-permute-start.5 = (bf16[2,2,48,640]{3,2,0,1:T(8,128)(2,1)S(1)}, bf16[2,2,48,640]{3,2,0,1:T(8,128)(2,1)S(1)}, u32[]{:S(2)}, u32[]{:S(2)}) collective-permute-start(bf16[2,2,48,640]{3,2,0,1:T(8,128)(2,1)S(1)} %get-tuple-element.63), channel_id=1, source_target_pairs={{0,1},{1,0},{2,3},{3,2},{4,5},{5,4},{6,7},{7,6},{8,9},{9,8},{10,11... | collective-permute-start | bytes 737288 | tf_op jit(solution)/shard_map/ppermute | solution.py:27
  55.6 11.5 %collective-permute-start.6 = (bf16[2,2,48,1280]{3,2,0,1:T(8,128)(2,1)S(1)}, bf16[2,2,48,1280]{3,2,0,1:T(8,128)(2,1)S(1)}, u32[]{:S(2)}, u32[]{:S(2)}) collective-permute-start(bf16[2,2,48,1280]{3,2,0,1:T(8,128)(2,1)S(1)} %pad_maximum_fusion.4), channel_id=1, source_target_pairs={{0,4},{2,6},{4,0},{6,2},{8,12},{10,14},{12,8},{14,10},{16,20},{18,... | collective-permute-start | bytes 1474568 | tf_op jit(solution)/shard_map/ppermute | solution.py:27
  57.2 10.9 %collective-permute-start.8 = (bf16[2,2,2,48,640]{4,3,0,1,2:T(8,128)(2,1)}, bf16[2,2,2,48,640]{4,3,0,1,2:T(8,128)(2,1)S(1)}, u32[]{:S(2)}, u32[]{:S(2)}) collective-permute-start(bf16[2,2,2,48,640]{4,3,0,1,2:T(8,128)(2,1)} %pad_maximum_fusion.3), channel_id=1, source_target_pairs={{0,1},{1,0},{2,3},{3,2},{4,5},{5,4},{6,7},{7,6},{8,9},{9,8},{10,11... | collective-permute-start | bytes 1474568 | tf_op jit(solution)/shard_map/ppermute | solution.py:27
  67.5 4.4 %collective-permute-start.7 = (bf16[8,48,1280]{2,1,0:T(8,128)(2,1)S(1)}, bf16[8,48,1280]{2,1,0:T(8,128)(2,1)S(1)}, u32[]{:S(2)}, u32[]{:S(2)}) collective-permute-start(bf16[8,48,1280]{2,1,0:T(8,128)(2,1)S(1)} %bitcast.222), channel_id=1, source_target_pairs={{0,2},{2,0},{4,6},{6,4},{8,10},{10,8},{12,14},{14,12},{16,18},{18,... | collective-permute-start | bytes 2949128 | tf_op jit(solution)/shard_map/ppermute | solution.py:27
  69.5 4.5 %collective-permute-start.9 = (bf16[8,48,1280]{2,1,0:T(8,128)(2,1)S(1)}, bf16[8,48,1280]{2,1,0:T(8,128)(2,1)}, u32[]{:S(2)}, u32[]{:S(2)}) collective-permute-start(bf16[8,48,1280]{2,1,0:T(8,128)(2,1)S(1)} %bitcast.225), channel_id=1, source_target_pairs={{0,2},{2,0},{4,6},{6,4},{8,10},{10,8},{12,14},{14,12},{16,18},{18,... | collective-permute-start | bytes 2949128 | tf_op jit(solution)/shard_map/ppermute | solution.py:27
  73.2 130.0 %copy-start.6 = (f32[1,768]{1,0:T(1,128)}, f32[1,768]{1,0:T(1,128)S(1)}, u32[]{:S(2)}) copy-start(f32[1,768]{1,0:T(1,128)S(1)} %get-tuple-element.181.gain_ref) | copy-start | bytes 9220
  104.5 47.2 %copy-start.17 = (s32[512]{0:T(512)S(1)}, s32[512]{0:T(512)}, u32[]{:S(2)}) copy-start(s32[512]{0:T(512)} %copy-done.16) | copy-start | bytes 6148
  104.5 50.0 %copy-start.19 = (bf16[2,512,768]{2,1,0:T(8,128)(2,1)S(1)}, bf16[2,512,768]{2,1,0:T(8,128)(2,1)}, u32[]{:S(2)}) copy-start(bf16[2,512,768]{2,1,0:T(8,128)(2,1)} %get-tuple-element.66) | copy-start | bytes 4718596
  151.4 8.3 %collective-permute-start.10 = (bf16[2304,1024]{1,0:T(8,128)(2,1)}, bf16[2304,1024]{1,0:T(8,128)(2,1)}, u32[]{:S(2)}, u32[]{:S(2)}) collective-permute-start(bf16[2304,1024]{1,0:T(8,128)(2,1)} %bitcast.263), channel_id=1, source_target_pairs={{0,2},{2,0},{4,6},{6,4},{8,10},{10,8},{12,14},{14,12},{16,18},{18,... | collective-permute-start | bytes 14155784 | tf_op jit(solution)/shard_map/ppermute | solution.py:108
  152.9 11.3 %collective-permute-start.11 = (bf16[2,128,768]{2,1,0:T(8,128)(2,1)S(1)}, bf16[2,128,768]{2,1,0:T(8,128)(2,1)S(1)}, u32[]{:S(2)}, u32[]{:S(2)}) collective-permute-start(bf16[2,128,768]{2,1,0:T(8,128)(2,1)S(1)} %slice_select_fusion), channel_id=1, source_target_pairs={{0,1},{1,0},{2,3},{3,2},{4,5},{5,4},{6,7},{7,6},{8,9},{9,8},{10,11... | collective-permute-start | bytes 1179656 | tf_op jit(solution)/shard_map/ppermute | solution.py:27
  164.3 49.8 %collective-permute-start.12 = (bf16[576,1024]{1,0:T(8,128)(2,1)S(1)}, bf16[576,1024]{1,0:T(8,128)(2,1)}, u32[]{:S(2)}, u32[]{:S(2)}) collective-permute-start(bf16[576,1024]{1,0:T(8,128)(2,1)S(1)} %bitcast.253), channel_id=1, source_target_pairs={{0,1},{1,0},{2,3},{3,2},{4,5},{5,4},{6,7},{7,6},{8,9},{9,8},{10,11... | collective-permute-start | bytes 3538952 | tf_op jit(solution)/shard_map/ppermute | solution.py:108
  165.8 48.2 %collective-permute-start.13 = (bf16[576,1024]{1,0:T(8,128)(2,1)S(1)}, bf16[576,1024]{1,0:T(8,128)(2,1)}, u32[]{:S(2)}, u32[]{:S(2)}) collective-permute-start(bf16[576,1024]{1,0:T(8,128)(2,1)S(1)} %bitcast.252), channel_id=1, source_target_pairs={{0,4},{2,6},{4,0},{6,2},{8,12},{10,14},{12,8},{14,10},{16,20},{18,... | collective-permute-start | bytes 3538952 | tf_op jit(solution)/shard_map/ppermute | solution.py:108
  166.3 52.1 %collective-permute-start.14 = (bf16[576,1024]{1,0:T(8,128)(2,1)S(1)}, bf16[576,1024]{1,0:T(8,128)(2,1)}, u32[]{:S(2)}, u32[]{:S(2)}) collective-permute-start(bf16[576,1024]{1,0:T(8,128)(2,1)S(1)} %bitcast.251), channel_id=1, source_target_pairs={{0,5},{1,4},{2,7},{3,6},{4,1},{5,0},{6,3},{7,2},{8,13},{9,12},{10,... | collective-permute-start | bytes 3538952 | tf_op jit(solution)/shard_map/ppermute | solution.py:108
  167.8 35.5 %copy-start.2 = (bf16[768,1280]{1,0:T(8,128)(2,1)S(1)}, bf16[768,1280]{1,0:T(8,128)(2,1)}, u32[]{:S(2)}) copy-start(bf16[768,1280]{1,0:T(8,128)(2,1)} %get-tuple-element.81.wa_ref) | copy-start | bytes 5898244
  218.4 5.2 %collective-permute-start.15 = (bf16[768,1664]{1,0:T(8,128)(2,1)}, bf16[768,1664]{1,0:T(8,128)(2,1)}, u32[]{:S(2)}, u32[]{:S(2)}) collective-permute-start(bf16[768,1664]{1,0:T(8,128)(2,1)} %bitcast.264), channel_id=1, source_target_pairs={{0,2},{2,0},{4,6},{6,4},{8,10},{10,8},{12,14},{14,12},{16,18},{18,... | collective-permute-start | bytes 7667720 | tf_op jit(solution)/shard_map/ppermute | solution.py:108
  226.9 18.6 %collective-permute-start.17 = (bf16[384,896]{1,0:T(8,128)(2,1)S(1)}, bf16[384,896]{1,0:T(8,128)(2,1)}, u32[]{:S(2)}, u32[]{:S(2)}) collective-permute-start(bf16[384,896]{1,0:T(8,128)(2,1)S(1)} %bitcast.254), channel_id=1, source_target_pairs={{0,1},{1,0},{2,3},{3,2},{4,5},{5,4},{6,7},{7,6},{8,9},{9,8},{10,11... | collective-permute-start | bytes 2064392 | tf_op jit(solution)/shard_map/ppermute | solution.py:108
  228.5 17.0 %collective-permute-start.16 = (bf16[384,768]{1,0:T(8,128)(2,1)}, bf16[384,768]{1,0:T(8,128)(2,1)}, u32[]{:S(2)}, u32[]{:S(2)}) collective-permute-start(bf16[384,768]{1,0:T(8,128)(2,1)} %bitcast.57), channel_id=1, source_target_pairs={{0,4},{2,6},{4,0},{6,2},{8,12},{10,14},{12,8},{14,10},{16,20},{18,... | collective-permute-start | bytes 1769480 | tf_op jit(solution)/shard_map/ppermute | solution.py:108
  228.9 21.5 %collective-permute-start.18 = (bf16[144,1024]{1,0:T(8,128)(2,1)}, bf16[144,1024]{1,0:T(8,128)(2,1)S(1)}, u32[]{:S(2)}, u32[]{:S(2)}) collective-permute-start(bf16[144,1024]{1,0:T(8,128)(2,1)} %bitcast.65), channel_id=1, source_target_pairs={{0,8},{2,10},{4,12},{6,14},{8,0},{10,2},{12,4},{14,6},{16,24},{18,... | collective-permute-start | bytes 884744 | tf_op jit(solution)/shard_map/ppermute | solution.py:108
  230.1 23.8 %collective-permute-start.19 = (bf16[144,1024]{1,0:T(8,128)(2,1)}, bf16[144,1024]{1,0:T(8,128)(2,1)}, u32[]{:S(2)}, u32[]{:S(2)}) collective-permute-start(bf16[144,1024]{1,0:T(8,128)(2,1)} %bitcast.67), channel_id=1, source_target_pairs={{0,16},{2,18},{4,20},{6,22},{8,24},{10,26},{12,28},{14,30},{16,0},... | collective-permute-start | bytes 884744 | tf_op jit(solution)/shard_map/ppermute | solution.py:108
  231.3 22.6 %collective-permute-start.20 = (bf16[144,1024]{1,0:T(8,128)(2,1)}, bf16[144,1024]{1,0:T(8,128)(2,1)}, u32[]{:S(2)}, u32[]{:S(2)}) collective-permute-start(bf16[144,1024]{1,0:T(8,128)(2,1)} %bitcast.69), channel_id=1, source_target_pairs={{0,24},{2,26},{4,28},{6,30},{8,16},{10,18},{12,20},{14,22},{16,8},... | collective-permute-start | bytes 884744 | tf_op jit(solution)/shard_map/ppermute | solution.py:108
  246.6 11.1 %collective-permute-start.22 = (bf16[192,896]{1,0:T(8,128)(2,1)S(1)}, bf16[192,896]{1,0:T(8,128)(2,1)S(1)}, u32[]{:S(2)}, u32[]{:S(2)}) collective-permute-start(bf16[192,896]{1,0:T(8,128)(2,1)S(1)} %fusion.4), channel_id=1, source_target_pairs={{0,4},{2,6},{4,0},{6,2},{8,12},{10,14},{12,8},{14,10},{16,20},{18,... | collective-permute-start | bytes 1032200 | tf_op jit(solution)/shard_map/ppermute | solution.py:108
  250.0 7.7 %collective-permute-start.21 = (bf16[192,768]{1,0:T(8,128)(2,1)}, bf16[192,768]{1,0:T(8,128)(2,1)}, u32[]{:S(2)}, u32[]{:S(2)}) collective-permute-start(bf16[192,768]{1,0:T(8,128)(2,1)} %fusion.9), channel_id=1, source_target_pairs={{0,1},{1,0},{2,3},{3,2},{4,5},{5,4},{6,7},{7,6},{8,9},{9,8},{10,11... | collective-permute-start | bytes 884744 | tf_op jit(solution)/shard_map/ppermute | solution.py:108
  260.3 7.3 %collective-permute-start.23 = (bf16[48,1664]{1,0:T(8,128)(2,1)S(1)}, bf16[48,1664]{1,0:T(8,128)(2,1)S(1)}, u32[]{:S(2)}, u32[]{:S(2)}) collective-permute-start(bf16[48,1664]{1,0:T(8,128)(2,1)S(1)} %pad_maximum_fusion.7), channel_id=1, source_target_pairs={{0,8},{2,10},{4,12},{6,14},{8,0},{10,2},{12,4},{14,6},{16,24},{18,... | collective-permute-start | bytes 479240 | tf_op jit(solution)/shard_map/ppermute | solution.py:108
  261.8 13.5 %collective-permute-start.24 = (bf16[48,1664]{1,0:T(8,128)(2,1)S(1)}, bf16[48,1664]{1,0:T(8,128)(2,1)S(1)}, u32[]{:S(2)}, u32[]{:S(2)}) collective-permute-start(bf16[48,1664]{1,0:T(8,128)(2,1)S(1)} %pad_maximum_fusion.8), channel_id=1, source_target_pairs={{0,16},{2,18},{4,20},{6,22},{8,24},{10,26},{12,28},{14,30},{16,0},... | collective-permute-start | bytes 479240 | tf_op jit(solution)/shard_map/ppermute | solution.py:108
  262.7 12.6 %collective-permute-start.25 = (bf16[48,1664]{1,0:T(8,128)(2,1)S(1)}, bf16[48,1664]{1,0:T(8,128)(2,1)S(1)}, u32[]{:S(2)}, u32[]{:S(2)}) collective-permute-start(bf16[48,1664]{1,0:T(8,128)(2,1)S(1)} %pad_maximum_fusion.9), channel_id=1, source_target_pairs={{0,24},{2,26},{4,28},{6,30},{8,16},{10,18},{12,20},{14,22},{16,8},... | collective-permute-start | bytes 479240 | tf_op jit(solution)/shard_map/ppermute | solution.py:108
  (19 other events, 209.2 us)
Sparse Core Ops, SparseCore 0:
  11.0 93.4 all-gather.1
